TPU v7x, 32 devices: a whole 2x2x4 slice. The times are simulated.
32 devices in a mesh: shard: 2 (over x), ctx: 4 (over y, core), tp: 4 (over z).
Axes of the slice: x: 2, y: 2, z: 4, core: 2. Of those that a mesh axis runs over, the one named last changes fastest.
Arguments:
- inputs: bfloat16 [2, 2, 4096, 768], P('shard', None, 'ctx'), may hold values from -6 to 6
- lengths: int32 [2, 2], P('shard'), may hold values from 2048 to 4096, as said below
- attn_gain: bfloat16 [768], P('shard'), may hold values from 0.099609375 to 1.8984375
- mlp_gain: bfloat16 [768], P('shard'), may hold values from 0.099609375 to 1.8984375
- qkv_weight: bfloat16 [768, 3, 768], P('shard', None, 'tp'), may hold values from -0.21875 to 0.21875
- attn_weight: bfloat16 [768, 768], P('tp', 'shard'), may hold values from -0.875 to 0.875
- mlp_in_weight: bfloat16 [768, 2, 1152], P('shard', None, 'tp'), may hold values from -0.21875 to 0.21875
- mlp_out_weight: bfloat16 [1152, 768], P('tp', 'shard'), may hold values from -0.1875 to 0.1875
- cotangent: bfloat16 [2, 2, 4096, 768], P('shard', None, 'ctx'), may hold values from -6 to 6
Outputs:
- layer_out: bfloat16 [2, 2, 4096, 768], P('shard', None, 'ctx')
- input_grad: bfloat16 [2, 2, 4096, 768], P('shard', None, 'ctx')
- qkv_grad: float32 [768, 3, 768], P('shard', None, 'tp')
- attn_grad: float32 [768, 768], P('tp', 'shard')
- mlp_in_grad: float32 [768, 2, 1152], P('shard', None, 'tp')
- mlp_out_grad: float32 [1152, 768], P('tp', 'shard')
- attn_gain_grad: float32 [768], P(('shard', 'tp'))
- mlp_gain_grad: float32 [768], P(('shard', 'tp'))
Inputs may be any that keep to these rules, and one draw needn't show every extreme that they name: `lengths`: among the 2 sequences of each index of shard one has length 4096; some sequence has length 2048.
All inputs are finite; a program needn't handle non-finite values.
Results may differ from a plain program's by a relative error of at most 0.017.
Values may be sent and summed in bfloat16 or wider, within the bound.
A program may use at most 192 MiB of HBM per device.

v0:
```python
import math

import jax
import jax.numpy as jnp
from jax import lax
from jax.sharding import PartitionSpec as P

HD = 64
HALF = 64


norm_eps = 1e-05
rope_base = 10000.0
masked_score = -1e30


def padded(cells, sides, width):
    for axis, dim in sides:
        count = lax.axis_size(axis)
        ends = count - 1
        head = lax.slice_in_dim(cells, 0, width, axis=dim)
        tail = lax.slice_in_dim(cells, cells.shape[dim] - width, cells.shape[dim], axis=dim)
        cells = jnp.concatenate(
            [
                lax.ppermute(tail, axis, [(i, (i + 1) % count) for i in range(ends)]),
                cells,
                lax.ppermute(head, axis, [((i + 1) % count, i) for i in range(ends)]),
            ],
            axis=dim,
        )
    return cells


def layer_norm(values, gain_row):
    center = values - jnp.mean(values, axis=-1, keepdims=True)
    variance = jnp.mean(center * center, axis=-1, keepdims=True)
    return center * lax.rsqrt(variance + norm_eps) * gain_row


def rope_tables(positions):
    exponents = jnp.arange(0, HD, 2).astype(jnp.float32) / HD
    inverse = jnp.power(rope_base, -exponents)
    angles = positions[:, None] * inverse[None, :]
    angles = jnp.concatenate([angles, angles], axis=-1)[:, None, :]
    return (jnp.cos(angles), jnp.sin(angles))


def rotate(vector, cosine, sine_table):
    half_size = vector.shape[-1] // 2
    turned = jnp.concatenate([-vector[..., half_size:], vector[..., :half_size]], axis=-1)
    return vector * cosine + turned * sine_table


def geglu(gate_up):
    return jax.nn.gelu(gate_up[..., 0, :], approximate=False) * gate_up[..., 1, :]


def on_device(
    inputs,
    lengths,
    attn_gain,
    mlp_gain,
    qkv_weight,
    attn_weight,
    mlp_in_weight,
    mlp_out_weight,
    cotangent,
):
    gathered = (
        lax.all_gather(qkv_weight, "shard", axis=0, tiled=True),
        lax.all_gather(attn_weight, "shard", axis=1, tiled=True),
        lax.all_gather(mlp_in_weight, "shard", axis=0, tiled=True),
        lax.all_gather(mlp_out_weight, "shard", axis=1, tiled=True),
        lax.all_gather(attn_gain, "shard", axis=0, tiled=True),
        lax.all_gather(mlp_gain, "shard", axis=0, tiled=True),
    )
    qkv_full, attn_full, mlp_in_full, mlp_out_full, attn_gain_low, mlp_gain_low = gathered
    gain_attn = attn_gain_low.astype(jnp.float32)
    gain_mlp = mlp_gain_low.astype(jnp.float32)
    seq_in = inputs[0].astype(jnp.float32)
    batch_count = seq_in.shape[0]
    local_len = seq_in.shape[1]
    tp_width = qkv_full.shape[2]
    local_heads = tp_width // HD
    ext_len = local_len + 2 * HALF
    scaling = 1.0 / math.sqrt(HD)
    query_tile = min(512, local_len)
    tile_count = local_len // query_tile
    key_span = query_tile + 2 * HALF
    ctx_index = lax.axis_index("ctx")
    positions = ctx_index * local_len + jnp.arange(local_len, dtype=jnp.int32)
    seq_lengths = lengths[0]
    valid_rows = (positions[None, :] < seq_lengths[:, None]).astype(jnp.float32)[:, :, None]
    tile_starts = jnp.arange(tile_count, dtype=jnp.int32) * query_tile
    query_pos = (
        ctx_index * local_len
        + tile_starts[:, None]
        + jnp.arange(query_tile, dtype=jnp.int32)[None, :]
    )
    key_pos = (
        ctx_index * local_len
        - HALF
        + tile_starts[:, None]
        + jnp.arange(key_span, dtype=jnp.int32)[None, :]
    )
    distance = query_pos[:, :, None] - key_pos[:, None, :]
    near_keys = (jnp.abs(distance) <= HALF) & (key_pos[:, None, :] >= 0)
    live_keys = (key_pos[None, :, None, :] < seq_lengths[:, None, None, None]) | (distance == 0)[
        None
    ]
    allowed = (near_keys[None] & live_keys)[:, :, None]
    cosine, sine_table = rope_tables(positions.astype(jnp.float32))

    def key_tiles(extended):
        return jnp.stack(
            [
                extended[:, index * query_tile : index * query_tile + key_span]
                for index in range(tile_count)
            ],
            axis=1,
        )

    def untile(tiles):
        total = jnp.zeros((batch_count, ext_len, local_heads, HD), jnp.float32)
        for index in range(tile_count):
            after = ext_len - index * query_tile - key_span
            total = total + jnp.pad(
                tiles[:, index], ((0, 0), (index * query_tile, after), (0, 0), (0, 0))
            )
        return total

    normed_attn, back_norm_attn = jax.vjp(layer_norm, seq_in, gain_attn)
    normed_low = normed_attn.astype(jnp.bfloat16)
    qkv_raw = jnp.einsum("mtd,dcf->mtcf", normed_low, qkv_full, preferred_element_type=jnp.float32)
    heads_raw = qkv_raw.reshape(batch_count, local_len, 3, local_heads, HD)

    def rope_pair(query_raw, key_raw):
        return (rotate(query_raw, cosine, sine_table), rotate(key_raw, cosine, sine_table))

    (query_rot, key_rot), back_rope = jax.vjp(rope_pair, heads_raw[:, :, 0], heads_raw[:, :, 1])
    queries = query_rot.astype(jnp.bfloat16)
    key_value = jnp.stack([key_rot.astype(jnp.bfloat16), heads_raw[:, :, 2].astype(jnp.bfloat16)])
    key_value = key_value.reshape(2, batch_count, local_len, tp_width)
    key_value_ext = padded(key_value, (("ctx", 2),), HALF)
    key_value_ext = key_value_ext.reshape(2, batch_count, ext_len, local_heads, HD)
    keys_tiled = key_tiles(key_value_ext[0])
    values_tiled = key_tiles(key_value_ext[1])
    queries_tiled = queries.reshape(batch_count, tile_count, query_tile, local_heads, HD)

    def masked_scores():
        raw_scores = (
            jnp.einsum(
                "mnqhd,mnkhd->mnhqk", queries_tiled, keys_tiled, preferred_element_type=jnp.float32
            )
            * scaling
        )
        return jnp.where(allowed, raw_scores, masked_score)

    scores = masked_scores()
    top_score = jnp.max(scores, axis=-1, keepdims=True)
    exponent_terms = jnp.exp(scores - top_score)
    denominator = jnp.sum(exponent_terms, axis=-1, keepdims=True)
    soft_low = (exponent_terms / denominator).astype(jnp.bfloat16)
    log_total = top_score + jnp.log(denominator)
    context = jnp.einsum(
        "mnhqk,mnkhd->mnqhd", soft_low, values_tiled, preferred_element_type=jnp.float32
    )
    context_low = context.astype(jnp.bfloat16).reshape(batch_count, local_len, tp_width)
    attn_part = jnp.einsum(
        "mtf,fd->mtd", context_low, attn_full, preferred_element_type=jnp.float32
    )
    attn_out = lax.psum(attn_part, "tp")
    middle = seq_in + attn_out
    normed_mlp, back_norm_mlp = jax.vjp(layer_norm, middle, gain_mlp)
    normed_mlp_low = normed_mlp.astype(jnp.bfloat16)
    gate_up = jnp.einsum(
        "mtd,dcf->mtcf", normed_mlp_low, mlp_in_full, preferred_element_type=jnp.float32
    )
    hidden, back_glu = jax.vjp(geglu, gate_up)
    hidden_low = hidden.astype(jnp.bfloat16)
    mlp_part = jnp.einsum(
        "mtf,fd->mtd", hidden_low, mlp_out_full, preferred_element_type=jnp.float32
    )
    mlp_out = lax.psum(mlp_part.astype(jnp.bfloat16), "tp").astype(jnp.float32)
    layer_out = ((middle + mlp_out) * valid_rows).astype(jnp.bfloat16)[None]
    grad_out = cotangent[0].astype(jnp.float32) * valid_rows
    grad_out_low = grad_out.astype(jnp.bfloat16)
    mlp_out_grad = jnp.einsum(
        "mtf,mtd->fd", hidden_low, grad_out_low, preferred_element_type=jnp.float32
    )
    grad_hidden = jnp.einsum(
        "mtd,fd->mtf", grad_out_low, mlp_out_full, preferred_element_type=jnp.float32
    )
    (grad_gate_up,) = back_glu(grad_hidden)
    grad_gate_low = grad_gate_up.astype(jnp.bfloat16)
    mlp_in_grad = jnp.einsum(
        "mtd,mtcf->dcf", normed_mlp_low, grad_gate_low, preferred_element_type=jnp.float32
    )
    grad_mlp_part = jnp.einsum(
        "mtcf,dcf->mtd", grad_gate_low, mlp_in_full, preferred_element_type=jnp.float32
    )
    grad_normed_mlp = lax.psum(grad_mlp_part, "tp")
    grad_mid_norm, mlp_gain_grad = back_norm_mlp(grad_normed_mlp)
    grad_middle = grad_out + grad_mid_norm
    grad_middle_low = grad_middle.astype(jnp.bfloat16)
    attn_grad = jnp.einsum(
        "mtf,mtd->fd", context_low, grad_middle_low, preferred_element_type=jnp.float32
    )
    grad_context = jnp.einsum(
        "mtd,fd->mtf", grad_middle_low, attn_full, preferred_element_type=jnp.float32
    )
    grad_context = grad_context.astype(jnp.bfloat16).reshape(
        batch_count, tile_count, query_tile, local_heads, HD
    )
    soft_again = jnp.exp(masked_scores() - log_total)
    soft_again_low = soft_again.astype(jnp.bfloat16)
    grad_values = jnp.einsum(
        "mnhqk,mnqhd->mnkhd", soft_again_low, grad_context, preferred_element_type=jnp.float32
    )
    grad_soft = jnp.einsum(
        "mnqhd,mnkhd->mnhqk", grad_context, values_tiled, preferred_element_type=jnp.float32
    )
    row_terms = jnp.sum(soft_again * grad_soft, axis=-1, keepdims=True)
    grad_scores = (soft_again * (grad_soft - row_terms)).astype(jnp.bfloat16)
    grad_queries = (
        jnp.einsum(
            "mnhqk,mnkhd->mnqhd", grad_scores, keys_tiled, preferred_element_type=jnp.float32
        )
        * scaling
    )
    grad_queries = grad_queries.reshape(batch_count, local_len, local_heads, HD)
    grad_keys = (
        jnp.einsum(
            "mnhqk,mnqhd->mnkhd", grad_scores, queries_tiled, preferred_element_type=jnp.float32
        )
        * scaling
    )
    grad_ext = jnp.stack([untile(grad_keys), untile(grad_values)]).reshape(
        2, batch_count, ext_len, tp_width
    )
    rim_pairs = jnp.concatenate([grad_ext[:, :, :HALF], grad_ext[:, :, ext_len - HALF :]], axis=2)
    arrived = padded(rim_pairs, (("ctx", 2),), HALF)
    from_lower = arrived[:, :, :HALF]
    from_upper = arrived[:, :, arrived.shape[2] - HALF :]
    grad_own = grad_ext[:, :, HALF : HALF + local_len]
    grad_own = grad_own + jnp.pad(from_lower, ((0, 0), (0, 0), (0, local_len - HALF), (0, 0)))
    grad_own = grad_own + jnp.pad(from_upper, ((0, 0), (0, 0), (local_len - HALF, 0), (0, 0)))
    grad_key_rot = grad_own[0].reshape(batch_count, local_len, local_heads, HD)
    grad_value_own = grad_own[1].reshape(batch_count, local_len, local_heads, HD)
    grad_query_raw, grad_key_raw = back_rope((grad_queries, grad_key_rot))
    grad_qkv = jnp.stack([grad_query_raw, grad_key_raw, grad_value_own], axis=2)
    grad_qkv_low = grad_qkv.reshape(batch_count, local_len, 3, tp_width).astype(jnp.bfloat16)
    qkv_grad = jnp.einsum(
        "mtd,mtcf->dcf", normed_low, grad_qkv_low, preferred_element_type=jnp.float32
    )
    grad_attn_part = jnp.einsum(
        "mtcf,dcf->mtd", grad_qkv_low, qkv_full, preferred_element_type=jnp.float32
    )
    grad_normed = lax.psum(grad_attn_part, "tp")
    grad_in_norm, attn_gain_grad = back_norm_attn(grad_normed)
    input_grad = (grad_middle + grad_in_norm).astype(jnp.bfloat16)[None]
    partials = (qkv_grad, attn_grad, mlp_in_grad, mlp_out_grad, attn_gain_grad, mlp_gain_grad)
    summed = lax.psum(
        (partials[0], partials[1], partials[2], partials[3], partials[4], partials[5]), "ctx"
    )
    reduced = (
        lax.psum_scatter(summed[0], "shard", scatter_dimension=0, tiled=True),
        lax.psum_scatter(summed[1], "shard", scatter_dimension=1, tiled=True),
        lax.psum_scatter(summed[2], "shard", scatter_dimension=0, tiled=True),
        lax.psum_scatter(summed[3], "shard", scatter_dimension=1, tiled=True),
        lax.psum_scatter(summed[4], "shard", scatter_dimension=0, tiled=True),
        lax.psum_scatter(summed[5], "shard", scatter_dimension=0, tiled=True),
    )
    gain_share = reduced[4].shape[0] // lax.axis_size("tp")
    gain_start = lax.axis_index("tp") * gain_share
    attn_gain_out = lax.dynamic_slice_in_dim(reduced[4], gain_start, gain_share)
    mlp_gain_out = lax.dynamic_slice_in_dim(reduced[5], gain_start, gain_share)
    return (
        layer_out,
        input_grad,
        reduced[0],
        reduced[1],
        reduced[2],
        reduced[3],
        attn_gain_out,
        mlp_gain_out,
    )


def solution(mesh):
    in_specs = (
        P("shard", None, "ctx", None),
        P("shard", None),
        P("shard"),
        P("shard"),
        P("shard", None, "tp"),
        P("tp", "shard"),
        P("shard", None, "tp"),
        P("tp", "shard"),
        P("shard", None, "ctx", None),
    )
    out_specs = (
        P("shard", None, "ctx", None),
        P("shard", None, "ctx", None),
        P("shard", None, "tp"),
        P("tp", "shard"),
        P("shard", None, "tp"),
        P("tp", "shard"),
        P(("shard", "tp")),
        P(("shard", "tp")),
    )
    return jax.shard_map(
        on_device, mesh=mesh, in_specs=in_specs, out_specs=out_specs, check_vma=False
    )
```

profile of v0, /device:TPU:0, one launch (start us, length us, event | category | flops | bytes accessed | tf_op | source)
XLA Modules:
  0.0 1094.5 jit_solution(6729855262283549967)
XLA Ops:
  8.1 5.3 all-gather
  13.5 2.4 convert_reduce_fusion
  17.6 11.8 %all_gather.19 = bf16[768,3,192]{0,2,1:T(8,128)(2,1)S(1)} all-gather(bf16[384,3,192]{0,2,1:T(8,128)(2,1)S(1)} %copy-done.45), channel_id=1, replica_groups=mesh['shard'=2,'ctx'=4,'tp'=4] {'shard'}, dimensions={0}, use_global_device_ids=true | all-gather | bytes 1327104 | tf_op jit(solution)/shard_map/all_gather | solution.py:70
  29.4 2.6 fusion.32
  33.0 3.1 fusion.178
  37.3 1.7 fusion.114
  43.7 3.7 collective-permute-start
  47.7 1.6 fusion.127
  49.4 3.4 squeeze.38
  55.7 2.0 or_and_fusion
  60.4 7.3 all_gather.20
  67.7 4.4 concatenate.47
  72.1 1.6 fusion.179
  75.9 3.7 fusion.182
  79.7 3.1 fusion
  82.9 2.2 copy-done
  85.1 5.0 fusion.106
  90.2 1.7 copy.52
  91.9 3.2 reshape.403
  95.1 4.8 fusion.122
  100.6 4.3 all-gather.1
  104.9 6.9 all_gather.23
  111.8 12.6 %all_gather.22 = bf16[768,2,288]{0,2,1:T(8,128)(2,1)} all-gather(bf16[384,2,288]{0,2,1:T(8,128)(2,1)} %param.15), channel_id=1, replica_groups=mesh['shard'=2,'ctx'=4,'tp'=4] {'shard'}, dimensions={0}, use_global_device_ids=true | all-gather | bytes 1327104 | tf_op jit(solution)/shard_map/all_gather | solution.py:72
  124.5 4.5 fusion.37
  129.1 194.1 %all-reduce.23.cloned.1.call-done = f32[2,1024,768]{2,1,0:T(8,128)} async-done(((f32[2,1024,768]{2,1,0:T(8,128)}), f32[2,1024,768]{2,1,0:T(8,128)}) %all-reduce.23.cloned.1.call-update) | async-done | bytes 6291472 | tf_op jit(solution)/shard_map/psum | solution.py:172
  323.2 3.5 fusion.176
  327.6 1.7 copy-done.3
  329.3 2.7 fusion.42
  332.0 5.1 multiply_bitcast_fusion
  339.8 4.6 convolution_bitcast_fusion.1
  345.3 6.4 convolution_convert_fusion
  351.8 1.8 copy-done.10
  353.6 9.3 fusion.103
  363.9 7.7 fusion.96
  371.7 194.6 %all-reduce.27.cloned.1.call-done = f32[2,1024,768]{2,1,0:T(8,128)} async-done(((f32[2,1024,768]{2,1,0:T(8,128)}), f32[2,1024,768]{2,1,0:T(8,128)}) %all-reduce.27.cloned.1.call-update) | async-done | bytes 6291472 | tf_op jit(solution)/shard_map/psum | solution.py:202
  566.3 6.2 multiply_reduce_fusion.1
  572.5 116.8 %all-reduce.25.cloned.1.call-done = bf16[2,1024,768]{2,1,0:T(8,128)(2,1)} async-done(((bf16[2,1024,768]{2,1,0:T(8,128)(2,1)}), bf16[2,1024,768]{2,1,0:T(8,128)(2,1)}) %all-reduce.25.cloned.1.call-update) | async-done | bytes 3145744 | tf_op jit(solution)/shard_map/psum | solution.py:184
  689.3 8.3 fusion.174
  698.8 1.5 copy-done.4
  700.4 1.7 copy-done.8
  702.0 2.1 convolution_convert_fusion.1
  704.1 3.4 reshape.404
  707.5 14.0 %multiply_reduce_fusion = (f32[2,2,3,512]{3,2,1,0:T(4,128)S(1)}, f32[2,2,3,512,640]{4,3,2,1,0:T(8,128)}) fusion(f32[2,2,3,512,640]{4,3,2,1,0:T(8,128)} %copy-done, f32[2,2,3,512]{3,2,1,0:T(4,128)S(1)} %log_add_fusion, bf16[2,1,640,3,64]{2,4,3,1,0:T(8,128)(2,1)} %copy-done.33, bf16[2,1,640,3,64]{2,4,3,1,0:T(8,128)(2,1)} %copy-done.32, ...), kind=kOutput, calls=%fused_computation.1 | convolution fusion | flops 515598336 | bytes 33275904 | tf_op jit(solution)/shard_map/mnqhd,mnkhd->mnhqk/dot_general | solution.py:220
  722.7 7.4 multiply_convert_fusion
  730.2 2.5 multiply_bitcast_fusion.2
  734.0 4.3 fusion.89
  738.3 1.7 slice_bitcast_fusion.2
  740.0 1.5 multiply_bitcast_fusion.1
  743.0 2.6 collective-permute-start.2
  746.9 1.6 convolution_bitcast_fusion.2
  748.6 1.5 collective-permute-done.3
  750.1 2.1 fusion.28
  757.4 3.5 fusion.99
  761.0 7.3 convolution_bitcast_fusion
  770.3 25.6 %reduce-scatter.5.cloned.1.call-done = f32[384,3,192]{0,2,1:T(8,128)} async-done(((f32[768,3,192]{0,2,1:T(8,128)}), f32[384,3,192]{0,2,1:T(8,128)}) %reduce-scatter.5.cloned.1.call-update) | async-done | bytes 884752 | tf_op jit(solution)/shard_map/reduce_scatter | solution.py:267
  795.9 225.4 %all-reduce.29.cloned.1.call-done = f32[2,1024,768]{2,1,0:T(8,128)} async-done(((f32[2,1024,768]{2,1,0:T(8,128)}), f32[2,1024,768]{2,1,0:T(8,128)}) %all-reduce.29.cloned.1.call-update) | async-done | bytes 6291472 | tf_op jit(solution)/shard_map/psum | solution.py:259
  1021.2 4.0 fusion.21
  1025.9 3.2 fusion.15
  1029.1 5.0 all-reduce.16
  1034.2 6.7 all-reduce.14
  1042.1 9.2 fusion.30
  1051.3 30.6 %all-reduce.31.cloned.1.call-done = (f32[384,3,192]{0,2,1:T(8,128)}, f32[192,384]{1,0:T(8,128)}, f32[384,2,288]{0,2,1:T(8,128)}, f32[288,384]{1,0:T(8,128)}) async-done(((f32[384,3,192]{0,2,1:T(8,128)}, f32[192,384]{1,0:T(8,128)}, f32[384,2,288]{0,2,1:T(8,128)}, f32[288,384]{1,0:T(8,128)}), (f32[384,3,192]{0,2,1:T(8,128)}, f32[192,384]{1,0:T(8,128)}, f32[384,2,288]{0,2,1:T(8,128)}, ...) | async-done | bytes 2506768 | tf_op jit(solution)/shard_map/psum | solution.py:263
  1081.9 2.2 copy.93
  1084.2 1.7 copy.94
  (214 shorter events, 40.4 us)
Async XLA Ops:
  7.2 8.7 copy-start.1
  7.2 316.0 %all-reduce.23.cloned.1.call-start = ((), (), s32[]{:S(2)}) async-start(), calls=%async_computation.4 | async-start | bytes 12582912 | tf_op jit(solution)/shard_map/psum | solution.py:172
  13.4 15.9 %copy-start.54 = (f32[768]{0:T(1024)}, f32[768]{0:T(1024)S(1)}, u32[]{:S(2)}) copy-start(f32[768]{0:T(1024)S(1)} %reshape.411) | copy-start | bytes 9220
  15.8 1.7 copy-start.45
  15.9 16.1 %copy-start.46 = (f32[2,1024]{1,0:T(2,128)}, f32[2,1024]{1,0:T(2,128)S(1)}, u32[]{:S(2)}) copy-start(f32[2,1024]{1,0:T(2,128)S(1)} %broadcast_multiply_fusion.5) | copy-start | bytes 24580
  17.6 14.4 %copy-start.52 = (f32[2,1024]{1,0:T(2,128)}, f32[2,1024]{1,0:T(2,128)S(1)}, u32[]{:S(2)}) copy-start(f32[2,1024]{1,0:T(2,128)S(1)} %fusion.130) | copy-start | bytes 24580
  29.4 2.7 copy-start.39
  37.2 1.9 copy-start.22
  37.2 2.0 copy-start.24
  41.0 1.4 copy-start.16
  42.4 25.3 %collective-permute-start.1 = (bf16[2,2,64,192]{2,3,1,0:T(8,128)(2,1)}, bf16[2,2,64,192]{2,3,1,0:T(8,128)(2,1)}, u32[]{:S(2)}, u32[]{:S(2)}) collective-permute-start(bf16[2,2,64,192]{2,3,1,0:T(8,128)(2,1)} %get-tuple-element.43), channel_id=1, source_target_pairs={{4,0},{8,4},{12,8},{5,1},{9,5},{13,9},{6,2},{10,6},{14,10},{7,3},{... | collective-permute-start | bytes 294920 | tf_op jit(solution)/shard_map/ppermute | solution.py:27
  43.7 24.0 %collective-permute-start = (bf16[2,2,64,192]{2,3,1,0:T(8,128)(2,1)}, bf16[2,2,64,192]{2,3,1,0:T(8,128)(2,1)}, u32[]{:S(2)}, u32[]{:S(2)}) collective-permute-start(bf16[2,2,64,192]{2,3,1,0:T(8,128)(2,1)} %get-tuple-element.44), channel_id=1, source_target_pairs={{0,4},{4,8},{8,12},{1,5},{5,9},{9,13},{2,6},{6,10},{10,14},{3,7},{... | collective-permute-start | bytes 294920 | tf_op jit(solution)/shard_map/ppermute | solution.py:25
  52.8 1.5 copy-start.57
  55.5 2.1 copy-start.19
  55.5 2.1 copy-start.37
  57.7 1.4 copy-start.15
  57.7 1.4 copy-start.17
  73.7 2.3 copy-start.36
  73.8 5.9 copy-start.28
  73.8 5.9 copy-start.30
  73.9 8.9 copy-start.32
  74.0 8.9 copy-start.33
  79.7 5.4 copy-start
  82.8 7.3 copy-start.49
  99.9 466.4 %all-reduce.27.cloned.1.call-start = ((), (), s32[]{:S(2)}) async-start(), calls=%async_computation.6 | async-start | bytes 12582912 | tf_op jit(solution)/shard_map/psum | solution.py:202
  111.8 12.7 %copy-start.34 = (bf16[288,768]{1,0:T(8,128)(2,1)}, bf16[288,768]{1,0:T(8,128)(2,1)S(1)}, u32[]{:S(2)}) copy-start(bf16[288,768]{1,0:T(8,128)(2,1)S(1)} %all_gather.23) | copy-start | bytes 1327108
  326.7 2.6 copy-start.3
  326.7 2.6 copy-start.40
  329.3 2.7 copy-start.11
  332.0 5.2 copy-start.6
  337.1 1.9 copy-start.26
  344.4 345.0 %all-reduce.25.cloned.1.call-start = ((), (), s32[]{:S(2)}) async-start(), calls=%async_computation.5 | async-start | bytes 6291456 | tf_op jit(solution)/shard_map/psum | solution.py:184
  351.7 1.9 copy-start.10
  351.7 418.5 %reduce-scatter.11.cloned.1.call-start = ((), (), s32[]{:S(2)}) async-start(), calls=%async_computation.11 | async-start | bytes 1327104 | tf_op jit(solution)/shard_map/reduce_scatter | solution.py:270
  362.9 407.3 %reduce-scatter.9.cloned.1.call-start = ((), (), s32[]{:S(2)}) async-start(), calls=%async_computation.10 | async-start | bytes 2654208 | tf_op jit(solution)/shard_map/reduce_scatter | solution.py:269
  371.7 398.6 %reduce-scatter.7.cloned.1.call-start = ((), (), s32[]{:S(2)}) async-start(), calls=%async_computation.9 | async-start | bytes 884736 | tf_op jit(solution)/shard_map/reduce_scatter | solution.py:268
  697.6 2.7 copy-start.4
  700.4 1.7 copy-start.8
  704.1 17.4 %slice-start = ((s8[15728640]{0:T(1024)(128)(4,1)}), s8[3145728]{0:T(1024)(128)(4,1)S(1)}, s32[]{:S(2)}) async-start(s8[15728640]{0:T(1024)(128)(4,1)} %bitcast.348), calls=%async_computation.13 | async-start | bytes 6291456
  707.5 14.0 %slice-start.1 = ((s8[15728640]{0:T(1024)(128)(4,1)}), s8[4194304]{0:T(1024)(128)(4,1)S(1)}, s32[]{:S(2)}) async-start(s8[15728640]{0:T(1024)(128)(4,1)} %bitcast.348), calls=%async_computation.14 | async-start | bytes 8388608
  707.5 14.0 %slice-start.2 = ((s8[15728640]{0:T(1024)(128)(4,1)}), s8[4194304]{0:T(1024)(128)(4,1)S(1)}, s32[]{:S(2)}) async-start(s8[15728640]{0:T(1024)(128)(4,1)} %bitcast.348), calls=%async_computation.15 | async-start | bytes 8388608
  707.5 15.2 %slice-start.3 = ((s8[15728640]{0:T(1024)(128)(4,1)}), s8[4194304]{0:T(1024)(128)(4,1)S(1)}, s32[]{:S(2)}) async-start(s8[15728640]{0:T(1024)(128)(4,1)} %bitcast.348), calls=%async_computation.16 | async-start | bytes 8388608
  722.7 7.4 copy-start.29
  722.7 7.4 copy-start.31
  738.3 1.7 copy-start.21
  742.0 4.9 copy-start.9
  742.0 4.9 copy-start.13
  743.0 5.6 collective-permute-start.2
  745.6 4.5 collective-permute-start.3
  748.5 47.3 %reduce-scatter.5.cloned.1.call-start = ((), (), s32[]{:S(2)}) async-start(), calls=%async_computation.8 | async-start | bytes 2654208 | tf_op jit(solution)/shard_map/reduce_scatter | solution.py:267
  752.2 1.7 copy-start.7
  752.2 1.7 copy-start.25
  752.3 3.9 copy-start.41
  755.3 2.1 copy-start.2
  755.3 2.1 copy-start.47
  755.3 2.1 copy-start.53
  755.3 2.1 copy-start.55
  760.9 260.3 %all-reduce.29.cloned.1.call-start = ((), (), s32[]{:S(2)}) async-start(), calls=%async_computation.7 | async-start | bytes 12582912 | tf_op jit(solution)/shard_map/psum | solution.py:259
  768.3 313.6 %all-reduce.31.cloned.1.call-start = ((), (), s32[]{:S(2)}) async-start(), calls=%async_computation.12 | async-start | bytes 5013504 | tf_op jit(solution)/shard_map/psum | solution.py:263
  795.9 229.3 %copy-start.51 = (f32[2,1024]{1,0:T(2,128)S(1)}, f32[2,1024]{1,0:T(2,128)}, u32[]{:S(2)}) copy-start(f32[2,1024]{1,0:T(2,128)} %copy-done.50) | copy-start | bytes 24580
  1021.2 4.6 copy-start.5
  1025.9 3.2 copy-start.56
  1081.9 3.9 copy-start.38
  1081.9 4.9 copy-start.44
  (13 other events, 13.8 us)
Sparse Core Ops, SparseCore 0:
  100.0 223.1 all-reduce.22
  344.5 221.7 all-reduce.26
  569.3 120.0 all-reduce.24
  692.0 17.5 reduce-scatter.10
  711.7 28.2 reduce-scatter.8
  748.6 16.0 reduce-scatter.6
  767.6 28.2 reduce-scatter.4
  798.3 222.8 all-reduce.28
  1024.0 57.8 all-reduce.30
where the time goes:
time: 1100 us; the launch traced here: 1090 us
  waiting for transfers between devices  789 us (72%)
  matrix products  88.2 us (8%)
  other arithmetic  76 us (7%)
  blocking collectives  60 us (5%)
  local copies, waits for them, and re-layouts  56.3 us (5%)
  between operations  15.9 us (1%)
    psum x1, waiting for transfers between devices, on_device(): grad_normed = lax.psum(grad_attn_part, 'tp')  225 us
    psum x1, waiting for transfers between devices, on_device(): grad_normed_mlp = lax.psum(grad_mlp_part, 'tp')  195 us
    psum x1, waiting for transfers between devices, on_device(): attn_out = lax.psum(attn_part, 'tp')  194 us
    psum x1, waiting for transfers between devices, on_device(): mlp_out = lax.psum(mlp_part.astype(jnp.bfloat16), 'tp').astype(jnp.float32)  117 us
    psum x1, waiting for transfers between devices, on_device(): lax.psum((partials[0], partials[1], partials[2], partials[3], partials[4]...  30.6 us
    unnamed x137, local copies, waits for them, and re-layouts  29.4 us
    reduce_scatter x1, waiting for transfers between devices, on_device(): lax.psum_scatter(summed[0], 'shard', scatter_dimension=0, tiled=True)  25.6 us
  transfers between devices with their start and end apart: 13, of which 7 were waited for; matrix products, arithmetic and copies ran while one was open for 12% of the time, Pallas kernels for 0%

commit v1 on v0

v1 whole, which is shorter than its diff:
```python
import math

import numpy as np

import jax
import jax.numpy as jnp
from jax import lax
from jax.experimental import pallas as pl
from jax.experimental.pallas import tpu as pltpu
from jax.sharding import PartitionSpec as P

HD = 64
HALF = 64
TILE = 128
LANES = 128
norm_eps = 1e-05
rope_base = 10000.0
masked_score = -1e30
F32 = jnp.float32
BF16 = jnp.bfloat16
VMEM_LIMIT = 60 * 1024 * 1024


def nt(a, b):
    return lax.dot_general(a, b, (((1,), (1,)), ((), ())), preferred_element_type=F32)


def nn(a, b):
    return lax.dot_general(a, b, (((1,), (0,)), ((), ())), preferred_element_type=F32)


def tn(a, b):
    return lax.dot_general(a, b, (((0,), (0,)), ((), ())), preferred_element_type=F32)


def rope_constants(seq):
    w = rope_base ** (-np.arange(0, HD, 2) / HD)
    w = np.tile(w, 2 * LANES // HD)
    rows = np.arange(TILE)[:, None] * w
    blocks = (np.arange(seq // HALF + 4)[:, None] - 1) * HALF * w
    tables = (np.cos(rows), np.sin(rows), np.cos(blocks), np.sin(blocks))
    return tuple(t.astype(np.float32) for t in tables)


def rope_tile(tables, block):
    cos_r, sin_r, cos_b, sin_b = tables
    cb = cos_b[pl.ds(block + 1, 1), :]
    sb = sin_b[pl.ds(block + 1, 1), :]
    cr = cos_r[...]
    sr = sin_r[...]
    cosine = cr * cb - sr * sb
    sine = sr * cb + cr * sb
    first = lax.broadcasted_iota(jnp.int32, sine.shape, 1) % HD < HD // 2
    return cosine, jnp.where(first, -sine, sine), first


def turn(u, cosine, sine, first):
    other = jnp.where(first, pltpu.roll(u, LANES - HD // 2, 1), pltpu.roll(u, HD // 2, 1))
    return u * cosine + other * sine


def layer_stats(z):
    center = z - jnp.mean(z, axis=-1, keepdims=True)
    inv = lax.rsqrt(jnp.mean(center * center, axis=-1, keepdims=True) + norm_eps)
    return center * inv, inv


def layer_back(e, xhat, inv):
    return (e - jnp.mean(e, axis=-1, keepdims=True) - xhat * jnp.mean(e * xhat, axis=-1, keepdims=True)) * inv


def head_masks(shape):
    lane = lax.broadcasted_iota(jnp.int32, shape, 1)
    return lane < HD


def split_heads(c, low_head):
    zero = jnp.zeros_like(c)
    return jnp.concatenate([jnp.where(low_head, c, zero), jnp.where(low_head, zero, c)], axis=0)


def phase_qkv(x_ref, gain_ref, w_ref, tables, normed_ref, q_ref, k_ref, v_ref, block0, rows):
    width = x_ref.shape[1]
    scaling = 1.0 / math.sqrt(HD)

    def body(t, carry):
        r0 = pl.multiple_of(t * rows, rows)
        xhat, _ = layer_stats(x_ref[pl.ds(r0, rows), :].astype(F32))
        normed = (xhat * gain_ref[...].astype(F32)).astype(BF16)
        normed_ref[pl.ds(r0, rows), :] = normed
        for part, ref in enumerate((q_ref, k_ref, v_ref)):
            out = nt(normed, w_ref[part * width : (part + 1) * width, :])
            if part == 2:
                ref[pl.ds(r0, rows), :] = out.astype(BF16)
                continue
            for s in range(rows // TILE):
                cosine, sine, first = rope_tile(tables, block0 + t * (rows // HALF) + s * (TILE // HALF))
                if part == 0:
                    cosine, sine = cosine * scaling, sine * scaling
                for j in range(width // LANES):
                    u = out[s * TILE : (s + 1) * TILE, j * LANES : (j + 1) * LANES]
                    ref[pl.ds(r0 + s * TILE, TILE), j * LANES : (j + 1) * LANES] = turn(u, cosine, sine, first).astype(BF16)
        return carry

    lax.fori_loop(0, x_ref.shape[0] // rows, body, 0)


def phase_attend(q_ref, k_ref, v_ref, p_ref, ctx_ref, pos0, length):
    width = q_ref.shape[1]
    span = TILE + 2 * HALF

    def body(t, carry):
        r0 = pl.multiple_of(t * TILE, TILE)
        row = lax.broadcasted_iota(jnp.int32, (TILE, span), 0)
        col = lax.broadcasted_iota(jnp.int32, (TILE, span), 1)
        offset = col - row
        key_pos = pos0 + t * TILE - HALF + col
        allowed = (offset >= 0) & (offset <= 2 * HALF) & (key_pos >= 0) & ((key_pos < length) | (offset == HALF))
        bias = jnp.where(allowed, 0.0, masked_score).astype(F32)
        bias = jnp.concatenate([bias, bias], axis=0)
        low_head = head_masks((TILE, LANES))
        for j in range(width // LANES):
            lanes = slice(j * LANES, (j + 1) * LANES)
            q2 = split_heads(q_ref[pl.ds(r0 + HALF, TILE), lanes], low_head)
            scores = nt(q2, k_ref[pl.ds(r0, span), lanes]) + bias
            terms = jnp.exp(scores - jnp.max(scores, axis=-1, keepdims=True))
            probs = (terms * (1.0 / jnp.sum(terms, axis=-1, keepdims=True))).astype(BF16)
            p_ref[t, j] = probs
            out = nn(probs, v_ref[pl.ds(r0, span), lanes])
            ctx_ref[pl.ds(r0, TILE), lanes] = jnp.where(low_head, out[:TILE], out[TILE:]).astype(BF16)
        return carry

    lax.fori_loop(0, ctx_ref.shape[0] // TILE, body, 0)


def phase_mlp(x_ref, cot_ref, ctx_ref, gain_ref, wo_ref, wi_ref, wm_ref, out_ref, gm_ref, gml_ref, go_ref, nm_ref, hid_ref, dgu_ref, dctx_ref, gg_ref, pos0, length, rows):
    ff = wm_ref.shape[0]
    half = hid_ref.shape[1]
    gg_ref[...] = jnp.zeros_like(gg_ref)

    def body(t, carry):
        r0 = pl.multiple_of(t * rows, rows)
        here = pl.ds(r0, rows)
        gain = gain_ref[...].astype(F32)
        middle = x_ref[pl.ds(r0 + HALF, rows), :].astype(F32) + nn(ctx_ref[here, :], wo_ref[...])
        xhat, inv = layer_stats(middle)
        nm = (xhat * gain).astype(BF16)
        nm_ref[here, :] = nm
        gate = nt(nm, wi_ref[:ff, :])
        up = nt(nm, wi_ref[ff:, :])
        cdf = 0.5 + 0.5 * lax.erf(gate * math.sqrt(0.5))
        gelu = gate * cdf
        slope = cdf + gate * (jnp.exp(-0.5 * gate * gate) * (1.0 / math.sqrt(2.0 * math.pi)))
        hidden = (gelu * up).astype(BF16)
        hid_ref[here, :] = hidden[:, :half]
        valid = pos0 + r0 + lax.broadcasted_iota(jnp.int32, (rows, 1), 0) < length
        out_ref[here, :] = jnp.where(valid, middle + nn(hidden, wm_ref[...]), 0.0).astype(BF16)
        grad_out = jnp.where(valid, cot_ref[here, :].astype(F32), 0.0)
        grad_low = grad_out.astype(BF16)
        go_ref[here, :] = grad_low
        grad_hidden = nt(grad_low, wm_ref[...])
        grad_gate = (grad_hidden * up * slope).astype(BF16)
        grad_up = (grad_hidden * gelu).astype(BF16)
        dgu_ref[here, :half] = grad_gate[:, :half]
        dgu_ref[here, half:] = grad_up[:, :half]
        grad_nm = nn(grad_gate, wi_ref[:ff, :]) + nn(grad_up, wi_ref[ff:, :])
        gg_ref[...] += jnp.sum((grad_nm * xhat).reshape(rows // 8, 8, -1), axis=0)
        grad_middle = grad_out + layer_back(grad_nm * gain, xhat, inv)
        gm_ref[here, :] = grad_middle
        gm_low = grad_middle.astype(BF16)
        gml_ref[here, :] = gm_low
        dctx_ref[here, :] = nt(gm_low, wo_ref[...]).astype(BF16)
        return carry

    lax.fori_loop(0, ctx_ref.shape[0] // rows, body, 0)


def phase_attend_back(q_ref, k_ref, v_ref, p_ref, ctx_ref, dctx_ref, tables, dq_ref, dk_ref, dv_ref, block0):
    width = q_ref.shape[1]
    span = TILE + 2 * HALF
    scaling = 1.0 / math.sqrt(HD)
    dk_ref[...] = jnp.zeros_like(dk_ref)
    dv_ref[...] = jnp.zeros_like(dv_ref)

    def body(t, carry):
        r0 = pl.multiple_of(t * TILE, TILE)
        low_head = head_masks((TILE, LANES))
        cosine, sine, first = rope_tile(tables, block0 + 1 + t * (TILE // HALF))
        cosine, sine = cosine * scaling, sine * -scaling
        keys = pl.ds(r0, span)
        for j in range(width // LANES):
            lanes = slice(j * LANES, (j + 1) * LANES)
            probs = p_ref[t, j]
            kc = k_ref[keys, lanes]
            dc = dctx_ref[pl.ds(r0, TILE), lanes]
            row_term = dc.astype(F32) * ctx_ref[pl.ds(r0, TILE), lanes].astype(F32)
            row_low = jnp.sum(jnp.where(low_head, row_term, 0.0), axis=-1, keepdims=True)
            row_high = jnp.sum(jnp.where(low_head, 0.0, row_term), axis=-1, keepdims=True)
            row_term = jnp.concatenate([row_low, row_high], axis=0)
            dc2 = split_heads(dc, low_head)
            grad_probs = nt(dc2, v_ref[keys, lanes])
            grad_scores = (probs.astype(F32) * (grad_probs - row_term)).astype(BF16)
            dq2 = nn(grad_scores, kc)
            dq = jnp.where(low_head, dq2[:TILE], dq2[TILE:])
            dq_ref[pl.ds(r0, TILE), lanes] = turn(dq, cosine, sine, first).astype(BF16)
            q2 = split_heads(q_ref[pl.ds(r0 + HALF, TILE), lanes], low_head)
            dk_ref[keys, lanes] += tn(grad_scores, q2)
            dv_ref[keys, lanes] += tn(probs, dc2)
        return carry

    lax.fori_loop(0, dq_ref.shape[0] // TILE, body, 0)


def phase_input(x_ref, gm_ref, dq_ref, dk_ref, dv_ref, gain_ref, w_ref, tables, dqkv_ref, out_ref, gg_ref, block0, rows, half):
    width = x_ref.shape[1]
    gg_ref[...] = jnp.zeros_like(gg_ref)

    def body(t, carry):
        r0 = pl.multiple_of(t * rows, rows)
        here = pl.ds(r0, rows)
        gain = gain_ref[...].astype(F32)
        pieces = []
        for s in range(rows // TILE):
            cosine, sine, first = rope_tile(tables, block0 + 1 + t * (rows // HALF) + s * (TILE // HALF))
            sub = pl.ds(r0 + s * TILE, TILE)
            chunk = [turn(dk_ref[sub, j * LANES : (j + 1) * LANES], cosine, -sine, first).astype(BF16) for j in range(width // LANES)]
            pieces.append(jnp.concatenate(chunk, axis=1))
        dk = jnp.concatenate(pieces, axis=0)
        dq = dq_ref[here, :]
        dv = dv_ref[here, :].astype(BF16)
        for part, piece in enumerate((dq, dk, dv)):
            dqkv_ref[here, part * half : (part + 1) * half] = piece[:, :half]
        grad_normed = nn(dq, w_ref[:width, :]) + nn(dk, w_ref[width : 2 * width, :]) + nn(dv, w_ref[2 * width :, :])
        xhat, inv = layer_stats(x_ref[here, :].astype(F32))
        gg_ref[...] += jnp.sum((grad_normed * xhat).reshape(rows // 8, 8, -1), axis=0)
        out_ref[here, :] = (gm_ref[here, :] + layer_back(grad_normed * gain, xhat, inv)).astype(BF16)
        return carry

    lax.fori_loop(0, x_ref.shape[0] // rows, body, 0)


def weight_grad(a_ref, b_ref, out_ref, columns):
    for c in range(0, a_ref.shape[1], columns):
        out_ref[c : c + columns, :] = tn(a_ref[:, c : c + columns], b_ref[...]).astype(out_ref.dtype)


def call(kernel, outs, *args, scratch=(), name=None):
    vmem = pl.BlockSpec(memory_space=pltpu.VMEM)
    smem = pl.BlockSpec(memory_space=pltpu.SMEM)
    return pl.pallas_call(
        kernel,
        out_shape=[jax.ShapeDtypeStruct(s, d) for s, d in outs],
        in_specs=[smem if a.dtype == jnp.int32 else vmem for a in args],
        out_specs=[vmem] * len(outs),
        scratch_shapes=list(scratch),
        compiler_params=pltpu.CompilerParams(vmem_limit_bytes=VMEM_LIMIT),
        name=name,
    )(*args)


def on_device(inputs, lengths, attn_gain, mlp_gain, qkv_weight, attn_weight, mlp_in_weight, mlp_out_weight, cotangent):
    n_tp = lax.axis_size("tp")
    n_ctx = lax.axis_size("ctx")
    tp = lax.axis_index("tp")
    ctx = lax.axis_index("ctx")
    seqs, local = inputs.shape[1], inputs.shape[2]
    width = inputs.shape[3]
    group = n_tp // 2
    mine = tp % seqs
    pair = tp // 2
    tables = tuple(jnp.asarray(t) for t in rope_constants(local * n_ctx))

    def gather(shard):
        full = lax.all_gather(shard, "shard", axis=2, tiled=True)
        full = lax.all_gather(full, "tp", axis=1, tiled=False)
        k, _, own, cols = full.shape
        full = full.reshape(k, 2, 2 * own, cols)
        first = lax.dynamic_index_in_dim(full, pair, 1, keepdims=False)
        second = lax.dynamic_index_in_dim(full, 1 - pair, 1, keepdims=False)
        return jnp.concatenate([first, second], axis=1).reshape(k * n_tp * own, cols)

    wqkv = gather(jnp.transpose(qkv_weight, (1, 2, 0)))
    wo = gather(attn_weight[None])
    wi = gather(jnp.transpose(mlp_in_weight, (1, 2, 0)))
    wm = gather(mlp_out_weight[None])
    gain1 = lax.all_gather(attn_gain, "shard", axis=0, tiled=True)[None]
    gain2 = lax.all_gather(mlp_gain, "shard", axis=0, tiled=True)[None]

    x_own = lax.dynamic_index_in_dim(inputs[0], mine, 0, keepdims=False)
    cot = lax.dynamic_index_in_dim(cotangent[0], mine, 0, keepdims=False)
    length = lax.dynamic_index_in_dim(lengths[0], mine, 0, keepdims=True)
    up = [(i, i + 1) for i in range(n_ctx - 1)]
    down = [(i + 1, i) for i in range(n_ctx - 1)]
    before = lax.ppermute(x_own[local - HALF :], "ctx", up)
    after = lax.ppermute(x_own[:HALF], "ctx", down)
    x_ext = jnp.concatenate([before, x_own, after], axis=0)
    ext = local + 2 * HALF
    block0 = ctx * (local // HALF) - 1
    pos0 = ctx * local
    scalars = jnp.stack([length[0], pos0.astype(jnp.int32), block0.astype(jnp.int32)])
    tiles = local // TILE
    chunks = width // LANES
    span = TILE + 2 * HALF

    def kernel_a(s_ref, x_ref, g_ref, w_ref, c0, s0, c1, s1, normed, q, k, v, p, ctx_out):
        phase_qkv(x_ref, g_ref, w_ref, (c0, s0, c1, s1), normed, q, k, v, s_ref[2], 384)
        phase_attend(q, k, v, p, ctx_out, s_ref[1], s_ref[0])

    wide = ((ext, width), BF16)
    tall = ((local, width), BF16)
    normed, q, k, v, probs, context = call(
        kernel_a,
        [wide, wide, wide, wide, ((tiles, chunks, 2 * TILE, span), BF16), tall],
        scalars, x_ext, gain1, wqkv, *tables,
        name="attend",
    )
    ff = wm.shape[0]
    ff_half = ff // 2

    def kernel_d(s_ref, x_ref, cot_ref, ctx_ref, g_ref, wo_ref, wi_ref, wm_ref, out, gm, gml, dctx, gg, dwm, dwi, go, nm, hid, dgu):
        phase_mlp(x_ref, cot_ref, ctx_ref, g_ref, wo_ref, wi_ref, wm_ref, out, gm, gml, go, nm, hid, dgu, dctx, gg, s_ref[1], s_ref[0], 256)
        weight_grad(hid, go, dwm, 192)
        weight_grad(dgu, nm, dwi, 384)

    layer_out, gm, gml, dctx, gain2_part, dwm, dwi = call(
        kernel_d,
        [tall, ((local, width), F32), tall, tall, ((8, width), F32), ((ff_half, width), F32), ((2 * ff_half, width), F32)],
        scalars, x_ext, cot, context, gain2, wo, wi, wm,
        scratch=[pltpu.VMEM((local, width), BF16), pltpu.VMEM((local, width), BF16), pltpu.VMEM((local, ff_half), BF16), pltpu.VMEM((local, 2 * ff_half), BF16)],
        name="feed_forward",
    )
    width_half = width // 2

    def kernel_e(s_ref, q_ref, k_ref, v_ref, p_ref, ctx_ref, dctx_ref, gml_ref, c0, s0, c1, s1, dq, dk, dv, dwo):
        phase_attend_back(q_ref, k_ref, v_ref, p_ref, ctx_ref, dctx_ref, (c0, s0, c1, s1), dq, dk, dv, s_ref[2])
        for c in range(0, width_half, LANES):
            dwo[c : c + LANES, :] = tn(ctx_ref[:, c : c + LANES], gml_ref[...])

    dq, dk, dv, dwo = call(
        kernel_e,
        [tall, ((ext, width), F32), ((ext, width), F32), ((width_half, width), F32)],
        scalars, q, k, v, probs, context, dctx, gml, *tables,
        name="attend_back",
    )
    rims = jnp.stack([dk, dv])
    to_lower = lax.ppermute(rims[:, :HALF], "ctx", down)
    to_upper = lax.ppermute(rims[:, ext - HALF :], "ctx", up)
    rims = rims[:, HALF : HALF + local]
    rims = jnp.concatenate([rims[:, :HALF] + to_upper, rims[:, HALF : local - HALF], rims[:, local - HALF :] + to_lower], axis=1)

    def kernel_g(s_ref, x_ref, n_ref, gm_ref, dq_ref, dk_ref, dv_ref, g_ref, w_ref, c0, s0, c1, s1, out, gg, dw, dqkv):
        phase_input(x_ref, gm_ref, dq_ref, dk_ref, dv_ref, g_ref, w_ref, (c0, s0, c1, s1), dqkv, out, gg, s_ref[2], 256, width_half)
        weight_grad(dqkv, n_ref, dw, 384)

    input_grad, gain1_part, dwqkv = call(
        kernel_g,
        [tall, ((8, width), F32), ((3 * width_half, width), F32)],
        scalars, x_own, normed[HALF : HALF + local], gm, dq, rims[0], rims[1], gain1, wqkv, *tables,
        scratch=[pltpu.VMEM((local, 3 * width_half), BF16)],
        name="input_back",
    )

    def both(own):
        turn_z = [(i, (i + 1) % n_tp) for i in range(n_tp)]
        other = lax.ppermute(own, "tp", turn_z)
        low = jnp.where(mine == 0, own, other)
        high = jnp.where(mine == 0, other, own)
        return jnp.stack([low, high])[None]

    def owned(grad, parts):
        g = grad.reshape(parts, 2, -1, grad.shape[-1])
        keep = lax.dynamic_index_in_dim(g, tp % 2, 1, keepdims=False)
        send = lax.dynamic_index_in_dim(g, 1 - tp % 2, 1, keepdims=False)
        swap = [(i, i ^ 1) for i in range(n_tp)]
        g = keep + lax.ppermute(send.astype(BF16), "tp", swap).astype(F32)
        g = lax.psum(g, "ctx")
        return lax.psum_scatter(g, "shard", scatter_dimension=2, tiled=True)

    qkv_grad = jnp.transpose(owned(dwqkv, 3), (2, 0, 1))
    attn_grad = owned(dwo, 1)[0]
    mlp_in_grad = jnp.transpose(owned(dwi, 2), (2, 0, 1))
    mlp_out_grad = owned(dwm, 1)[0]
    gains = jnp.stack([jnp.sum(gain1_part, 0), jnp.sum(gain2_part, 0)])
    gains = jnp.where(tp < 2, gains, 0.0)
    gains = lax.psum(gains, ("shard", "ctx", "tp"))
    share = width // (lax.axis_size("shard") * n_tp)
    gains = lax.dynamic_slice_in_dim(gains, (lax.axis_index("shard") * n_tp + tp) * share, share, axis=1)
    return (both(layer_out), both(input_grad), qkv_grad, attn_grad, mlp_in_grad, mlp_out_grad, gains[0], gains[1])


def solution(mesh):
    in_specs = (
        P("shard", None, "ctx", None),
        P("shard", None),
        P("shard"),
        P("shard"),
        P("shard", None, "tp"),
        P("tp", "shard"),
        P("shard", None, "tp"),
        P("tp", "shard"),
        P("shard", None, "ctx", None),
    )
    out_specs = (
        P("shard", None, "ctx", None),
        P("shard", None, "ctx", None),
        P("shard", None, "tp"),
        P("tp", "shard"),
        P("shard", None, "tp"),
        P("tp", "shard"),
        P(("shard", "tp")),
        P(("shard", "tp")),
    )
    return jax.shard_map(on_device, mesh=mesh, in_specs=in_specs, out_specs=out_specs, check_vma=False)
```

time: 1100 us -> 586 us (0.53)
  waiting for transfers between devices: 789 us -> 266 us
  Pallas kernels: 0 us -> 98.1 us
  matrix products: 88.2 us -> 0 us
  blocking collectives: 60 us -> 144 us
  other arithmetic: 76 us -> 27.1 us
  local copies, waits for them, and re-layouts: 56.3 us -> 27 us
    psum x5 -> x1, waiting for transfers between devices: 761 us -> 51 us  [owned(): g = lax.psum(g, 'ctx')]
    all_gather x0 -> x4, waiting for transfers between devices: none -> 153 us  [gather(): full = lax.all_gather(full, 'tp', axis=1, tiled=False)]
    pallas_call x0 -> x4, Pallas kernels: none -> 98.1 us  [call(): pl.pallas_call(kernel, out_shape=[jax.ShapeDtypeStruct(s, d) for s, d in...]
    dot_general x18 -> x0, matrix products: 88.2 us -> none  [the longest x1 14 us: on_device(): jnp.einsum('mnqhd,mnkhd->mnhqk', grad_context, values_tiled, preferred_el...]
    psum x1, blocking collectives: 6.7 us -> 93.3 us  [on_device(): gains = lax.psum(gains, ('shard', 'ctx', 'tp'))]
    ppermute x4 -> x10, waiting for transfers between devices: 1.52 us -> 61 us  [the longest x4 53.9 us: owned(): g = keep + lax.ppermute(send.astype(BF16), 'tp', swap).astype(F32)]
    reduce_sum x9 -> x2, other arithmetic: 32.6 us -> 0.02 us  [on_device(): gains = jnp.stack([jnp.sum(gain1_part, 0), jnp.sum(gain2_part, 0)])]
    reduce_scatter x4, waiting for transfers between devices: 25.6 us -> 0.02 us  [owned(): return lax.psum_scatter(g, 'shard', scatter_dimension=2, tiled=True)]
  transfers between devices with their start and end apart: 13 -> 19, of which waited for: 7 -> 10; matrix products, arithmetic and copies ran while one was open for 12% -> 7% of each run, Pallas kernels for 0% -> 3%
where the time goes in v1:
time: 586 us
  waiting for transfers between devices  266 us (45%)
  blocking collectives  144 us (25%)
  Pallas kernels  98.1 us (17%)
  other arithmetic  27.1 us (5%)
  local copies, waits for them, and re-layouts  27 us (5%)
  between operations  14.3 us (2%)
  starting transfers between devices  9.38 us (2%)
    all_gather x4, waiting for transfers between devices, gather(): full = lax.all_gather(full, 'tp', axis=1, tiled=False)  153 us
    pallas_call x4, Pallas kernels, call(): pl.pallas_call(kernel, out_shape=[jax.ShapeDtypeStruct(s, d) for s, d in...  98.1 us
    psum x1, blocking collectives, on_device(): gains = lax.psum(gains, ('shard', 'ctx', 'tp'))  93.3 us
    ppermute x4, waiting for transfers between devices, owned(): g = keep + lax.ppermute(send.astype(BF16), 'tp', swap).astype(F32)  53.9 us
    psum x1, waiting for transfers between devices, owned(): g = lax.psum(g, 'ctx')  51 us
    all_gather x4, blocking collectives, gather(): full = lax.all_gather(shard, 'shard', axis=2, tiled=True)  42.1 us
  transfers between devices with their start and end apart: 19, of which 10 were waited for; matrix products, arithmetic and copies ran while one was open for 7% of the time, Pallas kernels for 3%

profile of v1, /device:TPU:0, one launch (start us, length us, event | category | flops | bytes accessed | tf_op | source)
XLA Modules:
  0.0 585.7 jit_solution(1782093153556471929)
XLA Ops:
  7.2 9.6 %all-gather.1 = bf16[192,768]{1,0:T(8,128)(2,1)} all-gather(bf16[192,384]{1,0:T(8,128)(2,1)} %param.18), channel_id=3, replica_groups=mesh['shard'=2,'ctx'=4,'tp'=4] {'shard'}, dimensions={1}, use_global_device_ids=true | all-gather | bytes 442368 | tf_op jit(solution)/shard_map/all_gather | solution.py:274
  16.9 7.6 %all-gather.4 = bf16[288,768]{1,0:T(8,128)(2,1)} all-gather(bf16[288,384]{1,0:T(8,128)(2,1)} %param.20), channel_id=6, replica_groups=mesh['shard'=2,'ctx'=4,'tp'=4] {'shard'}, dimensions={1}, use_global_device_ids=true | all-gather | bytes 663552 | tf_op jit(solution)/shard_map/all_gather | solution.py:274
  24.6 13.8 %all_gather.43 = bf16[3,192,768]{2,1,0:T(8,128)(2,1)} all-gather(bf16[3,192,384]{2,1,0:T(8,128)(2,1)} %bitcast.121), channel_id=1, replica_groups=mesh['shard'=2,'ctx'=4,'tp'=4] {'shard'}, dimensions={2}, use_global_device_ids=true | all-gather | bytes 1327104 | tf_op jit(solution)/shard_map/all_gather | solution.py:274
  38.5 11.1 %all_gather.50 = bf16[2,288,768]{2,1,0:T(8,128)(2,1)} all-gather(bf16[2,288,384]{2,1,0:T(8,128)(2,1)} %bitcast.122), channel_id=1, replica_groups=mesh['shard'=2,'ctx'=4,'tp'=4] {'shard'}, dimensions={2}, use_global_device_ids=true | all-gather | bytes 1327104 | tf_op jit(solution)/shard_map/all_gather | solution.py:274
  49.7 1.0 dynamic-slice_bitcast_fusion.11
  50.6 1.3 collective-permute-start
  51.9 1.3 collective-permute-start.1
  53.3 0.6 constant_dynamic-slice_fusion.1
  53.9 4.3 all-gather.6
  58.2 4.5 all-gather.7
  62.7 1.5 dynamic-slice_bitcast_fusion.5.x_ref
  64.3 1.4 dynamic-slice_bitcast_fusion.4.cot_ref
  65.6 1.2 pad_add_fusion.s_ref
  66.8 1.3 pad_maximum_fusion.3.x_ref
  68.2 1.3 dynamic-slice_bitcast_fusion.9
  69.5 1.1 maximum_bitcast_fusion.3.wo_ref
  70.6 18.2 %all-gather.19.cloned.1.call-done = bf16[1152,768]{1,0:T(8,128)(2,1)} async-done(((bf16[288,768]{1,0:T(8,128)(2,1)}), bf16[1152,768]{1,0:T(8,128)(2,1)}) %all-gather.19.cloned.1.call-update) | async-done | bytes 1769488 | tf_op jit(solution)/shard_map/all_gather | solution.py:275
  88.8 1.5 dynamic-slice_bitcast_fusion.7
  90.3 1.4 maximum_bitcast_fusion.2.wm_ref
  91.7 67.5 %all-gather.13.cloned.1.call-done = bf16[3,768,768]{2,1,0:T(8,128)(2,1)} async-done(((bf16[3,192,768]{2,1,0:T(8,128)(2,1)}), bf16[3,768,768]{2,1,0:T(8,128)(2,1)}) %all-gather.13.cloned.1.call-update) | async-done | bytes 3538960 | tf_op jit(solution)/shard_map/all_gather | solution.py:275
  159.2 2.2 dynamic-slice_bitcast_fusion.3
  161.5 67.8 %all-gather.17.cloned.1.call-done = bf16[2,1152,768]{2,1,0:T(8,128)(2,1)} async-done(((bf16[2,288,768]{2,1,0:T(8,128)(2,1)}), bf16[2,1152,768]{2,1,0:T(8,128)(2,1)}) %all-gather.17.cloned.1.call-update) | async-done | bytes 3538960 | tf_op jit(solution)/shard_map/all_gather | solution.py:275
  229.3 2.2 dynamic-slice_bitcast_fusion.1
  231.5 2.1 pad_maximum_fusion.1
  233.6 2.0 pad_maximum_fusion.2
  235.5 23.7 %attend.1 = (bf16[1152,768]{1,0:T(8,128)(2,1)}, bf16[1152,768]{1,0:T(8,128)(2,1)}, bf16[1152,768]{1,0:T(8,128)(2,1)}, bf16[1152,768]{1,0:T(8,128)(2,1)}, bf16[8,...) custom-call(s32[3]{0:T(128)} %pad_add_fusion.s_ref, bf16[1152,768]{1,0:T(8,128)(2,1)} %pad_maximum_fusion.3.x_ref, ...), custom_call_target="tpu_custom_call" | custom-call | tf_op jit(solution)/shard_map/attend/pallas_call | solution.py:250
  259.2 30.8 %feed_forward.1 = (bf16[1024,768]{1,0:T(8,128)(2,1)}, f32[1024,768]{1,0:T(8,128)}, bf16[1024,768]{1,0:T(8,128)(2,1)}, bf16[1024,768]{1,0:T(8,128)(2,1)}, f32[8,7...) custom-call(s32[3]{0:T(128)} %pad_add_fusion.s_ref, bf16[1152,768]{1,0:T(8,128)(2,1)} %pad_maximum_fusion.3.x_ref, ...), custom_call_target="tpu_custom_call" | custom-call | tf_op jit(solution)/shard_map/feed_forward/pallas_call | solution.py:250
  290.0 27.1 %attend_back.1 = (bf16[1024,768]{1,0:T(8,128)(2,1)}, f32[1152,768]{1,0:T(8,128)}, f32[1152,768]{1,0:T(8,128)}, f32[384,768]{1,0:T(8,128)}) custom-call(s32[3]{0:T(128)} %pad_add_fusion.s_ref, bf16[1152,768]{1,0:T(8,128)(2,1)} %get-tuple-element.32.q_ref, bf16[1152,768]{1,0:T(8,128)(2,1)} %get-tuple-element.33.k_ref, ...), custom_call_target="tpu_custom_call" | custom-call | tf_op jit(solution)/shard_map/attend_back/pallas_call | solution.py:250
  317.2 1.2 fusion.6
  318.5 8.7 %collective-permute-done.7 = bf16[1,192,768]{2,1,0:T(8,128)(2,1)S(1)} collective-permute-done((bf16[1,192,768]{2,1,0:T(8,128)(2,1)S(1)}, bf16[1,192,768]{2,1,0:T(8,128)(2,1)S(1)}, u32[]{:S(2)}, u32[]{:S(2)}) %collective-permute-start.7) | collective-permute-done | bytes 294944 | tf_op jit(solution)/shard_map/ppermute | solution.py:375
  327.2 1.9 bitcast_add_fusion.3
  329.6 10.8 %collective-permute-done.9 = bf16[1,288,768]{2,1,0:T(8,128)(2,1)S(1)} collective-permute-done((bf16[1,288,768]{2,1,0:T(8,128)(2,1)S(1)}, bf16[1,288,768]{2,1,0:T(8,128)(2,1)S(1)}, u32[]{:S(2)}, u32[]{:S(2)}) %collective-permute-start.9) | collective-permute-done | bytes 442400 | tf_op jit(solution)/shard_map/ppermute | solution.py:375
  340.4 1.0 bitcast_add_fusion.2
  341.4 1.6 fusion.2
  343.0 0.7 collective-permute-start.8
  343.7 19.1 %collective-permute-done.8 = bf16[2,288,768]{2,1,0:T(8,128)(2,1)S(1)} collective-permute-done((bf16[2,288,768]{2,1,0:T(8,128)(2,1)S(1)}, bf16[2,288,768]{2,1,0:T(8,128)(2,1)S(1)}, u32[]{:S(2)}, u32[]{:S(2)}) %collective-permute-start.8) | collective-permute-done | bytes 884768 | tf_op jit(solution)/shard_map/ppermute | solution.py:375
  362.8 2.9 bitcast_add_fusion
  365.8 1.1 pad_maximum_fusion.5
  367.0 1.4 collective-permute-start.3
  368.4 1.3 collective-permute-done.3
  369.8 1.3 collective-permute-start.4
  371.1 1.3 slice.50.n_ref
  372.4 0.4 fusion
  372.8 5.8 collective-permute-done.4
  378.6 0.4 pad_maximum_fusion
  379.0 3.2 slice_bitcast_fusion
  382.2 16.5 %input_back.1 = (bf16[1024,768]{1,0:T(8,128)(2,1)}, f32[8,768]{1,0:T(8,128)}, f32[1152,768]{1,0:T(8,128)}) custom-call(s32[3]{0:T(128)} %pad_add_fusion.s_ref, bf16[1024,768]{1,0:T(8,128)(2,1)} %copy-done.4, bf16[1024,768]{1,0:T(8,128)(2,1)} %slice.50.n_ref, f32[1024,768]{1,0:T(8,128)} %get-tuple-element.31.gm_ref, ...), custom_call_target="tpu_custom_call" | custom-call | tf_op jit(solution)/shard_map/input_back/pallas_call | solution.py:250
  398.6 1.6 fusion.1
  400.3 1.0 collective-permute-start.6
  401.3 15.3 %collective-permute-done.6 = bf16[3,192,768]{2,1,0:T(8,128)(2,1)S(1)} collective-permute-done((bf16[3,192,768]{2,1,0:T(8,128)(2,1)S(1)}, bf16[3,192,768]{2,1,0:T(8,128)(2,1)S(1)}, u32[]{:S(2)}, u32[]{:S(2)}) %collective-permute-start.6) | collective-permute-done | bytes 884768 | tf_op jit(solution)/shard_map/ppermute | solution.py:375
  416.6 2.9 bitcast_add_fusion.1
  419.6 1.0 collective-permute-start.2
  420.6 0.6 collective-permute-start.5
  421.3 93.3 %psum.39 = f32[2,768]{1,0:T(2,128)S(1)} all-reduce(f32[2,768]{1,0:T(2,128)S(1)} %maximum_select_fusion), channel_id=1, replica_groups=mesh['shard'=2,'ctx'=4,'tp'=4] {'shard','ctx','tp'}, use_global_device_ids=true, to_apply=%region_10.11 | all-reduce | flops 1536 | bytes 12288 | tf_op jit(solution)/shard_map/psum | solution.py:385
  514.7 0.5 slice_bitcast_fusion.2
  515.3 1.6 select_bitcast_fusion.3
  516.9 1.9 maximum_bitcast_fusion
  518.8 1.7 select_bitcast_fusion.1
  520.6 1.9 maximum_bitcast_fusion.1
  522.5 51.0 %all-reduce.3.cloned.1.call-done = (f32[3,192,384]{2,1,0:T(8,128)}, f32[1,192,384]{2,1,0:T(8,128)}, f32[2,288,384]{2,1,0:T(8,128)}, f32[1,288,384]{2,1,0:T(8,128)}) async-done(((f32[3,192,384]{2,1,0:T(8,128)}, f32[1,192,384]{2,1,0:T(8,128)}, f32[2,288,384]{2,1,0:T(8,128)}, f32[1,288,384]{2,1,0:T(8,128)}), (f32[3,192,384]{2,1,0:T(8,128)}, f32[1,192,384]{2,1,0:T(8,128)}, f32[2,288,384]{2,1,0:T(8,128)}, ...) | async-done | bytes 2506768 | tf_op jit(solution)/shard_map/psum | solution.py:376
  573.5 2.3 copy.31
  575.8 1.7 copy.32
  577.4 0.9 copy.33
  578.4 0.8 copy.34
  (72 shorter events, 1.4 us)
Async XLA Ops:
  7.2 57.1 %copy-start = (bf16[1,2,1024,768]{3,2,1,0:T(8,128)(2,1)S(1)}, bf16[1,2,1024,768]{3,2,1,0:T(8,128)(2,1)}, u32[]{:S(2)}) copy-start(bf16[1,2,1024,768]{3,2,1,0:T(8,128)(2,1)} %param.21) | copy-start | bytes 9437188
  7.2 61.0 %all-gather.15.cloned.1.call-start = ((), (), s32[]{:S(2)}) async-start(), calls=%async_computation.5 | async-start | bytes 1474560 | tf_op jit(solution)/shard_map/all_gather | solution.py:275
  16.8 72.0 %all-gather.19.cloned.1.call-start = ((), (), s32[]{:S(2)}) async-start(), calls=%async_computation.7 | async-start | bytes 2211840 | tf_op jit(solution)/shard_map/all_gather | solution.py:275
  24.5 134.7 %all-gather.13.cloned.1.call-start = ((), (), s32[]{:S(2)}) async-start(), calls=%async_computation.4 | async-start | bytes 4423680 | tf_op jit(solution)/shard_map/all_gather | solution.py:275
  24.6 28.7 %copy-start.15 = (s32[1,2]{1,0:T(1,128)S(1)}, s32[1,2]{1,0:T(1,128)}, u32[]{:S(2)}) copy-start(s32[1,2]{1,0:T(1,128)} %param.14) | copy-start | bytes 28
  24.6 29.3 %copy-start.13 = (bf16[384]{0:T(512)(128)(2,1)S(1)}, bf16[384]{0:T(512)(128)(2,1)}, u32[]{:S(2)}) copy-start(bf16[384]{0:T(512)(128)(2,1)} %param.15) | copy-start | bytes 2308
  24.6 29.3 %copy-start.14 = (bf16[384]{0:T(512)(128)(2,1)S(1)}, bf16[384]{0:T(512)(128)(2,1)}, u32[]{:S(2)}) copy-start(bf16[384]{0:T(512)(128)(2,1)} %param.16) | copy-start | bytes 2308
  38.4 190.8 %all-gather.17.cloned.1.call-start = ((), (), s32[]{:S(2)}) async-start(), calls=%async_computation.6 | async-start | bytes 4423680 | tf_op jit(solution)/shard_map/all_gather | solution.py:275
  49.6 465.1 %reduce-scatter.7.cloned.1.call-start = ((), (), s32[]{:S(2)}) async-start(), calls=%async_computation.9 | async-start | bytes 884736 | tf_op jit(solution)/shard_map/reduce_scatter | solution.py:377
  50.6 16.2 %collective-permute-start = (bf16[64,768]{1,0:T(8,128)(2,1)S(1)}, bf16[64,768]{1,0:T(8,128)(2,1)S(1)}, u32[]{:S(2)}, u32[]{:S(2)}) collective-permute-start(bf16[64,768]{1,0:T(8,128)(2,1)S(1)} %get-tuple-element.64), channel_id=1, source_target_pairs={{0,4},{4,8},{8,12},{1,5},{5,9},{9,13},{2,6},{6,10},{10,14},{3,7},{... | collective-permute-start | bytes 294920 | tf_op jit(solution)/shard_map/ppermute | solution.py:294
  51.9 14.9 %collective-permute-start.1 = (bf16[64,768]{1,0:T(8,128)(2,1)S(1)}, bf16[64,768]{1,0:T(8,128)(2,1)S(1)}, u32[]{:S(2)}, u32[]{:S(2)}) collective-permute-start(bf16[64,768]{1,0:T(8,128)(2,1)S(1)} %get-tuple-element.65), channel_id=1, source_target_pairs={{4,0},{8,4},{12,8},{5,1},{9,5},{13,9},{6,2},{10,6},{14,10},{7,3},{... | collective-permute-start | bytes 294920 | tf_op jit(solution)/shard_map/ppermute | solution.py:295
  64.3 2.6 copy-start.4
  317.2 12.1 %copy-start.8 = (f32[576,768]{1,0:T(8,128)S(1)}, f32[576,768]{1,0:T(8,128)}, u32[]{:S(2)}) copy-start(f32[576,768]{1,0:T(8,128)} %get-tuple-element.45) | copy-start | bytes 5308420
  318.4 8.8 %collective-permute-start.7 = (bf16[1,192,768]{2,1,0:T(8,128)(2,1)S(1)}, bf16[1,192,768]{2,1,0:T(8,128)(2,1)S(1)}, u32[]{:S(2)}, u32[]{:S(2)}) collective-permute-start(bf16[1,192,768]{2,1,0:T(8,128)(2,1)S(1)} %fusion.6), channel_id=1, source_target_pairs={{0,1},{1,0},{2,3},{3,2},{4,5},{5,4},{6,7},{7,6},{8,9},{9,8},{10,11... | collective-permute-start | bytes 884744 | tf_op jit(solution)/shard_map/ppermute | solution.py:375
  329.2 185.5 %reduce-scatter.11.cloned.1.call-start = ((), (), s32[]{:S(2)}) async-start(), calls=%async_computation.11 | async-start | bytes 1327104 | tf_op jit(solution)/shard_map/reduce_scatter | solution.py:377
  329.3 11.1 %collective-permute-start.9 = (bf16[1,288,768]{2,1,0:T(8,128)(2,1)S(1)}, bf16[1,288,768]{2,1,0:T(8,128)(2,1)S(1)}, u32[]{:S(2)}, u32[]{:S(2)}) collective-permute-start(bf16[1,288,768]{2,1,0:T(8,128)(2,1)S(1)} %fusion.3), channel_id=1, source_target_pairs={{0,1},{1,0},{2,3},{3,2},{4,5},{5,4},{6,7},{7,6},{8,9},{9,8},{10,11... | collective-permute-start | bytes 1327112 | tf_op jit(solution)/shard_map/ppermute | solution.py:375
  341.4 173.3 %reduce-scatter.9.cloned.1.call-start = ((), (), s32[]{:S(2)}) async-start(), calls=%async_computation.10 | async-start | bytes 2654208 | tf_op jit(solution)/shard_map/reduce_scatter | solution.py:377
  343.0 22.8 %copy-start.2 = (f32[1152,768]{1,0:T(8,128)S(1)}, f32[1152,768]{1,0:T(8,128)}, u32[]{:S(2)}) copy-start(f32[1152,768]{1,0:T(8,128)} %get-tuple-element.39) | copy-start | bytes 10616836
  343.0 19.8 %collective-permute-start.8 = (bf16[2,288,768]{2,1,0:T(8,128)(2,1)S(1)}, bf16[2,288,768]{2,1,0:T(8,128)(2,1)S(1)}, u32[]{:S(2)}, u32[]{:S(2)}) collective-permute-start(bf16[2,288,768]{2,1,0:T(8,128)(2,1)S(1)} %fusion.2), channel_id=1, source_target_pairs={{0,1},{1,0},{2,3},{3,2},{4,5},{5,4},{6,7},{7,6},{8,9},{9,8},{10,11... | collective-permute-start | bytes 2654216 | tf_op jit(solution)/shard_map/ppermute | solution.py:375
  365.8 148.9 %reduce-scatter.5.cloned.1.call-start = ((), (), s32[]{:S(2)}) async-start(), calls=%async_computation.8 | async-start | bytes 2654208 | tf_op jit(solution)/shard_map/reduce_scatter | solution.py:377
  365.8 3.9 copy-start.3
  366.9 4.2 copy-start.7
  367.0 2.8 collective-permute-start.3
  369.8 8.7 %collective-permute-start.4 = (f32[2,64,768]{2,1,0:T(8,128)S(1)}, f32[2,64,768]{2,1,0:T(8,128)S(1)}, u32[]{:S(2)}, u32[]{:S(2)}) collective-permute-start(f32[2,64,768]{2,1,0:T(8,128)S(1)} %get-tuple-element.53), channel_id=1, source_target_pairs={{4,0},{8,4},{12,8},{5,1},{9,5},{13,9},{6,2},{10,6},{14,10},{7,3},{... | collective-permute-start | bytes 1179656 | tf_op jit(solution)/shard_map/ppermute | solution.py:346
  400.2 19.3 %copy-start.5 = (bf16[1024,768]{1,0:T(8,128)(2,1)S(1)}, bf16[1024,768]{1,0:T(8,128)(2,1)}, u32[]{:S(2)}) copy-start(bf16[1024,768]{1,0:T(8,128)(2,1)} %get-tuple-element.29) | copy-start | bytes 4718596
  400.2 20.4 %copy-start.6 = (bf16[1024,768]{1,0:T(8,128)(2,1)S(1)}, bf16[1024,768]{1,0:T(8,128)(2,1)}, u32[]{:S(2)}) copy-start(bf16[1024,768]{1,0:T(8,128)(2,1)} %get-tuple-element.41) | copy-start | bytes 4718596
  400.2 20.9 %copy-start.11 = (f32[8,768]{1,0:T(8,128)S(1)}, f32[8,768]{1,0:T(8,128)}, u32[]{:S(2)}) copy-start(f32[8,768]{1,0:T(8,128)} %get-tuple-element.47) | copy-start | bytes 73732
  400.2 21.0 %copy-start.12 = (f32[8,768]{1,0:T(8,128)S(1)}, f32[8,768]{1,0:T(8,128)}, u32[]{:S(2)}) copy-start(f32[8,768]{1,0:T(8,128)} %get-tuple-element.46) | copy-start | bytes 73732
  400.3 16.3 %collective-permute-start.6 = (bf16[3,192,768]{2,1,0:T(8,128)(2,1)S(1)}, bf16[3,192,768]{2,1,0:T(8,128)(2,1)S(1)}, u32[]{:S(2)}, u32[]{:S(2)}) collective-permute-start(bf16[3,192,768]{2,1,0:T(8,128)(2,1)S(1)} %fusion.1), channel_id=1, source_target_pairs={{0,1},{1,0},{2,3},{3,2},{4,5},{5,4},{6,7},{7,6},{8,9},{9,8},{10,11... | collective-permute-start | bytes 2654216 | tf_op jit(solution)/shard_map/ppermute | solution.py:375
  419.5 154.0 %all-reduce.3.cloned.1.call-start = ((), (), s32[]{:S(2)}) async-start(), calls=%async_computation.12 | async-start | bytes 5013504 | tf_op jit(solution)/shard_map/psum | solution.py:376
  419.6 95.7 %collective-permute-start.2 = (bf16[1024,768]{1,0:T(8,128)(2,1)S(1)}, bf16[1024,768]{1,0:T(8,128)(2,1)}, u32[]{:S(2)}, u32[]{:S(2)}) collective-permute-start(bf16[1024,768]{1,0:T(8,128)(2,1)S(1)} %copy-done.5), channel_id=1, source_target_pairs={{0,1},{1,2},{2,3},{3,0},{4,5},{5,6},{6,7},{7,4},{8,9},{9,10},{10,1... | collective-permute-start | bytes 4718600 | tf_op jit(solution)/shard_map/ppermute | solution.py:365
  420.6 98.2 %collective-permute-start.5 = (bf16[1024,768]{1,0:T(8,128)(2,1)S(1)}, bf16[1024,768]{1,0:T(8,128)(2,1)}, u32[]{:S(2)}, u32[]{:S(2)}) collective-permute-start(bf16[1024,768]{1,0:T(8,128)(2,1)S(1)} %copy-done.6), channel_id=1, source_target_pairs={{0,1},{1,2},{2,3},{3,0},{4,5},{5,6},{6,7},{7,4},{8,9},{9,10},{10,1... | collective-permute-start | bytes 4718600 | tf_op jit(solution)/shard_map/ppermute | solution.py:365
  573.5 4.0 copy-start.9
  573.5 4.9 copy-start.10
  573.5 5.7 copy-start.1
Sparse Core Ops, SparseCore 0:
  16.9 30.7 all-gather.14
  49.3 39.4 all-gather.18
  90.4 68.8 all-gather.12
  160.6 68.5 all-gather.16
  329.3 13.9 reduce-scatter.6
  346.1 18.5 reduce-scatter.10
  367.0 28.2 reduce-scatter.8
  419.6 35.2 reduce-scatter.4
  514.9 58.5 all-reduce.2

commit v2 on v1

--- a/solution.py
+++ b/solution.py
@@ -1,3 +1,4 @@
+import functools
 import math
 
 import numpy as np
@@ -79,34 +80,42 @@
     return jnp.concatenate([jnp.where(low_head, c, zero), jnp.where(low_head, zero, c)], axis=0)
 
 
-def phase_qkv(x_ref, gain_ref, w_ref, tables, normed_ref, q_ref, k_ref, v_ref, block0, rows):
-    width = x_ref.shape[1]
+def phase_norm(x_ref, gain_ref, normed_ref):
+    def body(t, carry):
+        r0 = pl.multiple_of(t * TILE, TILE)
+        xhat, _ = layer_stats(x_ref[pl.ds(r0, TILE), :].astype(F32))
+        normed_ref[pl.ds(r0, TILE), :] = (xhat * gain_ref[:1, :].astype(F32)).astype(BF16)
+        return carry
+
+    lax.fori_loop(0, x_ref.shape[0] // TILE, body, 0)
+
+
+def phase_qkv(normed_ref, w_ref, tables, q_ref, k_ref, v_ref, block0, rows, which):
+    width = normed_ref.shape[1]
+    half = width // 2
     scaling = 1.0 / math.sqrt(HD)
 
     def body(t, carry):
         r0 = pl.multiple_of(t * rows, rows)
-        xhat, _ = layer_stats(x_ref[pl.ds(r0, rows), :].astype(F32))
-        normed = (xhat * gain_ref[...].astype(F32)).astype(BF16)
-        normed_ref[pl.ds(r0, rows), :] = normed
-        for part, ref in enumerate((q_ref, k_ref, v_ref)):
-            out = nt(normed, w_ref[part * width : (part + 1) * width, :])
-            if part == 2:
-                ref[pl.ds(r0, rows), :] = out.astype(BF16)
-                continue
-            for s in range(rows // TILE):
-                cosine, sine, first = rope_tile(tables, block0 + t * (rows // HALF) + s * (TILE // HALF))
+        out = nt(normed_ref[pl.ds(r0, rows), :], w_ref[which].reshape(3 * half, width))
+        for s in range(rows // TILE):
+            here = pl.ds(r0 + s * TILE, TILE)
+            cosine, sine, first = rope_tile(tables, block0 + t * (rows // HALF) + s * (TILE // HALF))
+            for part, ref in enumerate((q_ref, k_ref)):
                 if part == 0:
-                    cosine, sine = cosine * scaling, sine * scaling
-                for j in range(width // LANES):
-                    u = out[s * TILE : (s + 1) * TILE, j * LANES : (j + 1) * LANES]
-                    ref[pl.ds(r0 + s * TILE, TILE), j * LANES : (j + 1) * LANES] = turn(u, cosine, sine, first).astype(BF16)
+                    turns = cosine * scaling, sine * scaling, first
+                else:
+                    turns = cosine, sine, first
+                for j in range(half // LANES):
+                    u = out[s * TILE : (s + 1) * TILE, part * half + j * LANES : part * half + (j + 1) * LANES]
+                    ref[here, which * half + j * LANES : which * half + (j + 1) * LANES] = turn(u, *turns).astype(BF16)
+        v_ref[pl.ds(r0, rows), which * half : (which + 1) * half] = out[:, 2 * half :].astype(BF16)
         return carry
 
-    lax.fori_loop(0, x_ref.shape[0] // rows, body, 0)
-
-
-def phase_attend(q_ref, k_ref, v_ref, p_ref, ctx_ref, pos0, length):
-    width = q_ref.shape[1]
+    lax.fori_loop(0, normed_ref.shape[0] // rows, body, 0)
+
+
+def phase_attend(q_ref, k_ref, v_ref, p_ref, ctx_ref, pos0, length, chunks, lo, hi):
     span = TILE + 2 * HALF
 
     def body(t, carry):
@@ -119,7 +128,7 @@
         bias = jnp.where(allowed, 0.0, masked_score).astype(F32)
         bias = jnp.concatenate([bias, bias], axis=0)
         low_head = head_masks((TILE, LANES))
-        for j in range(width // LANES):
+        for j in chunks:
             lanes = slice(j * LANES, (j + 1) * LANES)
             q2 = split_heads(q_ref[pl.ds(r0 + HALF, TILE), lanes], low_head)
             scores = nt(q2, k_ref[pl.ds(r0, span), lanes]) + bias
@@ -130,7 +139,7 @@
             ctx_ref[pl.ds(r0, TILE), lanes] = jnp.where(low_head, out[:TILE], out[TILE:]).astype(BF16)
         return carry
 
-    lax.fori_loop(0, ctx_ref.shape[0] // TILE, body, 0)
+    lax.fori_loop(lo, hi, body, 0)
 
 
 def phase_mlp(x_ref, cot_ref, ctx_ref, gain_ref, wo_ref, wi_ref, wm_ref, out_ref, gm_ref, gml_ref, go_ref, nm_ref, hid_ref, dgu_ref, dctx_ref, gg_ref, pos0, length, rows):
@@ -142,7 +151,7 @@
         r0 = pl.multiple_of(t * rows, rows)
         here = pl.ds(r0, rows)
         gain = gain_ref[...].astype(F32)
-        middle = x_ref[pl.ds(r0 + HALF, rows), :].astype(F32) + nn(ctx_ref[here, :], wo_ref[...])
+        middle = x_ref[here, :].astype(F32) + nn(ctx_ref[here, :], wo_ref[...])
         xhat, inv = layer_stats(middle)
         nm = (xhat * gain).astype(BF16)
         nm_ref[here, :] = nm
@@ -211,8 +220,9 @@
     lax.fori_loop(0, dq_ref.shape[0] // TILE, body, 0)
 
 
-def phase_input(x_ref, gm_ref, dq_ref, dk_ref, dv_ref, gain_ref, w_ref, tables, dqkv_ref, out_ref, gg_ref, block0, rows, half):
+def phase_input(x_ref, gm_ref, dq_ref, dk_ref, dv_ref, gain_ref, w_ref, tables, dqkv_ref, out_ref, gg_ref, block0, rows):
     width = x_ref.shape[1]
+    half = width // 2
     gg_ref[...] = jnp.zeros_like(gg_ref)
 
     def body(t, carry):
@@ -228,9 +238,10 @@
         dk = jnp.concatenate(pieces, axis=0)
         dq = dq_ref[here, :]
         dv = dv_ref[here, :].astype(BF16)
-        for part, piece in enumerate((dq, dk, dv)):
-            dqkv_ref[here, part * half : (part + 1) * half] = piece[:, :half]
-        grad_normed = nn(dq, w_ref[:width, :]) + nn(dk, w_ref[width : 2 * width, :]) + nn(dv, w_ref[2 * width :, :])
+        own = jnp.concatenate([g[:, :half] for g in (dq, dk, dv)], axis=1)
+        other = jnp.concatenate([g[:, half:] for g in (dq, dk, dv)], axis=1)
+        dqkv_ref[here, :] = own
+        grad_normed = nn(jnp.concatenate([own, other], axis=1), w_ref[...])
         xhat, inv = layer_stats(x_ref[here, :].astype(F32))
         gg_ref[...] += jnp.sum((grad_normed * xhat).reshape(rows // 8, 8, -1), axis=0)
         out_ref[here, :] = (gm_ref[here, :] + layer_back(grad_normed * gain, xhat, inv)).astype(BF16)
@@ -242,6 +253,303 @@
 def weight_grad(a_ref, b_ref, out_ref, columns):
     for c in range(0, a_ref.shape[1], columns):
         out_ref[c : c + columns, :] = tn(a_ref[:, c : c + columns], b_ref[...]).astype(out_ref.dtype)
+
+
+def slot_of(at, of):
+    return (of + 2 * (at // 2)) % 4
+
+
+class Place:
+    def __init__(self, n_shard):
+        self.split = n_shard == 2
+        self.x = lax.axis_index("shard")
+        self.c = lax.axis_index("ctx")
+        self.z = lax.axis_index("tp")
+        self.k = self.c % 2
+        self.y = self.c // 2
+        self.up = (self.z + 1) % 4
+        self.down = (self.z + 3) % 4
+        self.mate = self.z + 1 - 2 * (self.z % 2)
+        self.core = self.c + 1 - 2 * self.k
+        self.across = (self.c + 2) % 4
+        self.to_x = {"shard": 1 - self.x}
+        self.to_up = {"tp": self.up}
+        self.to_down = {"tp": self.down}
+        self.to_mate = {"tp": self.mate}
+        self.to_core = {"ctx": self.core}
+        self.to_y = {"ctx": self.across}
+        self.to_next = {"ctx": (self.c + 1) % 4}
+        self.to_prev = {"ctx": (self.c + 3) % 4}
+
+    def meet(self, partners):
+        barrier = pltpu.get_barrier_semaphore()
+        for device in partners:
+            pl.semaphore_signal(barrier, inc=1, device_id=device, device_id_type=pl.DeviceIdType.MESH)
+        pl.semaphore_wait(barrier, len(partners))
+
+
+class Wires:
+    def __init__(self, send, recv, base=0):
+        self.send, self.recv, self.next, self.open = send, recv, base, []
+
+    def go(self, src, dst, device):
+        i = self.next
+        self.next += 1
+        copy = pltpu.make_async_remote_copy(
+            src_ref=src, dst_ref=dst, send_sem=self.send.at[i], recv_sem=self.recv.at[i], device_id=device, device_id_type=pl.DeviceIdType.MESH
+        )
+        copy.start()
+        self.open.append(copy)
+        return copy
+
+    def own(self, src, dst):
+        i = self.next
+        self.next += 1
+        copy = pltpu.make_async_copy(src, dst, self.recv.at[i])
+        copy.start()
+        return copy
+
+    def close(self):
+        for copy in self.open:
+            copy.wait_send()
+        self.open = []
+
+
+def landed(copies):
+    for copy in copies:
+        copy.wait_recv()
+
+
+class Gather:
+    def __init__(self, shard, full, which, wires, here):
+        self.shard, self.full, self.which, self.wires, self.here = shard, full, which, wires, here
+        rows = shard.shape[0] // 6
+        self.mine = pl.ds(rows * here.c, rows)
+        self.rest = pl.ds(rows * (4 + here.k), rows)
+        self.theirs = pl.ds(rows * here.across, rows)
+        other = (here.z + 2) % 4
+        self.to = ([here.mate] if which != 1 else []) + ([other, other + 1 - 2 * (other % 2)] if which != 0 else [])
+        self.base = 2 if which == 1 else 0
+
+    def cols(self, x):
+        cols = self.shard.shape[1]
+        return pl.ds(pl.multiple_of(x * cols, LANES), cols) if self.here.split else pl.ds(0, cols)
+
+    def begin(self):
+        h, go = self.here, self.wires.go
+        cols = self.cols(h.x)
+        self.kept, self.spread = [], []
+        for rows in (self.rest, self.mine):
+            src = self.shard.at[rows, :]
+            for to in self.to:
+                self.spread.append(go(src, self.full.at[slot_of(to, h.z) - self.base, rows, cols], {"tp": to}))
+            if self.which != 1:
+                self.kept.append(self.wires.own(src, self.full.at[slot_of(h.z, h.z), rows, cols]))
+
+    def cross(self):
+        landed(self.spread)
+        for copy in self.kept:
+            copy.wait()
+        self.crossed = []
+        if self.here.split:
+            cols = self.cols(self.here.x)
+            for rows in (self.rest, self.mine):
+                block = self.full.at[:, rows, cols]
+                self.crossed.append(self.wires.go(block, block, self.here.to_x))
+
+    def share(self):
+        h, go = self.here, self.wires.go
+        landed(self.crossed)
+        mine, rest = self.full.at[:, self.mine, :], self.full.at[:, self.rest, :]
+        self.level = go(mine, mine, h.to_y)
+        self.pooled = [go(rest, rest, h.to_core), go(mine, mine, h.to_core)]
+
+    def relay(self):
+        landed([self.level])
+        theirs = self.full.at[:, self.theirs, :]
+        self.pooled.append(self.wires.go(theirs, theirs, self.here.to_core))
+
+    def end(self):
+        landed(self.pooled)
+
+
+class Reduce:
+    def __init__(self, grad, out, bufs, wires, here, x_first):
+        self.grad, self.out, self.wires, self.here = grad, out, wires, here
+        self.a, self.b, self.d, self.e, self.s1, self.s2, self.s3 = bufs
+        self.x_first = x_first and here.split
+        rows = grad.shape[2] // 2
+        self.keep = pl.ds(rows * here.k, rows)
+        self.give = pl.ds(rows * (1 - here.k), rows)
+        self.zs = here.z % 2
+
+    @staticmethod
+    def scratch(shape, n_shard, x_first):
+        k, two, rows, width = shape
+        split = n_shard == 2
+        cols = width // n_shard if split else width
+        half = rows // 2
+        if split and x_first:
+            middle = (k, two, half, cols)
+        else:
+            middle = (k, half, width)
+        last = (k, half, cols)
+        shapes = [(k, two, half, width), middle, last, last, (k, two, half, width), middle, last]
+        return [pltpu.VMEM(s, BF16) for s in shapes]
+
+    def cols(self, x):
+        cols = self.out.shape[2]
+        return pl.ds(pl.multiple_of(x * cols, LANES), cols)
+
+    def begin(self):
+        self.copy = self.wires.go(self.grad.at[:, :, self.give, :], self.a, self.here.to_core)
+
+    def first(self):
+        h = self.here
+        landed([self.copy])
+        self.s1[...] = (self.grad[:, :, self.keep, :].astype(F32) + self.a[...].astype(F32)).astype(BF16)
+        if self.x_first:
+            self.copy = self.wires.go(self.s1.at[:, :, :, self.cols(1 - h.x)], self.b, h.to_x)
+        else:
+            self.copy = self.wires.go(self.s1.at[:, 1 - self.zs, :, :], self.b, h.to_mate)
+
+    def second(self):
+        h = self.here
+        landed([self.copy])
+        if self.x_first:
+            own = self.s1[:, :, :, self.cols(h.x)]
+        else:
+            own = self.s1[:, self.zs, :, :]
+        total = (own.astype(F32) + self.b[...].astype(F32)).astype(BF16)
+        if not h.split:
+            self.s3[...] = total
+            self.copy = None
+            return
+        self.s2[...] = total
+        if self.x_first:
+            self.copy = self.wires.go(self.s2.at[:, 1 - self.zs, :, :], self.d, h.to_mate)
+        else:
+            self.copy = self.wires.go(self.s2.at[:, :, self.cols(1 - h.x)], self.d, h.to_x)
+
+    def third(self):
+        h = self.here
+        if self.copy is not None:
+            landed([self.copy])
+            if self.x_first:
+                own = self.s2[:, self.zs, :, :]
+            else:
+                own = self.s2[:, :, self.cols(h.x)]
+            self.s3[...] = (own.astype(F32) + self.d[...].astype(F32)).astype(BF16)
+        self.copy = self.wires.go(self.s3, self.e, h.to_y)
+
+    def fourth(self):
+        landed([self.copy])
+        self.out[:, self.keep, :] = (self.s3[...].astype(F32) + self.e[...].astype(F32)).astype(BF16)
+        done = self.out.at[:, self.keep, :]
+        self.copy = self.wires.go(done, done, self.here.to_core)
+
+    def end(self):
+        landed([self.copy])
+
+
+REDUCE_COPIES = 5
+
+
+def wavefront(jobs, names):
+    for step in range(len(jobs) + len(names) - 1):
+        for i, job in enumerate(jobs):
+            if 0 <= step - i < len(names):
+                getattr(job, names[step - i])()
+
+
+REDUCE_STAGES = ("begin", "first", "second", "third", "fourth", "end")
+
+
+def attend_kernel(n_shard, s_ref, x_ref, gains_ref, *refs):
+    shards, tables, refs = refs[:4], refs[4:8], refs[8:]
+    wqkv, wo, wi, wm, gains, normed, q, k, v, p, ctx, ext, send, recv = refs
+    h = Place(n_shard)
+    near = [{"tp": (h.z + i) % 4} for i in (1, 2, 3)] + [{"ctx": (h.c + i) % 4} for i in (1, 2, 3)]
+    if h.split:
+        near.append(h.to_x)
+    h.meet(near)
+    wires = Wires(send, recv)
+    local = x_ref.shape[2]
+    seq = x_ref.at[0, h.z % 2]
+    kept = [wires.own(seq, ext.at[pl.ds(HALF, local), :])]
+    rims = [
+        wires.go(seq.at[pl.ds(0, HALF), :], ext.at[pl.ds(HALF + local, HALF), :], h.to_prev),
+        wires.go(seq.at[pl.ds(local - HALF, HALF), :], ext.at[pl.ds(0, HALF), :], h.to_next),
+    ]
+    if h.split:
+        cols = gains_ref.shape[1]
+        mine = gains.at[:, pl.ds(pl.multiple_of(h.x * cols, LANES), cols)]
+        kept.append(wires.own(gains_ref, mine))
+        rims.append(wires.go(gains_ref, mine, h.to_x))
+    else:
+        kept.append(wires.own(gains_ref, gains))
+    near_jobs = [Gather(shards[0].at[i], wqkv.at[0, i], 0, wires, h) for i in range(3)]
+    far_jobs = [Gather(shards[0].at[i], wqkv.at[1, i], 1, wires, h) for i in range(3)]
+    late = [(1, wo, 0), (2, wi, 0), (2, wi, 1), (3, wm, 0)]
+    late = [Gather(shards[i].at[part], full.at[part], None, wires, h) for i, full, part in late]
+    run(near_jobs, "begin")
+    run(far_jobs, "begin")
+    run(late, "begin")
+    for copy in kept:
+        copy.wait()
+    landed(rims)
+    phase_norm(ext, gains, normed)
+    run(near_jobs, "cross")
+    run(near_jobs, "share")
+    run(near_jobs, "relay")
+    run(near_jobs, "end")
+    run(far_jobs, "cross")
+    qkv = functools.partial(phase_qkv, normed, wqkv, tables, q, k, v, s_ref[2], 384)
+    attend = functools.partial(phase_attend, q, k, v, p, ctx, s_ref[1], s_ref[0])
+    tiles = local // TILE
+    half = p.shape[1] // 2
+    qkv(0)
+    run(far_jobs, "share")
+    run(late[:1], "cross")
+    attend(range(half), 0, tiles // 2)
+    run(far_jobs, "relay")
+    run(late[:1], "share")
+    run(late[1:2], "cross")
+    attend(range(half), tiles // 2, tiles)
+    run(far_jobs, "end")
+    run(late[:1], "relay")
+    run(late[1:2], "share")
+    run(late[2:3], "cross")
+    qkv(1)
+    run(late[:1], "end")
+    run(late[1:2], "relay")
+    run(late[2:3], "share")
+    run(late[3:4], "cross")
+    attend(range(half, 2 * half), 0, tiles // 2)
+    run(late[2:3], "relay")
+    run(late[3:4], "share")
+    attend(range(half, 2 * half), tiles // 2, tiles)
+    run(late[3:4], "relay")
+    run(late[1:4], "end")
+    wires.close()
+
+
+def run(jobs, stage):
+    for job in jobs:
+        getattr(job, stage)()
+
+
+def reduce_kernel(n_shard, n, *refs):
+    grads, outs, (send, recv), bufs = refs[:n], refs[n : 2 * n], refs[2 * n : 2 * n + 2], refs[2 * n + 2 :]
+    h = Place(n_shard)
+    near = [h.to_mate, h.to_core, h.to_y]
+    if h.split:
+        near.append(h.to_x)
+    h.meet(near)
+    wires = Wires(send, recv)
+    jobs = [Reduce(g, o, bufs[7 * i : 7 * i + 7], wires, h, i % 2 == 0) for i, (g, o) in enumerate(zip(grads, outs))]
+    wavefront(jobs, REDUCE_STAGES)
+    wires.close()
 
 
 def call(kernel, outs, *args, scratch=(), name=None):
@@ -270,50 +578,49 @@
     pair = tp // 2
     tables = tuple(jnp.asarray(t) for t in rope_constants(local * n_ctx))
 
-    def gather(shard):
-        full = lax.all_gather(shard, "shard", axis=2, tiled=True)
-        full = lax.all_gather(full, "tp", axis=1, tiled=False)
-        k, _, own, cols = full.shape
-        full = full.reshape(k, 2, 2 * own, cols)
-        first = lax.dynamic_index_in_dim(full, pair, 1, keepdims=False)
-        second = lax.dynamic_index_in_dim(full, 1 - pair, 1, keepdims=False)
-        return jnp.concatenate([first, second], axis=1).reshape(k * n_tp * own, cols)
-
-    wqkv = gather(jnp.transpose(qkv_weight, (1, 2, 0)))
-    wo = gather(attn_weight[None])
-    wi = gather(jnp.transpose(mlp_in_weight, (1, 2, 0)))
-    wm = gather(mlp_out_weight[None])
-    gain1 = lax.all_gather(attn_gain, "shard", axis=0, tiled=True)[None]
-    gain2 = lax.all_gather(mlp_gain, "shard", axis=0, tiled=True)[None]
-
-    x_own = lax.dynamic_index_in_dim(inputs[0], mine, 0, keepdims=False)
-    cot = lax.dynamic_index_in_dim(cotangent[0], mine, 0, keepdims=False)
+    n_shard = lax.axis_size("shard")
+    shards = [jnp.transpose(qkv_weight, (1, 2, 0)), attn_weight[None], jnp.transpose(mlp_in_weight, (1, 2, 0)), mlp_out_weight[None]]
+    gains = jnp.pad(jnp.stack([attn_gain, mlp_gain]), ((0, 14), (0, 0)))
+    if n_shard != 2:
+        shards = [lax.all_gather(s, "shard", axis=2, tiled=True) for s in shards]
+        gains = lax.all_gather(gains, "shard", axis=1, tiled=True)
+    hbm = pl.BlockSpec(memory_space=pl.ANY)
+    vmem = pl.BlockSpec(memory_space=pltpu.VMEM)
+    smem = pl.BlockSpec(memory_space=pltpu.SMEM)
     length = lax.dynamic_index_in_dim(lengths[0], mine, 0, keepdims=True)
-    up = [(i, i + 1) for i in range(n_ctx - 1)]
-    down = [(i + 1, i) for i in range(n_ctx - 1)]
-    before = lax.ppermute(x_own[local - HALF :], "ctx", up)
-    after = lax.ppermute(x_own[:HALF], "ctx", down)
-    x_ext = jnp.concatenate([before, x_own, after], axis=0)
-    ext = local + 2 * HALF
     block0 = ctx * (local // HALF) - 1
     pos0 = ctx * local
     scalars = jnp.stack([length[0], pos0.astype(jnp.int32), block0.astype(jnp.int32)])
+    ext = local + 2 * HALF
     tiles = local // TILE
     chunks = width // LANES
     span = TILE + 2 * HALF
-
-    def kernel_a(s_ref, x_ref, g_ref, w_ref, c0, s0, c1, s1, normed, q, k, v, p, ctx_out):
-        phase_qkv(x_ref, g_ref, w_ref, (c0, s0, c1, s1), normed, q, k, v, s_ref[2], 384)
-        phase_attend(q, k, v, p, ctx_out, s_ref[1], s_ref[0])
-
     wide = ((ext, width), BF16)
     tall = ((local, width), BF16)
-    normed, q, k, v, probs, context = call(
-        kernel_a,
-        [wide, wide, wide, wide, ((tiles, chunks, 2 * TILE, span), BF16), tall],
-        scalars, x_ext, gain1, wqkv, *tables,
+    outs = [
+        ((2, 3, 2, shards[0].shape[1], width), BF16),
+        *(((s.shape[0], n_tp, s.shape[1], width), BF16) for s in shards[1:]),
+        ((16, width), BF16),
+        wide, wide, wide, wide,
+        ((tiles, chunks, 2 * TILE, span), BF16),
+        tall,
+    ]
+    copies = 124
+    wqkv, wo, wi, wm, gains, normed, q, k, v, probs, context = pl.pallas_call(
+        functools.partial(attend_kernel, n_shard),
+        out_shape=[jax.ShapeDtypeStruct(*o) for o in outs],
+        in_specs=[smem] + [hbm] * 6 + [vmem] * 4,
+        out_specs=[vmem] + [hbm] * 3 + [vmem] * 7,
+        scratch_shapes=[pltpu.VMEM((ext, width), BF16), pltpu.SemaphoreType.DMA((copies,)), pltpu.SemaphoreType.DMA((copies,))],
+        compiler_params=pltpu.CompilerParams(collective_id=0, has_side_effects=True, vmem_limit_bytes=VMEM_LIMIT),
         name="attend",
-    )
+    )(scalars, inputs, gains, *shards, *tables)
+    wqkv, wo, wi, wm = (f.reshape(-1, width) for f in (wqkv, wo, wi, wm))
+    gain1, gain2 = gains[:1], gains[1:2]
+    x_own = lax.dynamic_index_in_dim(inputs[0], mine, 0, keepdims=False)
+    cot = lax.dynamic_index_in_dim(cotangent[0], mine, 0, keepdims=False)
+    up = [(i, i + 1) for i in range(n_ctx - 1)]
+    down = [(i + 1, i) for i in range(n_ctx - 1)]
     ff = wm.shape[0]
     ff_half = ff // 2
 
@@ -324,8 +631,8 @@
 
     layer_out, gm, gml, dctx, gain2_part, dwm, dwi = call(
         kernel_d,
-        [tall, ((local, width), F32), tall, tall, ((8, width), F32), ((ff_half, width), F32), ((2 * ff_half, width), F32)],
-        scalars, x_ext, cot, context, gain2, wo, wi, wm,
+        [tall, ((local, width), F32), tall, tall, ((8, width), F32), ((ff_half, width), BF16), ((2 * ff_half, width), BF16)],
+        scalars, x_own, cot, context, gain2, wo, wi, wm,
         scratch=[pltpu.VMEM((local, width), BF16), pltpu.VMEM((local, width), BF16), pltpu.VMEM((local, ff_half), BF16), pltpu.VMEM((local, 2 * ff_half), BF16)],
         name="feed_forward",
     )
@@ -334,11 +641,11 @@
     def kernel_e(s_ref, q_ref, k_ref, v_ref, p_ref, ctx_ref, dctx_ref, gml_ref, c0, s0, c1, s1, dq, dk, dv, dwo):
         phase_attend_back(q_ref, k_ref, v_ref, p_ref, ctx_ref, dctx_ref, (c0, s0, c1, s1), dq, dk, dv, s_ref[2])
         for c in range(0, width_half, LANES):
-            dwo[c : c + LANES, :] = tn(ctx_ref[:, c : c + LANES], gml_ref[...])
+            dwo[c : c + LANES, :] = tn(ctx_ref[:, c : c + LANES], gml_ref[...]).astype(BF16)
 
     dq, dk, dv, dwo = call(
         kernel_e,
-        [tall, ((ext, width), F32), ((ext, width), F32), ((width_half, width), F32)],
+        [tall, ((ext, width), F32), ((ext, width), F32), ((width_half, width), BF16)],
         scalars, q, k, v, probs, context, dctx, gml, *tables,
         name="attend_back",
     )
@@ -349,42 +656,48 @@
     rims = jnp.concatenate([rims[:, :HALF] + to_upper, rims[:, HALF : local - HALF], rims[:, local - HALF :] + to_lower], axis=1)
 
     def kernel_g(s_ref, x_ref, n_ref, gm_ref, dq_ref, dk_ref, dv_ref, g_ref, w_ref, c0, s0, c1, s1, out, gg, dw, dqkv):
-        phase_input(x_ref, gm_ref, dq_ref, dk_ref, dv_ref, g_ref, w_ref, (c0, s0, c1, s1), dqkv, out, gg, s_ref[2], 256, width_half)
+        phase_input(x_ref, gm_ref, dq_ref, dk_ref, dv_ref, g_ref, w_ref, (c0, s0, c1, s1), dqkv, out, gg, s_ref[2], 256)
         weight_grad(dqkv, n_ref, dw, 384)
 
     input_grad, gain1_part, dwqkv = call(
         kernel_g,
-        [tall, ((8, width), F32), ((3 * width_half, width), F32)],
+        [tall, ((8, width), F32), ((3 * width_half, width), BF16)],
         scalars, x_own, normed[HALF : HALF + local], gm, dq, rims[0], rims[1], gain1, wqkv, *tables,
         scratch=[pltpu.VMEM((local, 3 * width_half), BF16)],
         name="input_back",
     )
 
     def both(own):
-        turn_z = [(i, (i + 1) % n_tp) for i in range(n_tp)]
-        other = lax.ppermute(own, "tp", turn_z)
+        other = lax.ppermute(own, "tp", [(i, i ^ 1) for i in range(n_tp)])
         low = jnp.where(mine == 0, own, other)
         high = jnp.where(mine == 0, other, own)
         return jnp.stack([low, high])[None]
 
-    def owned(grad, parts):
-        g = grad.reshape(parts, 2, -1, grad.shape[-1])
-        keep = lax.dynamic_index_in_dim(g, tp % 2, 1, keepdims=False)
-        send = lax.dynamic_index_in_dim(g, 1 - tp % 2, 1, keepdims=False)
-        swap = [(i, i ^ 1) for i in range(n_tp)]
-        g = keep + lax.ppermute(send.astype(BF16), "tp", swap).astype(F32)
-        g = lax.psum(g, "ctx")
-        return lax.psum_scatter(g, "shard", scatter_dimension=2, tiled=True)
-
-    qkv_grad = jnp.transpose(owned(dwqkv, 3), (2, 0, 1))
-    attn_grad = owned(dwo, 1)[0]
-    mlp_in_grad = jnp.transpose(owned(dwi, 2), (2, 0, 1))
-    mlp_out_grad = owned(dwm, 1)[0]
-    gains = jnp.stack([jnp.sum(gain1_part, 0), jnp.sum(gain2_part, 0)])
-    gains = jnp.where(tp < 2, gains, 0.0)
-    gains = lax.psum(gains, ("shard", "ctx", "tp"))
-    share = width // (lax.axis_size("shard") * n_tp)
-    gains = lax.dynamic_slice_in_dim(gains, (lax.axis_index("shard") * n_tp + tp) * share, share, axis=1)
+    gain_rows = jnp.concatenate([gain1_part, gain2_part]).astype(BF16)
+    gain_rows = jnp.broadcast_to(gain_rows[None, None], (1, 2, 16, width))
+    grads = [g.reshape(k, 2, -1, width) for g, k in ((dwqkv, 3), (dwi, 2), (dwo, 1), (dwm, 1))]
+    grads.append(jnp.concatenate([gain_rows, gain_rows], axis=2))
+    cols = width // n_shard if n_shard == 2 else width
+    sends = REDUCE_COPIES * len(grads)
+    owned = pl.pallas_call(
+        functools.partial(reduce_kernel, n_shard, len(grads)),
+        out_shape=[jax.ShapeDtypeStruct((g.shape[0], g.shape[2], cols), BF16) for g in grads],
+        in_specs=[vmem] * len(grads),
+        out_specs=[vmem] * len(grads),
+        scratch_shapes=[pltpu.SemaphoreType.DMA((sends,)), pltpu.SemaphoreType.DMA((sends,))]
+        + [b for i, g in enumerate(grads) for b in Reduce.scratch(g.shape, n_shard, i % 2 == 0)],
+        compiler_params=pltpu.CompilerParams(collective_id=1, has_side_effects=True, vmem_limit_bytes=VMEM_LIMIT),
+        name="reduce",
+    )(*grads)
+    owned = [g.astype(F32) for g in owned]
+    if n_shard != 2:
+        owned = [lax.psum_scatter(g, "shard", scatter_dimension=2, tiled=True) for g in owned]
+    qkv_grad = jnp.transpose(owned[0], (2, 0, 1))
+    mlp_in_grad = jnp.transpose(owned[1], (2, 0, 1))
+    attn_grad, mlp_out_grad = owned[2][0], owned[3][0]
+    share = owned[4].shape[2] // n_tp
+    gains = lax.dynamic_slice_in_dim(owned[4][0, :16], tp * share, share, axis=1)
+    gains = jnp.sum(gains.reshape(2, 8, share), axis=1)
     return (both(layer_out), both(input_grad), qkv_grad, attn_grad, mlp_in_grad, mlp_out_grad, gains[0], gains[1])
 
 

time: 586 us -> 289 us (0.49)
  waiting for transfers between devices: 266 us -> 25.3 us
  blocking collectives: 144 us -> 0 us
  Pallas kernels: 98.1 us -> 220 us
  between operations: 14.3 us -> 0.76 us
  local copies, waits for them, and re-layouts: 27 us -> 14.1 us
    all_gather x4 -> x0, waiting for transfers between devices: 153 us -> none  [gather(): full = lax.all_gather(full, 'tp', axis=1, tiled=False)]
    pallas_call x0 -> x2, Pallas kernels: none -> 146 us  [the longest x1 80.1 us: on_device(): pl.pallas_call(functools.partial(attend_kernel, n_shard), out_shape=[jax....]
    psum x1 -> x0, blocking collectives: 93.3 us -> none  [on_device(): gains = lax.psum(gains, ('shard', 'ctx', 'tp'))]
    psum x1 -> x0, waiting for transfers between devices: 51 us -> none  [owned(): g = lax.psum(g, 'ctx')]
    all_gather x6 -> x0, blocking collectives: 50.9 us -> none  [the longest x4 42.1 us: gather(): full = lax.all_gather(shard, 'shard', axis=2, tiled=True)]
    ppermute x8 -> x2, waiting for transfers between devices: 53.9 us -> 23.1 us  [both(): other = lax.ppermute(own, 'tp', [(i, i ^ 1) for i in range(n_tp)])]
    pallas_call x4 -> x3, Pallas kernels: 98.1 us -> 73.5 us  [call(): pl.pallas_call(kernel, out_shape=[jax.ShapeDtypeStruct(s, d) for s, d in...]
    squeeze x5 -> x0, local copies, waits for them, and re-layouts: 8.87 us -> none  [the longest x4 7.35 us: gather(): first = lax.dynamic_index_in_dim(full, pair, 1, keepdims=False)]
  transfers between devices with their start and end apart: 19 -> 4, of which waited for: 10 -> 3; matrix products, arithmetic and copies ran while one was open for 7% -> 8% of each run, Pallas kernels for 3% -> 28%
where the time goes in v2:
time: 289 us
  Pallas kernels  220 us (76%)
  waiting for transfers between devices  25.3 us (9%)
  other arithmetic  23.3 us (8%)
  local copies, waits for them, and re-layouts  14.1 us (5%)
  starting transfers between devices  5.76 us (2%)
    pallas_call x1, Pallas kernels, on_device(): pl.pallas_call(functools.partial(attend_kernel, n_shard), out_shape=[jax....  80.1 us
    pallas_call x3, Pallas kernels, call(): pl.pallas_call(kernel, out_shape=[jax.ShapeDtypeStruct(s, d) for s, d in...  73.5 us
    pallas_call x1, Pallas kernels, on_device(): pl.pallas_call(functools.partial(reduce_kernel, n_shard, len(grads)), out...  66 us
    ppermute x2, waiting for transfers between devices, both(): other = lax.ppermute(own, 'tp', [(i, i ^ 1) for i in range(n_tp)])  23.1 us
  transfers between devices with their start and end apart: 4, of which 3 were waited for; matrix products, arithmetic and copies ran while one was open for 8% of the time, Pallas kernels for 28%

profile of v2, /device:TPU:0, one launch (start us, length us, event | category | flops | bytes accessed | tf_op | source)
XLA Modules:
  0.0 288.8 jit_solution(1933818417251528276)
XLA Ops:
  0.6 0.0 copy-start
  0.7 0.7 stack.48
  1.4 0.7 stack.49
  2.0 0.0 copy-done
  2.0 0.6 constant_dynamic-slice_fusion
  2.6 0.6 fusion.5.gains_ref
  3.2 3.7 %dynamic-slice_bitcast_fusion = (bf16[1024,768]{1,0:T(8,128)(2,1)}, bf16[1024,768]{1,0:T(8,128)(2,1)}) fusion(bf16[1,2,1024,768]{3,2,1,0:T(8,128)(2,1)} %param.21, s32[]{:T(128)S(6)} %select_n.39, bf16[1,2,1024,768]{3,2,1,0:T(8,128)(2,1)} %x_ref.1), kind=kLoop, calls=%fused_computation.14 | loop fusion | bytes 6291460 | tf_op jit(solution)/shard_map/jit(dynamic_index_in_dim)/squeeze | solution.py:621
  7.0 1.3 pad_add_fusion.s_ref
  8.2 80.1 %attend.1 = (bf16[2,3,2,192,768]{4,3,2,1,0:T(8,128)(2,1)}, bf16[1,4,192,768]{3,2,1,0:T(8,128)(2,1)}, bf16[2,4,288,768]{3,2,1,0:T(8,128)(2,1)}, bf16[1,4,288,768]...) custom-call(s32[3]{0:T(128)} %pad_add_fusion.s_ref, ...), custom_call_target="tpu_custom_call" | custom-call | tf_op jit(solution)/shard_map/attend/pallas_call | solution.py:609
  88.4 1.4 fusion.6
  89.7 30.5 %feed_forward.1 = (bf16[1024,768]{1,0:T(8,128)(2,1)}, f32[1024,768]{1,0:T(8,128)}, bf16[1024,768]{1,0:T(8,128)(2,1)}, bf16[1024,768]{1,0:T(8,128)(2,1)}, f32[8,7...) custom-call(s32[3]{0:T(128)} %pad_add_fusion.s_ref, bf16[1024,768]{1,0:T(8,128)(2,1)} %get-tuple-element.81.x_ref, ...), custom_call_target="tpu_custom_call" | custom-call | tf_op jit(solution)/shard_map/feed_forward/pallas_call | solution.py:558
  120.2 26.9 %attend_back.1 = (bf16[1024,768]{1,0:T(8,128)(2,1)}, f32[1152,768]{1,0:T(8,128)}, f32[1152,768]{1,0:T(8,128)}, bf16[384,768]{1,0:T(8,128)(2,1)}) custom-call(s32[3]{0:T(128)} %pad_add_fusion.s_ref, bf16[1152,768]{1,0:T(8,128)(2,1)} %get-tuple-element.46.q_ref, bf16[1152,768]{1,0:T(8,128)(2,1)} %get-tuple-element.47.k_ref, ...), custom_call_target="tpu_custom_call" | custom-call | tf_op jit(solution)/shard_map/attend_back/pallas_call | solution.py:558
  147.1 0.0 copy-start.2
  147.1 0.0 copy-start.3
  147.1 1.2 pad_maximum_fusion.2
  148.3 2.7 collective-permute-start.1
  151.0 1.3 collective-permute-done.1
  152.3 0.0 copy-done.2
  152.3 0.0 copy-done.3
  152.3 0.9 maximum_add_fusion
  153.3 1.3 collective-permute-start.2
  154.6 0.1 collective-permute-start
  154.7 0.0 copy-start.7
  154.7 2.7 slice.47.n_ref
  157.4 0.0 copy-done.7
  157.4 0.0 copy-start.4
  157.4 2.6 fusion
  160.0 0.0 copy-start.5
  160.0 0.9 collective-permute-done.2
  160.9 0.0 copy-done.4
  160.9 1.1 fusion.2
  162.0 0.0 copy-done.5
  162.0 0.4 pad_maximum_fusion
  162.4 3.1 %slice_bitcast_fusion = (f32[1024,768]{1,0:T(8,128)}, f32[1024,768]{1,0:T(8,128)}) fusion(f32[2,1024,768]{2,1,0:T(8,128)S(1)} %pad_maximum_fusion), kind=kLoop, calls=%fused_computation.6 | loop fusion | bytes 12582912 | tf_op jit(solution)/shard_map/squeeze | solution.py:665
  165.5 16.2 %input_back.1 = (bf16[1024,768]{1,0:T(8,128)(2,1)}, f32[8,768]{1,0:T(8,128)}, bf16[1152,768]{1,0:T(8,128)(2,1)}) custom-call(s32[3]{0:T(128)} %pad_add_fusion.s_ref, bf16[1024,768]{1,0:T(8,128)(2,1)} %get-tuple-element.81.x_ref, bf16[1024,768]{1,0:T(8,128)(2,1)} %slice.47.n_ref, f32[1024,768]{1,0:T(8,128)} %get-tuple-element.45.gm_ref, ...), custom_call_target="tpu_custom_call" | custom-call | tf_op jit(solution)/shard_map/input_back/pallas_call | solution.py:558
  181.7 0.0 copy-start.6
  181.7 0.9 convert.11
  182.6 0.6 pad_maximum_fusion.3.refs_4_
  183.2 66.0 %reduce.1 = (bf16[3,192,384]{2,1,0:T(8,128)(2,1)}, bf16[2,288,384]{2,1,0:T(8,128)(2,1)}, bf16[1,192,384]{2,1,0:T(8,128)(2,1)}, bf16[1,288,384]{2,1,0:T(8,128)(2,1)}, bf16[1,32,384]{2,1,0:T(8,128)(2,1)}) custom-call(bf16[3,2,192,768]{3,2,1,0:T(8,128)(2,1)} %bitcast.64, bf16[2,2,288,768]{3,2,1,0:T(8,128)(2,1)} %bitcast.63, bf16[1,2,192,768]{3,2,1,0:T(8,128)(2,1)} %bitcast.68, ...), custom_call_target="tpu_custom_call" | custom-call | tf_op jit(solution)/shard_map/reduce/pallas_call | solution.py:682
  249.2 0.7 slice.56
  249.9 0.0 copy-done.6
  249.9 1.6 collective-permute-start.3
  251.6 0.1 bitcast_reduce_fusion
  251.7 0.5 slice_bitcast_fusion.2
  252.2 1.6 bitcast_convert_fusion.1
  253.8 1.7 bitcast_convert_fusion
  255.6 2.0 convert_bitcast_fusion.1
  257.5 2.0 convert_bitcast_fusion
  259.5 0.0 collective-permute-done
  259.5 2.1 select_bitcast_fusion.3
  261.6 1.9 maximum_bitcast_fusion
  263.6 23.1 %collective-permute-done.3 = bf16[1024,768]{1,0:T(8,128)(2,1)S(1)} collective-permute-done((bf16[1024,768]{1,0:T(8,128)(2,1)S(1)}, bf16[1024,768]{1,0:T(8,128)(2,1)S(1)}, u32[]{:S(2)}, u32[]{:S(2)}) %collective-permute-start.3) | collective-permute-done | bytes 1572896 | tf_op jit(solution)/shard_map/ppermute | solution.py:671
  286.6 0.2 select_bitcast_fusion.1
  286.8 0.0 copy-start.1
  286.8 1.9 maximum_bitcast_fusion.1
  288.8 0.0 copy-done.1
  (3 shorter events, 0.0 us)
Async XLA Ops:
  0.6 1.4 copy-start
  147.1 5.3 %copy-start.2 = (f32[1152,768]{1,0:T(8,128)S(1)}, f32[1152,768]{1,0:T(8,128)}, u32[]{:S(2)}) copy-start(f32[1152,768]{1,0:T(8,128)} %get-tuple-element.53) | copy-start | bytes 10616836
  147.1 5.3 %copy-start.3 = (f32[1152,768]{1,0:T(8,128)S(1)}, f32[1152,768]{1,0:T(8,128)}, u32[]{:S(2)}) copy-start(f32[1152,768]{1,0:T(8,128)} %get-tuple-element.54) | copy-start | bytes 10616836
  148.3 4.0 %collective-permute-start.1 = (f32[2,64,768]{2,1,0:T(8,128)S(1)}, f32[2,64,768]{2,1,0:T(8,128)S(1)}, u32[]{:S(2)}, u32[]{:S(2)}) collective-permute-start(f32[2,64,768]{2,1,0:T(8,128)S(1)} %pad_maximum_fusion.2), channel_id=1, source_target_pairs={{0,4},{4,8},{8,12},{1,5},{5,9},{9,13},{2,6},{6,10},{10,14},{3,7},{... | collective-permute-start | bytes 1179656 | tf_op jit(solution)/shard_map/ppermute | solution.py:654
  153.3 7.7 %collective-permute-start.2 = (f32[2,64,768]{2,1,0:T(8,128)}, f32[2,64,768]{2,1,0:T(8,128)}, u32[]{:S(2)}, u32[]{:S(2)}) collective-permute-start(f32[2,64,768]{2,1,0:T(8,128)} %get-tuple-element.69), channel_id=1, source_target_pairs={{4,0},{8,4},{12,8},{5,1},{9,5},{13,9},{6,2},{10,6},{14,10},{7,3},{... | collective-permute-start | bytes 1179656 | tf_op jit(solution)/shard_map/ppermute | solution.py:653
  154.6 105.0 %collective-permute-start = (bf16[1024,768]{1,0:T(8,128)(2,1)}, bf16[1024,768]{1,0:T(8,128)(2,1)}, u32[]{:S(2)}, u32[]{:S(2)}) collective-permute-start(bf16[1024,768]{1,0:T(8,128)(2,1)} %get-tuple-element.43), channel_id=1, source_target_pairs={{0,1},{1,0},{2,3},{3,2},{4,5},{5,4},{6,7},{7,6},{8,9},{9,8},{10,11... | collective-permute-start | bytes 4718600 | tf_op jit(solution)/shard_map/ppermute | solution.py:671
  154.7 2.7 copy-start.7
  157.4 3.6 %copy-start.4 = (f32[1152,768]{1,0:T(8,128)S(1)}, f32[1152,768]{1,0:T(8,128)}, u32[]{:S(2)}) copy-start(f32[1152,768]{1,0:T(8,128)} %get-tuple-element.54) | copy-start | bytes 10616836
  160.0 2.0 copy-start.5
  181.7 68.2 %copy-start.6 = (bf16[1024,768]{1,0:T(8,128)(2,1)S(1)}, bf16[1024,768]{1,0:T(8,128)(2,1)}, u32[]{:S(2)}) copy-start(bf16[1024,768]{1,0:T(8,128)(2,1)} %get-tuple-element.56) | copy-start | bytes 4718596
  249.9 36.7 %collective-permute-start.3 = (bf16[1024,768]{1,0:T(8,128)(2,1)S(1)}, bf16[1024,768]{1,0:T(8,128)(2,1)S(1)}, u32[]{:S(2)}, u32[]{:S(2)}) collective-permute-start(bf16[1024,768]{1,0:T(8,128)(2,1)S(1)} %copy-done.6), channel_id=1, source_target_pairs={{0,1},{1,0},{2,3},{3,2},{4,5},{5,4},{6,7},{7,6},{8,9},{9,8},{10,11... | collective-permute-start | bytes 4718600 | tf_op jit(solution)/shard_map/ppermute | solution.py:671
  286.8 2.0 copy-start.1

commit v3 on v2

--- a/solution.py
+++ b/solution.py
@@ -142,7 +142,7 @@
     lax.fori_loop(lo, hi, body, 0)
 
 
-def phase_mlp(x_ref, cot_ref, ctx_ref, gain_ref, wo_ref, wi_ref, wm_ref, out_ref, gm_ref, gml_ref, go_ref, nm_ref, hid_ref, dgu_ref, dctx_ref, gg_ref, pos0, length, rows):
+def phase_mlp(x_ref, cot_ref, ctx_ref, gain_ref, wo_ref, wi_ref, wm_ref, out_ref, gml_ref, go_ref, nm_ref, hid_ref, dgu_ref, dctx_ref, gg_ref, pos0, length, rows):
     ff = wm_ref.shape[0]
     half = hid_ref.shape[1]
     gg_ref[...] = jnp.zeros_like(gg_ref)
@@ -175,7 +175,6 @@
         grad_nm = nn(grad_gate, wi_ref[:ff, :]) + nn(grad_up, wi_ref[ff:, :])
         gg_ref[...] += jnp.sum((grad_nm * xhat).reshape(rows // 8, 8, -1), axis=0)
         grad_middle = grad_out + layer_back(grad_nm * gain, xhat, inv)
-        gm_ref[here, :] = grad_middle
         gm_low = grad_middle.astype(BF16)
         gml_ref[here, :] = gm_low
         dctx_ref[here, :] = nt(gm_low, wo_ref[...]).astype(BF16)
@@ -184,12 +183,11 @@
     lax.fori_loop(0, ctx_ref.shape[0] // rows, body, 0)
 
 
-def phase_attend_back(q_ref, k_ref, v_ref, p_ref, ctx_ref, dctx_ref, tables, dq_ref, dk_ref, dv_ref, block0):
+def phase_attend_back(q_ref, k_ref, v_ref, p_ref, ctx_ref, dctx_ref, tables, dqkv_ref, dk_ref, dv_ref, block0, lo, hi):
     width = q_ref.shape[1]
+    half = width // 2
     span = TILE + 2 * HALF
     scaling = 1.0 / math.sqrt(HD)
-    dk_ref[...] = jnp.zeros_like(dk_ref)
-    dv_ref[...] = jnp.zeros_like(dv_ref)
 
     def body(t, carry):
         r0 = pl.multiple_of(t * TILE, TILE)
@@ -211,48 +209,46 @@
             grad_scores = (probs.astype(F32) * (grad_probs - row_term)).astype(BF16)
             dq2 = nn(grad_scores, kc)
             dq = jnp.where(low_head, dq2[:TILE], dq2[TILE:])
-            dq_ref[pl.ds(r0, TILE), lanes] = turn(dq, cosine, sine, first).astype(BF16)
+            at = 3 * half * (j * LANES // half) + j * LANES % half
+            dqkv_ref[pl.ds(r0, TILE), at : at + LANES] = turn(dq, cosine, sine, first).astype(BF16)
             q2 = split_heads(q_ref[pl.ds(r0 + HALF, TILE), lanes], low_head)
             dk_ref[keys, lanes] += tn(grad_scores, q2)
             dv_ref[keys, lanes] += tn(probs, dc2)
         return carry
 
-    lax.fori_loop(0, dq_ref.shape[0] // TILE, body, 0)
-
-
-def phase_input(x_ref, gm_ref, dq_ref, dk_ref, dv_ref, gain_ref, w_ref, tables, dqkv_ref, out_ref, gg_ref, block0, rows):
-    width = x_ref.shape[1]
+    lax.fori_loop(lo, hi, body, 0)
+
+
+def phase_pack(dk_ref, dv_ref, tables, dqkv_ref, block0, lo, hi):
+    width = dk_ref.shape[1]
     half = width // 2
-    gg_ref[...] = jnp.zeros_like(gg_ref)
 
     def body(t, carry):
-        r0 = pl.multiple_of(t * rows, rows)
-        here = pl.ds(r0, rows)
-        gain = gain_ref[...].astype(F32)
-        pieces = []
-        for s in range(rows // TILE):
-            cosine, sine, first = rope_tile(tables, block0 + 1 + t * (rows // HALF) + s * (TILE // HALF))
-            sub = pl.ds(r0 + s * TILE, TILE)
-            chunk = [turn(dk_ref[sub, j * LANES : (j + 1) * LANES], cosine, -sine, first).astype(BF16) for j in range(width // LANES)]
-            pieces.append(jnp.concatenate(chunk, axis=1))
-        dk = jnp.concatenate(pieces, axis=0)
-        dq = dq_ref[here, :]
-        dv = dv_ref[here, :].astype(BF16)
-        own = jnp.concatenate([g[:, :half] for g in (dq, dk, dv)], axis=1)
-        other = jnp.concatenate([g[:, half:] for g in (dq, dk, dv)], axis=1)
-        dqkv_ref[here, :] = own
-        grad_normed = nn(jnp.concatenate([own, other], axis=1), w_ref[...])
-        xhat, inv = layer_stats(x_ref[here, :].astype(F32))
-        gg_ref[...] += jnp.sum((grad_normed * xhat).reshape(rows // 8, 8, -1), axis=0)
-        out_ref[here, :] = (gm_ref[here, :] + layer_back(grad_normed * gain, xhat, inv)).astype(BF16)
+        r0 = pl.multiple_of(t * TILE, TILE)
+        cosine, sine, first = rope_tile(tables, block0 + 1 + t * (TILE // HALF))
+        ext = pl.ds(r0 + HALF, TILE)
+        for j in range(width // LANES):
+            lanes = slice(j * LANES, (j + 1) * LANES)
+            at = 3 * half * (j * LANES // half) + j * LANES % half
+            dqkv_ref[pl.ds(r0, TILE), at + half : at + half + LANES] = turn(dk_ref[ext, lanes], cosine, -sine, first).astype(BF16)
+            dqkv_ref[pl.ds(r0, TILE), at + 2 * half : at + 2 * half + LANES] = dv_ref[ext, lanes].astype(BF16)
         return carry
 
-    lax.fori_loop(0, x_ref.shape[0] // rows, body, 0)
-
-
-def weight_grad(a_ref, b_ref, out_ref, columns):
-    for c in range(0, a_ref.shape[1], columns):
-        out_ref[c : c + columns, :] = tn(a_ref[:, c : c + columns], b_ref[...]).astype(out_ref.dtype)
+    lax.fori_loop(lo, hi, body, 0)
+
+
+def phase_input(x_ref, gm_ref, gain_ref, w_ref, dqkv_ref, out_ref, gg_ref, r0, rows):
+    here = pl.ds(r0, rows)
+    gain = gain_ref[:1, :].astype(F32)
+    grad_normed = nn(dqkv_ref[here, :], w_ref[...])
+    xhat, inv = layer_stats(x_ref[here, :].astype(F32))
+    gg_ref[...] += jnp.sum((grad_normed * xhat).reshape(rows // 8, 8, -1), axis=0)
+    out_ref[here, :] = (gm_ref[here, :].astype(F32) + layer_back(grad_normed * gain, xhat, inv)).astype(BF16)
+
+
+def weight_grad(a_ref, b, out_ref, columns, at=0, count=None):
+    for c in range(0, a_ref.shape[1] if count is None else count, columns):
+        out_ref[c : c + columns, :] = tn(a_ref[:, at + c : at + c + columns], b).astype(out_ref.dtype)
 
 
 def slot_of(at, of):
@@ -539,16 +535,86 @@
         getattr(job, stage)()
 
 
-def reduce_kernel(n_shard, n, *refs):
-    grads, outs, (send, recv), bufs = refs[:n], refs[n : 2 * n], refs[2 * n : 2 * n + 2], refs[2 * n + 2 :]
+def back_kernel(n_shard, s_ref, q, k, v, p, ctx, dctx, gml, normed, gains_ref, wqkv, dwi, dwm, dwo, gain2, *refs):
+    tables, (x_ref, layer_ref), outs, refs = refs[:4], refs[4:6], refs[6:13], refs[13:]
+    layer_all, input_all, out_qkv, out_wi, out_wm, out_wo, out_gain = outs
+    x, dk, dv, dqkv, given, rim_out, rim_in, dw, gg, gbuf, send, recv = refs[:12]
+    bufs = refs[12:]
     h = Place(n_shard)
-    near = [h.to_mate, h.to_core, h.to_y]
+    near = [h.to_mate] + [{"ctx": (h.c + i) % 4} for i in (1, 2, 3)]
     if h.split:
         near.append(h.to_x)
     h.meet(near)
     wires = Wires(send, recv)
-    jobs = [Reduce(g, o, bufs[7 * i : 7 * i + 7], wires, h, i % 2 == 0) for i, (g, o) in enumerate(zip(grads, outs))]
-    wavefront(jobs, REDUCE_STAGES)
+    m = h.z % 2
+    local, width = x.shape
+    kept = [wires.own(x_ref.at[0, m], x), wires.own(layer_ref, layer_all.at[m])]
+    swaps = [wires.go(layer_ref, layer_all.at[m], h.to_mate)]
+    jobs = [Reduce(g, o, bufs[7 * i : 7 * i + 7], wires, h, True) for i, (g, o) in enumerate(((dwi, out_wi), (dwm, out_wm), (dwo, out_wo)))]
+    late = [Reduce(dw.at[pl.ds(i, 1)], out_qkv.at[pl.ds(i, 1)], bufs[7 * (3 + i) : 7 * (4 + i)], wires, h, True) for i in range(3)]
+    late.append(Reduce(gbuf, out_gain, bufs[42:49], wires, h, True))
+    run(jobs, "begin")
+    dk[...] = jnp.zeros_like(dk)
+    dv[...] = jnp.zeros_like(dv)
+    gg[...] = jnp.zeros_like(gg)
+    tiles = local // TILE
+    back = functools.partial(phase_attend_back, q, k, v, p, ctx, dctx, tables, dqkv, dk, dv, s_ref[2])
+    pack = functools.partial(phase_pack, dk, dv, tables, dqkv, s_ref[2])
+    rows = 2 * TILE
+
+    def finish(i):
+        r0 = i * rows
+        phase_input(x, gml, gains_ref, wqkv, dqkv, given, gg, r0, rows)
+        piece = given.at[pl.ds(r0, rows), :]
+        target = input_all.at[m, pl.ds(r0, rows), :]
+        kept.append(wires.own(piece, target))
+        swaps.append(wires.go(piece, target, h.to_mate))
+
+    back(tiles - 1, tiles)
+    back(0, 1)
+    ext = local + 2 * HALF
+    for i, ref in enumerate((dk, dv)):
+        rim_out[0, i] = ref[:HALF, :].astype(BF16)
+        rim_out[1, i] = ref[ext - HALF :, :].astype(BF16)
+    rims = [wires.go(rim_out.at[0], rim_in.at[0], h.to_prev), wires.go(rim_out.at[1], rim_in.at[1], h.to_next)]
+    run(jobs, "first")
+    back(1, 3)
+    landed(rims)
+    for i, ref in enumerate((dk, dv)):
+        ref[HALF : 2 * HALF, :] += rim_in[1, i].astype(F32)
+        ref[ext - 2 * HALF : ext - HALF, :] += rim_in[0, i].astype(F32)
+    kept[0].wait()
+    run(jobs, "second")
+    pack(0, 2)
+    finish(0)
+    run(jobs, "third")
+    back(3, 5)
+    run(jobs, "fourth")
+    pack(2, 4)
+    finish(1)
+    run(jobs, "end")
+    back(5, 7)
+    pack(4, 8)
+    half = width // 2
+    own = normed[HALF : HALF + local, :]
+    for i in range(3):
+        weight_grad(dqkv, own, dw.at[i].reshape(half, width), LANES, at=i * half, count=half)
+        late[i].begin()
+    finish(2)
+    run(late[:3], "first")
+    finish(3)
+    gain_rows = jnp.concatenate([gg[...], gain2[...]], axis=0).astype(BF16)
+    gain_rows = jnp.concatenate([gain_rows, gain_rows], axis=0)
+    gbuf[0, 0] = gain_rows
+    gbuf[0, 1] = gain_rows
+    late[3].begin()
+    for stage in REDUCE_STAGES[1:]:
+        if stage != "first":
+            run(late[:3], stage)
+        run(late[3:], stage)
+    landed(swaps)
+    for copy in kept[1:]:
+        copy.wait()
     wires.close()
 
 
@@ -619,86 +685,61 @@
     gain1, gain2 = gains[:1], gains[1:2]
     x_own = lax.dynamic_index_in_dim(inputs[0], mine, 0, keepdims=False)
     cot = lax.dynamic_index_in_dim(cotangent[0], mine, 0, keepdims=False)
-    up = [(i, i + 1) for i in range(n_ctx - 1)]
-    down = [(i + 1, i) for i in range(n_ctx - 1)]
     ff = wm.shape[0]
     ff_half = ff // 2
 
-    def kernel_d(s_ref, x_ref, cot_ref, ctx_ref, g_ref, wo_ref, wi_ref, wm_ref, out, gm, gml, dctx, gg, dwm, dwi, go, nm, hid, dgu):
-        phase_mlp(x_ref, cot_ref, ctx_ref, g_ref, wo_ref, wi_ref, wm_ref, out, gm, gml, go, nm, hid, dgu, dctx, gg, s_ref[1], s_ref[0], 256)
-        weight_grad(hid, go, dwm, 192)
-        weight_grad(dgu, nm, dwi, 384)
-
-    layer_out, gm, gml, dctx, gain2_part, dwm, dwi = call(
+    def kernel_d(s_ref, x_ref, cot_ref, ctx_ref, g_ref, wo_ref, wi_ref, wm_ref, out, gml, dctx, gg, dwm, dwi, dwo, go, nm, hid, dgu):
+        phase_mlp(x_ref, cot_ref, ctx_ref, g_ref, wo_ref, wi_ref, wm_ref, out, gml, go, nm, hid, dgu, dctx, gg, s_ref[1], s_ref[0], 256)
+        weight_grad(hid, go[...], dwm, 192)
+        weight_grad(dgu, nm[...], dwi, 384)
+        weight_grad(ctx_ref, gml[...], dwo, LANES, count=width // 2)
+
+    layer_own, gml, dctx, gain2_part, dwm, dwi, dwo = call(
         kernel_d,
-        [tall, ((local, width), F32), tall, tall, ((8, width), F32), ((ff_half, width), BF16), ((2 * ff_half, width), BF16)],
+        [tall, tall, tall, ((8, width), F32), ((ff_half, width), BF16), ((2 * ff_half, width), BF16), ((width // 2, width), BF16)],
         scalars, x_own, cot, context, gain2, wo, wi, wm,
         scratch=[pltpu.VMEM((local, width), BF16), pltpu.VMEM((local, width), BF16), pltpu.VMEM((local, ff_half), BF16), pltpu.VMEM((local, 2 * ff_half), BF16)],
         name="feed_forward",
     )
     width_half = width // 2
-
-    def kernel_e(s_ref, q_ref, k_ref, v_ref, p_ref, ctx_ref, dctx_ref, gml_ref, c0, s0, c1, s1, dq, dk, dv, dwo):
-        phase_attend_back(q_ref, k_ref, v_ref, p_ref, ctx_ref, dctx_ref, (c0, s0, c1, s1), dq, dk, dv, s_ref[2])
-        for c in range(0, width_half, LANES):
-            dwo[c : c + LANES, :] = tn(ctx_ref[:, c : c + LANES], gml_ref[...]).astype(BF16)
-
-    dq, dk, dv, dwo = call(
-        kernel_e,
-        [tall, ((ext, width), F32), ((ext, width), F32), ((width_half, width), BF16)],
-        scalars, q, k, v, probs, context, dctx, gml, *tables,
-        name="attend_back",
-    )
-    rims = jnp.stack([dk, dv])
-    to_lower = lax.ppermute(rims[:, :HALF], "ctx", down)
-    to_upper = lax.ppermute(rims[:, ext - HALF :], "ctx", up)
-    rims = rims[:, HALF : HALF + local]
-    rims = jnp.concatenate([rims[:, :HALF] + to_upper, rims[:, HALF : local - HALF], rims[:, local - HALF :] + to_lower], axis=1)
-
-    def kernel_g(s_ref, x_ref, n_ref, gm_ref, dq_ref, dk_ref, dv_ref, g_ref, w_ref, c0, s0, c1, s1, out, gg, dw, dqkv):
-        phase_input(x_ref, gm_ref, dq_ref, dk_ref, dv_ref, g_ref, w_ref, (c0, s0, c1, s1), dqkv, out, gg, s_ref[2], 256)
-        weight_grad(dqkv, n_ref, dw, 384)
-
-    input_grad, gain1_part, dwqkv = call(
-        kernel_g,
-        [tall, ((8, width), F32), ((3 * width_half, width), BF16)],
-        scalars, x_own, normed[HALF : HALF + local], gm, dq, rims[0], rims[1], gain1, wqkv, *tables,
-        scratch=[pltpu.VMEM((local, 3 * width_half), BF16)],
-        name="input_back",
-    )
-
-    def both(own):
-        other = lax.ppermute(own, "tp", [(i, i ^ 1) for i in range(n_tp)])
-        low = jnp.where(mine == 0, own, other)
-        high = jnp.where(mine == 0, other, own)
-        return jnp.stack([low, high])[None]
-
-    gain_rows = jnp.concatenate([gain1_part, gain2_part]).astype(BF16)
-    gain_rows = jnp.broadcast_to(gain_rows[None, None], (1, 2, 16, width))
-    grads = [g.reshape(k, 2, -1, width) for g, k in ((dwqkv, 3), (dwi, 2), (dwo, 1), (dwm, 1))]
-    grads.append(jnp.concatenate([gain_rows, gain_rows], axis=2))
     cols = width // n_shard if n_shard == 2 else width
-    sends = REDUCE_COPIES * len(grads)
-    owned = pl.pallas_call(
-        functools.partial(reduce_kernel, n_shard, len(grads)),
-        out_shape=[jax.ShapeDtypeStruct((g.shape[0], g.shape[2], cols), BF16) for g in grads],
-        in_specs=[vmem] * len(grads),
-        out_specs=[vmem] * len(grads),
-        scratch_shapes=[pltpu.SemaphoreType.DMA((sends,)), pltpu.SemaphoreType.DMA((sends,))]
-        + [b for i, g in enumerate(grads) for b in Reduce.scratch(g.shape, n_shard, i % 2 == 0)],
+    grads = [(3, 2, width_half // 2, width), (2, 2, ff_half // 2, width), (1, 2, ff_half // 2, width), (1, 2, width_half // 2, width), (1, 2, 32, width)]
+    dwi, dwm, dwo = (g.reshape(shape) for g, shape in zip((dwi, dwm, dwo), grads[1:]))
+    jobs = grads[1:4] + [(1, *grads[0][1:])] * 3 + grads[4:]
+    sends = 64
+    layer_out, input_grad, *owned = pl.pallas_call(
+        functools.partial(back_kernel, n_shard),
+        out_shape=[jax.ShapeDtypeStruct((seqs, local, width), BF16)] * 2 + [jax.ShapeDtypeStruct((g[0], g[2], cols), BF16) for g in grads],
+        in_specs=[smem] + [vmem] * 18 + [hbm] * 2,
+        out_specs=[hbm] * 2 + [vmem] * len(grads),
+        scratch_shapes=[
+            pltpu.VMEM((local, width), BF16),
+            pltpu.VMEM((ext, width), F32),
+            pltpu.VMEM((ext, width), F32),
+            pltpu.VMEM((local, 3 * width), BF16),
+            pltpu.VMEM((local, width), BF16),
+            pltpu.VMEM((2, 2, HALF, width), BF16),
+            pltpu.VMEM((2, 2, HALF, width), BF16),
+            pltpu.VMEM(grads[0], BF16),
+            pltpu.VMEM((8, width), F32),
+            pltpu.VMEM(grads[4], BF16),
+            pltpu.SemaphoreType.DMA((sends,)),
+            pltpu.SemaphoreType.DMA((sends,)),
+        ]
+        + [b for g in jobs for b in Reduce.scratch(g, n_shard, True)],
         compiler_params=pltpu.CompilerParams(collective_id=1, has_side_effects=True, vmem_limit_bytes=VMEM_LIMIT),
-        name="reduce",
-    )(*grads)
+        name="back",
+    )(scalars, q, k, v, probs, context, dctx, gml, normed, gains, wqkv, dwi, dwm, dwo, gain2_part, *tables, inputs, layer_own)
     owned = [g.astype(F32) for g in owned]
     if n_shard != 2:
         owned = [lax.psum_scatter(g, "shard", scatter_dimension=2, tiled=True) for g in owned]
     qkv_grad = jnp.transpose(owned[0], (2, 0, 1))
     mlp_in_grad = jnp.transpose(owned[1], (2, 0, 1))
-    attn_grad, mlp_out_grad = owned[2][0], owned[3][0]
+    mlp_out_grad, attn_grad = owned[2][0], owned[3][0]
     share = owned[4].shape[2] // n_tp
     gains = lax.dynamic_slice_in_dim(owned[4][0, :16], tp * share, share, axis=1)
     gains = jnp.sum(gains.reshape(2, 8, share), axis=1)
-    return (both(layer_out), both(input_grad), qkv_grad, attn_grad, mlp_in_grad, mlp_out_grad, gains[0], gains[1])
+    return (layer_out[None], input_grad[None], qkv_grad, attn_grad, mlp_in_grad, mlp_out_grad, gains[0], gains[1])
 
 
 def solution(mesh):

time: 289 us -> 236 us (0.82)
  waiting for transfers between devices: 25.3 us -> 0 us
  other arithmetic: 23.3 us -> 8.49 us
  Pallas kernels: 220 us -> 213 us
  starting transfers between devices: 5.76 us -> 0 us
    pallas_call x3 -> x1, Pallas kernels: 73.5 us -> 30.5 us  [call(): pl.pallas_call(kernel, out_shape=[jax.ShapeDtypeStruct(s, d) for s, d in...]
    pallas_call x1, Pallas kernels: 66 us -> 102 us  [on_device(): pl.pallas_call(functools.partial(back_kernel, n_shard), out_shape=[jax.Sh...]
    ppermute x4 -> x0, waiting for transfers between devices: 25.3 us -> none  [the longest x2 23.1 us: both(): other = lax.ppermute(own, 'tp', [(i, i ^ 1) for i in range(n_tp)])]
    another operation x5 -> x0, other arithmetic: 5.8 us -> none  [the longest x1 2.64 us: on_device(): rims = jnp.stack([dk, dv])]
    ppermute x4 -> x0, starting transfers between devices: 5.76 us -> none  [the longest x1 2.73 us: on_device(): to_upper = lax.ppermute(rims[:, ext - HALF:], 'ctx', up)]
    unnamed x16 -> x10, local copies, waits for them, and re-layouts: 0.04 us -> 5.33 us
    broadcast_in_dim x2 -> x0, other arithmetic: 3.87 us -> none  [both(): return jnp.stack([low, high])[None]]
    squeeze x1 -> x0, local copies, waits for them, and re-layouts: 3.09 us -> none  [on_device(): rims[1]]
  transfers between devices with their start and end apart: 4 -> 0, of which waited for: 3 -> 0; matrix products, arithmetic and copies ran while one was open for 8% -> 0% of each run, Pallas kernels for 28% -> 0%
where the time goes in v3:
time: 236 us; the launch traced here: 235 us
  Pallas kernels  213 us (90%)
  local copies, waits for them, and re-layouts  13.7 us (6%)
  other arithmetic  8.49 us (4%)
    pallas_call x1, Pallas kernels, on_device(): pl.pallas_call(functools.partial(back_kernel, n_shard), out_shape=[jax.Sh...  102 us
    pallas_call x1, Pallas kernels, on_device(): pl.pallas_call(functools.partial(attend_kernel, n_shard), out_shape=[jax....  80 us
    pallas_call x1, Pallas kernels, call(): pl.pallas_call(kernel, out_shape=[jax.ShapeDtypeStruct(s, d) for s, d in...  30.5 us
    unnamed x10, local copies, waits for them, and re-layouts  5.33 us

profile of v3, /device:TPU:0, one launch (start us, length us, event | category | flops | bytes accessed | tf_op | source)
XLA Modules:
  0.0 235.4 jit_solution(13310355578271489983)
XLA Ops:
  0.6 0.0 copy-start
  0.7 0.6 copy-done
  1.3 0.6 constant_dynamic-slice_fusion
  1.9 1.3 pad_add_fusion.s_ref
  3.2 0.7 stack.21
  3.9 0.7 stack.22
  4.6 0.6 fusion.2.gains_ref
  5.2 3.8 %dynamic-slice_bitcast_fusion = (bf16[1024,768]{1,0:T(8,128)(2,1)}, bf16[1024,768]{1,0:T(8,128)(2,1)}) fusion(bf16[1,2,1024,768]{3,2,1,0:T(8,128)(2,1)} %param.21, s32[]{:T(128)S(6)} %select_n.18, bf16[1,2,1024,768]{3,2,1,0:T(8,128)(2,1)} %refs_4_.2), kind=kLoop, calls=%fused_computation | loop fusion | bytes 6291460 | tf_op jit(solution)/shard_map/jit(dynamic_index_in_dim)/squeeze | solution.py:687
  9.0 80.0 %attend.1 = (bf16[2,3,2,192,768]{4,3,2,1,0:T(8,128)(2,1)}, bf16[1,4,192,768]{3,2,1,0:T(8,128)(2,1)}, bf16[2,4,288,768]{3,2,1,0:T(8,128)(2,1)}, bf16[1,4,288,768]...) custom-call(s32[3]{0:T(128)} %pad_add_fusion.s_ref, ...), custom_call_target="tpu_custom_call" | custom-call | tf_op jit(solution)/shard_map/attend/pallas_call | solution.py:675
  89.1 1.3 slice.15.g_ref
  90.3 30.5 %feed_forward.1 = (bf16[1024,768]{1,0:T(8,128)(2,1)}, bf16[1024,768]{1,0:T(8,128)(2,1)}, bf16[1024,768]{1,0:T(8,128)(2,1)}, f32[8,768]{1,0:T(8,128)}, bf16[576,7...) custom-call(s32[3]{0:T(128)} %pad_add_fusion.s_ref, ...), custom_call_target="tpu_custom_call" | custom-call | tf_op jit(solution)/shard_map/feed_forward/pallas_call | solution.py:624
  120.8 102.0 %back.1 = (bf16[2,1024,768]{2,1,0:T(8,128)(2,1)}, bf16[2,1024,768]{2,1,0:T(8,128)(2,1)}, bf16[3,192,384]{2,1,0:T(8,128)(2,1)}, bf16[2,288,384]{2,1,0:T(8,128)(2,...) custom-call(s32[3]{0:T(128)} %pad_add_fusion.s_ref, ...), custom_call_target="tpu_custom_call" | custom-call | tf_op jit(solution)/shard_map/back/pallas_call | solution.py:710
  222.9 0.0 copy-start.3
  222.9 0.8 slice.16
  223.6 0.1 bitcast_reduce_fusion
  223.7 0.5 slice_bitcast_fusion
  224.2 1.6 bitcast_convert_fusion.1
  225.9 0.0 copy-start.2
  225.9 1.9 bitcast_convert_fusion
  227.8 2.0 convert_bitcast_fusion.1
  229.7 0.0 copy-done.3
  229.7 1.0 convert_bitcast_fusion
  230.7 0.0 copy-done.2
  230.7 0.0 copy-start.1
  230.7 1.7 copy.23
  232.4 1.4 copy-done.1
  233.7 1.7 copy.24
Async XLA Ops:
  0.6 0.7 copy-start
  222.9 6.9 %copy-start.3 = (bf16[2,288,384]{2,1,0:T(8,128)(2,1)S(1)}, bf16[2,288,384]{2,1,0:T(8,128)(2,1)}, u32[]{:S(2)}) copy-start(bf16[2,288,384]{2,1,0:T(8,128)(2,1)} %get-tuple-element.55) | copy-start | bytes 1327108
  225.9 4.8 %copy-start.2 = (bf16[2,1024,768]{2,1,0:T(8,128)(2,1)S(1)}, bf16[2,1024,768]{2,1,0:T(8,128)(2,1)}, u32[]{:S(2)}) copy-start(bf16[2,1024,768]{2,1,0:T(8,128)(2,1)} %get-tuple-element.51) | copy-start | bytes 9437188
  230.7 3.0 %copy-start.1 = (bf16[2,1024,768]{2,1,0:T(8,128)(2,1)S(1)}, bf16[2,1024,768]{2,1,0:T(8,128)(2,1)}, u32[]{:S(2)}) copy-start(bf16[2,1024,768]{2,1,0:T(8,128)(2,1)} %get-tuple-element.52) | copy-start | bytes 9437188

commit v4 on v3

v4 whole, which is shorter than its diff:
```python
import functools
import math

import numpy as np

import jax
import jax.numpy as jnp
from jax import lax
from jax.experimental import pallas as pl
from jax.experimental.pallas import tpu as pltpu
from jax.sharding import PartitionSpec as P

HD = 64
HALF = 64
TILE = 128
LANES = 128
norm_eps = 1e-05
rope_base = 10000.0
masked_score = -1e30
F32 = jnp.float32
BF16 = jnp.bfloat16
VMEM_LIMIT = 60 * 1024 * 1024


def nt(a, b):
    return lax.dot_general(a, b, (((1,), (1,)), ((), ())), preferred_element_type=F32)


def nn(a, b):
    return lax.dot_general(a, b, (((1,), (0,)), ((), ())), preferred_element_type=F32)


def tn(a, b):
    return lax.dot_general(a, b, (((0,), (0,)), ((), ())), preferred_element_type=F32)


def rope_constants(seq):
    w = rope_base ** (-np.arange(0, HD, 2) / HD)
    w = np.tile(w, 2 * LANES // HD)
    rows = np.arange(TILE)[:, None] * w
    blocks = (np.arange(seq // HALF + 4)[:, None] - 1) * HALF * w
    tables = (np.cos(rows), np.sin(rows), np.cos(blocks), np.sin(blocks))
    return tuple(t.astype(np.float32) for t in tables)


def rope_tile(tables, block):
    cos_r, sin_r, cos_b, sin_b = tables
    cb = cos_b[pl.ds(block + 1, 1), :]
    sb = sin_b[pl.ds(block + 1, 1), :]
    cr = cos_r[...]
    sr = sin_r[...]
    cosine = cr * cb - sr * sb
    sine = sr * cb + cr * sb
    first = lax.broadcasted_iota(jnp.int32, sine.shape, 1) % HD < HD // 2
    return cosine, jnp.where(first, -sine, sine), first


def turn(u, cosine, sine, first):
    other = jnp.where(first, pltpu.roll(u, LANES - HD // 2, 1), pltpu.roll(u, HD // 2, 1))
    return u * cosine + other * sine


def layer_stats(z):
    center = z - jnp.mean(z, axis=-1, keepdims=True)
    inv = lax.rsqrt(jnp.mean(center * center, axis=-1, keepdims=True) + norm_eps)
    return center * inv, inv


def layer_back(e, xhat, inv):
    return (e - jnp.mean(e, axis=-1, keepdims=True) - xhat * jnp.mean(e * xhat, axis=-1, keepdims=True)) * inv


def head_masks(shape):
    lane = lax.broadcasted_iota(jnp.int32, shape, 1)
    return lane < HD


def split_heads(c, low_head):
    zero = jnp.zeros_like(c)
    return jnp.concatenate([jnp.where(low_head, c, zero), jnp.where(low_head, zero, c)], axis=0)


def phase_norm(x_ref, gain_ref, normed_ref):
    def body(t, carry):
        r0 = pl.multiple_of(t * TILE, TILE)
        xhat, _ = layer_stats(x_ref[pl.ds(r0, TILE), :].astype(F32))
        normed_ref[pl.ds(r0, TILE), :] = (xhat * gain_ref[:1, :].astype(F32)).astype(BF16)
        return carry

    lax.fori_loop(0, x_ref.shape[0] // TILE, body, 0)


def phase_qkv(normed_ref, w_ref, tables, q_ref, k_ref, v_ref, block0, rows, which, after):
    width = normed_ref.shape[1]
    half = width // 2
    scaling = 1.0 / math.sqrt(HD)

    def body(t, carry):
        r0 = pl.multiple_of(t * rows, rows)
        out = nt(normed_ref[pl.ds(r0, rows), :], w_ref[which].reshape(3 * half, width))
        for s in range(rows // TILE):
            here = pl.ds(r0 + s * TILE, TILE)
            cosine, sine, first = rope_tile(tables, block0 + t * (rows // HALF) + s * (TILE // HALF))
            for part, ref in enumerate((q_ref, k_ref)):
                if part == 0:
                    turns = cosine * scaling, sine * scaling, first
                else:
                    turns = cosine, sine, first
                for j in range(half // LANES):
                    u = out[s * TILE : (s + 1) * TILE, part * half + j * LANES : part * half + (j + 1) * LANES]
                    ref[here, which * half + j * LANES : which * half + (j + 1) * LANES] = turn(u, *turns).astype(BF16)
        v_ref[pl.ds(r0, rows), which * half : (which + 1) * half] = out[:, 2 * half :].astype(BF16)
        after(t)
        return carry

    lax.fori_loop(0, normed_ref.shape[0] // rows, body, 0)


def phase_attend(q_ref, k_ref, v_ref, p_ref, ctx_ref, pos0, length, chunks, lo, hi, after):
    span = TILE + 2 * HALF

    def body(t, carry):
        r0 = pl.multiple_of(t * TILE, TILE)
        row = lax.broadcasted_iota(jnp.int32, (TILE, span), 0)
        col = lax.broadcasted_iota(jnp.int32, (TILE, span), 1)
        offset = col - row
        key_pos = pos0 + t * TILE - HALF + col
        allowed = (offset >= 0) & (offset <= 2 * HALF) & (key_pos >= 0) & ((key_pos < length) | (offset == HALF))
        bias = jnp.where(allowed, 0.0, masked_score).astype(F32)
        bias = jnp.concatenate([bias, bias], axis=0)
        low_head = head_masks((TILE, LANES))
        for j in chunks:
            lanes = slice(j * LANES, (j + 1) * LANES)
            q2 = split_heads(q_ref[pl.ds(r0 + HALF, TILE), lanes], low_head)
            scores = nt(q2, k_ref[pl.ds(r0, span), lanes]) + bias
            terms = jnp.exp(scores - jnp.max(scores, axis=-1, keepdims=True))
            probs = (terms * (1.0 / jnp.sum(terms, axis=-1, keepdims=True))).astype(BF16)
            p_ref[t, j] = probs
            out = nn(probs, v_ref[pl.ds(r0, span), lanes])
            ctx_ref[pl.ds(r0, TILE), lanes] = jnp.where(low_head, out[:TILE], out[TILE:]).astype(BF16)
        after(t)
        return carry

    lax.fori_loop(lo, hi, body, 0)


def phase_mlp(x_ref, cot_ref, ctx_ref, gain_ref, wo_ref, wi_ref, wm_ref, out_ref, gml_ref, nm_ref, hid_ref, dgu_ref, dctx_ref, gg_ref, pos0, length, rows, ready):
    ff = wm_ref.shape[0]
    half = hid_ref.shape[1]
    gg_ref[...] = jnp.zeros_like(gg_ref)

    def body(t, carry):
        r0 = pl.multiple_of(t * rows, rows)
        here = pl.ds(r0, rows)
        gain = gain_ref[1:2, :].astype(F32)
        middle = x_ref[pl.ds(r0 + HALF, rows), :].astype(F32) + nn(ctx_ref[here, :], wo_ref[...])
        xhat, inv = layer_stats(middle)
        nm = (xhat * gain).astype(BF16)
        nm_ref[here, :] = nm
        gate = nt(nm, wi_ref[:ff, :])
        up = nt(nm, wi_ref[ff:, :])
        cdf = 0.5 + 0.5 * lax.erf(gate * math.sqrt(0.5))
        gelu = gate * cdf
        slope = cdf + gate * (jnp.exp(-0.5 * gate * gate) * (1.0 / math.sqrt(2.0 * math.pi)))
        hidden = (gelu * up).astype(BF16)
        hid_ref[here, :] = hidden[:, :half]
        valid = pos0 + r0 + lax.broadcasted_iota(jnp.int32, (rows, 1), 0) < length
        out_ref[here, :] = jnp.where(valid, middle + nn(hidden, wm_ref[...]), 0.0).astype(BF16)
        ready(t)
        grad_out = jnp.where(valid, cot_ref[here, :].astype(F32), 0.0)
        grad_low = grad_out.astype(BF16)
        cot_ref[here, :] = grad_low
        grad_hidden = nt(grad_low, wm_ref[...])
        grad_gate = (grad_hidden * up * slope).astype(BF16)
        grad_up = (grad_hidden * gelu).astype(BF16)
        dgu_ref[here, :half] = grad_gate[:, :half]
        dgu_ref[here, half:] = grad_up[:, :half]
        grad_nm = nn(grad_gate, wi_ref[:ff, :]) + nn(grad_up, wi_ref[ff:, :])
        gg_ref[...] += jnp.sum((grad_nm * xhat).reshape(rows // 8, 8, -1), axis=0)
        grad_middle = grad_out + layer_back(grad_nm * gain, xhat, inv)
        gm_low = grad_middle.astype(BF16)
        gml_ref[here, :] = gm_low
        dctx_ref[here, :] = nt(gm_low, wo_ref[...]).astype(BF16)
        return carry

    lax.fori_loop(0, ctx_ref.shape[0] // rows, body, 0)


def phase_attend_back(q_ref, k_ref, v_ref, p_ref, ctx_ref, dctx_ref, tables, dqkv_ref, dk_ref, dv_ref, block0, lo, hi, after):
    width = q_ref.shape[1]
    half = width // 2
    span = TILE + 2 * HALF
    scaling = 1.0 / math.sqrt(HD)

    def body(t, carry):
        r0 = pl.multiple_of(t * TILE, TILE)
        low_head = head_masks((TILE, LANES))
        cosine, sine, first = rope_tile(tables, block0 + 1 + t * (TILE // HALF))
        cosine, sine = cosine * scaling, sine * -scaling
        keys = pl.ds(r0, span)
        for j in range(width // LANES):
            lanes = slice(j * LANES, (j + 1) * LANES)
            probs = p_ref[t, j]
            kc = k_ref[keys, lanes]
            dc = dctx_ref[pl.ds(r0, TILE), lanes]
            row_term = dc.astype(F32) * ctx_ref[pl.ds(r0, TILE), lanes].astype(F32)
            row_low = jnp.sum(jnp.where(low_head, row_term, 0.0), axis=-1, keepdims=True)
            row_high = jnp.sum(jnp.where(low_head, 0.0, row_term), axis=-1, keepdims=True)
            row_term = jnp.concatenate([row_low, row_high], axis=0)
            dc2 = split_heads(dc, low_head)
            grad_probs = nt(dc2, v_ref[keys, lanes])
            grad_scores = (probs.astype(F32) * (grad_probs - row_term)).astype(BF16)
            dq2 = nn(grad_scores, kc)
            dq = jnp.where(low_head, dq2[:TILE], dq2[TILE:])
            at = 3 * half * (j * LANES // half) + j * LANES % half
            dqkv_ref[pl.ds(r0, TILE), at : at + LANES] = turn(dq, cosine, sine, first).astype(BF16)
            q2 = split_heads(q_ref[pl.ds(r0 + HALF, TILE), lanes], low_head)
            dk_ref[keys, lanes] += tn(grad_scores, q2)
            dv_ref[keys, lanes] += tn(probs, dc2)
        after(t)
        return carry

    lax.fori_loop(lo, hi, body, 0)


def phase_pack(dk_ref, dv_ref, tables, dqkv_ref, block0, lo, hi):
    width = dk_ref.shape[1]
    half = width // 2

    def body(t, carry):
        r0 = pl.multiple_of(t * TILE, TILE)
        cosine, sine, first = rope_tile(tables, block0 + 1 + t * (TILE // HALF))
        ext = pl.ds(r0 + HALF, TILE)
        for j in range(width // LANES):
            lanes = slice(j * LANES, (j + 1) * LANES)
            at = 3 * half * (j * LANES // half) + j * LANES % half
            dqkv_ref[pl.ds(r0, TILE), at + half : at + half + LANES] = turn(dk_ref[ext, lanes], cosine, -sine, first).astype(BF16)
            dqkv_ref[pl.ds(r0, TILE), at + 2 * half : at + 2 * half + LANES] = dv_ref[ext, lanes].astype(BF16)
        return carry

    lax.fori_loop(lo, hi, body, 0)


def phase_input(x_ref, gm_ref, gain_ref, w_ref, dqkv_ref, out_ref, gg_ref, r0, rows):
    here = pl.ds(r0, rows)
    gain = gain_ref[:1, :].astype(F32)
    grad_normed = nn(dqkv_ref[here, :], w_ref[...])
    xhat, inv = layer_stats(x_ref[here, :].astype(F32))
    gg_ref[...] += jnp.sum((grad_normed * xhat).reshape(rows // 8, 8, -1), axis=0)
    out_ref[here, :] = (gm_ref[here, :].astype(F32) + layer_back(grad_normed * gain, xhat, inv)).astype(BF16)


def weight_grad(a_ref, b, out_ref, columns, at=0, count=None):
    for c in range(0, a_ref.shape[1] if count is None else count, columns):
        out_ref[c : c + columns, :] = tn(a_ref[:, at + c : at + c + columns], b).astype(out_ref.dtype)


def slot_of(at, of):
    return (of + 2 * (at // 2)) % 4


class Place:
    def __init__(self, n_shard):
        self.split = n_shard == 2
        self.x = lax.axis_index("shard")
        self.c = lax.axis_index("ctx")
        self.z = lax.axis_index("tp")
        self.k = self.c % 2
        self.y = self.c // 2
        self.up = (self.z + 1) % 4
        self.down = (self.z + 3) % 4
        self.mate = self.z + 1 - 2 * (self.z % 2)
        self.core = self.c + 1 - 2 * self.k
        self.across = (self.c + 2) % 4
        self.to_x = {"shard": 1 - self.x}
        self.to_up = {"tp": self.up}
        self.to_down = {"tp": self.down}
        self.to_mate = {"tp": self.mate}
        self.to_core = {"ctx": self.core}
        self.to_y = {"ctx": self.across}
        self.to_next = {"ctx": (self.c + 1) % 4}
        self.to_prev = {"ctx": (self.c + 3) % 4}

    def meet(self, partners):
        barrier = pltpu.get_barrier_semaphore()
        for device in partners:
            pl.semaphore_signal(barrier, inc=1, device_id=device, device_id_type=pl.DeviceIdType.MESH)
        pl.semaphore_wait(barrier, len(partners))


class Wires:
    def __init__(self, send, recv):
        self.send, self.recv, self.next, self.open = send, recv, 0, []

    def block(self, count):
        base = self.next
        self.next += count
        return base

    def remote(self, i, src, dst, device):
        return pltpu.make_async_remote_copy(
            src_ref=src, dst_ref=dst, send_sem=self.send.at[i], recv_sem=self.recv.at[i], device_id=device, device_id_type=pl.DeviceIdType.MESH
        )

    def local(self, i, src, dst):
        return pltpu.make_async_copy(src, dst, self.recv.at[i])

    def go(self, src, dst, device):
        copy = self.remote(self.block(1), src, dst, device)
        copy.start()
        self.open.append(copy)
        return copy

    def own(self, src, dst):
        copy = self.local(self.block(1), src, dst)
        copy.start()
        return copy

    @staticmethod
    def done(copies):
        for copy in copies:
            copy.wait()

    def close(self):
        for copy in self.open:
            copy.wait_send()


def started(copies):
    for copy in copies:
        copy.start()


class Stream:
    def __init__(self, wires, here, stage, target, rows, count, shift=0):
        self.wires, self.here, self.stage, self.target, self.rows, self.count, self.shift = wires, here, stage, target, rows, count, shift
        self.base = wires.block(2 * count)

    def pair(self, t):
        rows = pl.ds(pl.multiple_of(t * self.rows, self.rows), self.rows)
        to = pl.ds(pl.multiple_of((t + self.shift) * self.rows, self.rows), self.rows)
        src, dst = self.stage.at[rows, :], self.target.at[self.here.z % 2, to, :]
        return self.wires.remote(self.base + t, src, dst, self.here.to_mate), self.wires.local(self.base + self.count + t, src, dst)

    def start(self, t):
        started(self.pair(t))

    def finish(self):
        for t in range(self.count):
            self.wires.done(self.pair(t))


def landed(copies):
    for copy in copies:
        copy.wait_recv()


class Gather:
    SEMS = 12

    def __init__(self, shard, full, which, wires, here):
        self.shard, self.full, self.wires, self.here = shard, full, wires, here
        rows = shard.shape[0] // 6
        self.mine = pl.ds(rows * here.c, rows)
        self.rest = pl.ds(rows * (4 + here.k), rows)
        self.theirs = pl.ds(rows * here.across, rows)
        other = (here.z + 2) % 4
        self.to = [other, other + 1 - 2 * (other % 2)] if which else [here.mate]
        self.slots = [slot_of(to, here.z) - 2 * which for to in self.to]
        self.keeps = which == 0
        self.own_slot = here.z % 2
        self.base = wires.block(self.SEMS)

    def cols(self, x):
        cols = self.shard.shape[1]
        return pl.ds(pl.multiple_of(x * cols, LANES), cols) if self.here.split else pl.ds(0, cols)

    def spread(self):
        cols = self.cols(self.here.x)
        jobs = [(rows, to, slot) for rows in (self.rest, self.mine) for to, slot in zip(self.to, self.slots)]
        return [
            self.wires.remote(self.base + i, self.shard.at[rows, :], self.full.at[slot, rows, cols], {"tp": to})
            for i, (rows, to, slot) in enumerate(jobs)
        ]

    def kept(self):
        cols = self.cols(self.here.x)
        if not self.keeps:
            return []
        return [
            self.wires.local(self.base + 4 + i, self.shard.at[rows, :], self.full.at[self.own_slot, rows, cols])
            for i, rows in enumerate((self.rest, self.mine))
        ]

    def crossed(self):
        if not self.here.split:
            return []
        cols = self.cols(self.here.x)
        blocks = [self.full.at[:, rows, cols] for rows in (self.rest, self.mine)]
        return [self.wires.remote(self.base + 6 + i, block, block, self.here.to_x) for i, block in enumerate(blocks)]

    def level(self):
        block = self.full.at[:, self.mine, :]
        return [self.wires.remote(self.base + 8, block, block, self.here.to_y)]

    def pooled(self):
        blocks = [self.full.at[:, rows, :] for rows in (self.rest, self.mine)]
        return [self.wires.remote(self.base + 9 + i, block, block, self.here.to_core) for i, block in enumerate(blocks)]

    def passed(self):
        block = self.full.at[:, self.theirs, :]
        return [self.wires.remote(self.base + 11, block, block, self.here.to_core)]

    def stage(self, number):
        if number == 0:
            started(self.spread())
            started(self.kept())
        elif number == 1:
            landed(self.spread())
            self.wires.done(self.kept())
            started(self.crossed())
        elif number == 2:
            landed(self.crossed())
            started(self.level())
            started(self.pooled())
        elif number == 3:
            landed(self.level())
            started(self.passed())
        else:
            landed(self.pooled())
            landed(self.passed())

    def close(self):
        for copy in self.spread() + self.crossed() + self.level() + self.pooled() + self.passed():
            copy.wait_send()


def fire(jobs, *events):
    for event in events:
        jobs[event % 100].stage(event // 100)


def between(jobs, table):
    def after(t):
        for step, events in table.items():
            pl.when(t == step)(functools.partial(fire, jobs, *events))

    return after


class Reduce:
    SEMS = 5

    def __init__(self, grad, out, bufs, wires, here):
        self.grad, self.out, self.wires, self.here = grad, out, wires, here
        self.a, self.b, self.d, self.e = bufs
        rows = grad.shape[2] // 2
        self.keep = pl.ds(rows * here.k, rows)
        self.give = pl.ds(rows * (1 - here.k), rows)
        self.zs = here.z % 2
        self.base = wires.block(self.SEMS)

    @staticmethod
    def scratch(shape, n_shard):
        k, two, rows, width = shape
        cols = width // n_shard if n_shard == 2 else width
        half = rows // 2
        return [pltpu.VMEM(s, BF16) for s in ((k, two, half, width), (k, two, half, cols), (k, half, cols), (k, half, cols))]

    def cols(self, x):
        cols = self.out.shape[2]
        return pl.ds(pl.multiple_of(x * cols, LANES), cols)

    def copy(self, number):
        h, remote = self.here, self.wires.remote
        if number == 0:
            return remote(self.base, self.grad.at[:, :, self.give, :], self.a, h.to_core)
        if number == 1:
            return remote(self.base + 1, self.a.at[:, :, :, self.cols(1 - h.x)], self.b, h.to_x)
        if number == 2:
            return remote(self.base + 2, self.b.at[:, 1 - self.zs, :, :], self.d, h.to_mate)
        if number == 3:
            return remote(self.base + 3, self.d, self.e, h.to_y)
        done = self.out.at[:, self.keep, :]
        return remote(self.base + 4, done, done, h.to_core)

    def stage(self, number):
        if number > 0 and (self.here.split or number != 2):
            self.copy(number - 1).wait_recv()
        if number == 1:
            total = (self.grad[:, :, self.keep, :].astype(F32) + self.a[...].astype(F32)).astype(BF16)
            if not self.here.split:
                self.b[...] = total
                return
            self.a[...] = total
        elif number == 2 and self.here.split:
            self.b[...] = (self.a[:, :, :, self.cols(self.here.x)].astype(F32) + self.b[...].astype(F32)).astype(BF16)
        elif number == 3:
            self.d[...] = (self.b[:, self.zs, :, :].astype(F32) + self.d[...].astype(F32)).astype(BF16)
        elif number == 4:
            self.out[:, self.keep, :] = (self.d[...].astype(F32) + self.e[...].astype(F32)).astype(BF16)
        if number < 5:
            self.copy(number).start()

    def close(self):
        for number in range(5):
            if self.here.split or number != 1:
                self.copy(number).wait_send()


def front_kernel(n_shard, s_ref, x_ref, cot_hbm, gains_ref, *refs):
    shards, tables, refs = refs[:4], refs[4:8], refs[8:]
    saved, (layer_all, layer_tail, gains, dctx, gml, gg, dwm, dwi, dwo), refs = refs[:7], refs[7:16], refs[16:]
    wqkv, normed, q, k, v, p, ctx, wo, wi, wm, ext, cot, out, nm, hid, dgu, send, recv = refs
    h = Place(n_shard)
    near = [{"tp": (h.z + i) % 4} for i in (1, 2, 3)] + [{"ctx": (h.c + i) % 4} for i in (1, 2, 3)]
    if h.split:
        near.append(h.to_x)
    h.meet(near)
    wires = Wires(send, recv)
    local = x_ref.shape[2]
    seq = x_ref.at[0, h.z % 2]
    kept = [wires.own(seq, ext.at[pl.ds(HALF, local), :]), wires.own(cot_hbm.at[0, h.z % 2], cot)]
    rims = [
        wires.go(seq.at[pl.ds(0, HALF), :], ext.at[pl.ds(HALF + local, HALF), :], h.to_prev),
        wires.go(seq.at[pl.ds(local - HALF, HALF), :], ext.at[pl.ds(0, HALF), :], h.to_next),
    ]
    if h.split:
        cols = gains_ref.shape[1]
        mine = gains.at[:, pl.ds(pl.multiple_of(h.x * cols, LANES), cols)]
        kept.append(wires.own(gains_ref, mine))
        rims.append(wires.go(gains_ref, mine, h.to_x))
    else:
        kept.append(wires.own(gains_ref, gains))
    others = [(shards[1], wo, 0), (shards[2], wi, 0), (shards[2], wi, 1), (shards[3], wm, 0)]
    jobs = [Gather(shards[0].at[i], wqkv.at[which, i], which, wires, h) for which in range(2) for i in range(3)]
    jobs += [Gather(src.at[part], full.at[part, pl.ds(2 * which, 2)], which, wires, h) for which in range(2) for src, full, part in others]
    stream = Stream(wires, h, out, layer_all, 2 * TILE, local // (2 * TILE) - 1)
    fire(jobs, *range(9))
    wires.done(kept)
    landed(rims)
    phase_norm(ext, gains, normed)
    fire(jobs, 100, 9, 101, 102, 106, 103, 200, 107, 108, 10, 201, 109, 104, 202, 300, 400, 11, 206, 301, 105, 401, 203, 302, 402)
    qkv = functools.partial(phase_qkv, normed, wqkv, tables, q, k, v, s_ref[2], 384)
    attend = functools.partial(phase_attend, q, k, v, p, ctx, s_ref[1], s_ref[0])
    tiles = local // TILE
    half = p.shape[1] // 2
    qkv(0, between(jobs, {0: (306, 207), 1: (303, 406, 110, 12), 2: (403, 208)}))
    attend(
        range(half),
        0,
        tiles,
        between(
            jobs,
            {
                1: (307,),
                2: (209, 111),
                3: (407, 13),
                4: (204,),
                5: (308,),
                6: (205,),
                7: (408, 210, 309, 112, 409, 304, 211, 404, 305, 405),
            },
        ),
    )
    qkv(1, between(jobs, {0: (310, 212, 113), 1: (410,), 2: (311,)}))
    attend(range(half, 2 * half), 0, tiles, between(jobs, {1: (411,), 2: (312, 213), 4: (412,), 7: (313, 413)}))
    stores = [wires.own(src, dst) for src, dst in zip((wqkv, normed, q, k, v, p, ctx), saved)]
    wo, wi, wm = (w.reshape(-1, w.shape[-1]) for w in (wo, wi, wm))
    blocks = local // (2 * TILE)

    def ready(t):
        pl.when(t < blocks - 1)(functools.partial(stream.start, t))

    phase_mlp(ext, cot, ctx, gains, wo, wi, wm, out, gml, nm, hid, dgu, dctx, gg, s_ref[1], s_ref[0], 2 * TILE, ready)
    stores.append(wires.own(out.at[pl.ds(local - 2 * TILE, 2 * TILE), :], layer_tail))
    weight_grad(hid, cot[...], dwm, 192)
    weight_grad(dgu, nm[...], dwi, 384)
    weight_grad(ctx, gml[...], dwo, LANES, count=dwo.shape[0])
    wires.done(stores)
    stream.finish()
    for job in jobs:
        job.close()
    wires.close()


def back_kernel(n_shard, s_ref, gains_ref, gain2, *refs):
    tables, homes, (x_ref, layer_in, layer_tail), outs, refs = refs[:4], refs[4:16], refs[16:19], refs[19:26], refs[26:]
    layer_all, input_all, out_qkv, out_wi, out_wm, out_wo, out_gain = outs
    q, k, v, p, ctx, dctx, gml, normed, wqkv, dwi, dwm, dwo, x = refs[:13]
    dk, dv, dqkv, given, rim_out, rim_in, dw, gg, gbuf, send, recv = refs[13:24]
    bufs = refs[24:]
    h = Place(n_shard)
    wires = Wires(send, recv)
    q_home, k_home, v_home, p_home, ctx_home, dctx_home, gml_home, normed_home, wqkv_home, dwi_home, dwm_home, dwo_home = homes
    local, width = x.shape
    tiles = local // TILE
    loads = [wires.own(src, dst) for src, dst in ((k_home, k), (v_home, v), (q_home, q), (dctx_home, dctx), (ctx_home, ctx))]
    order = [tiles - 1, *range(tiles - 1)]
    tile_loads = {t: wires.own(p_home.at[t], p.at[t]) for t in order[:3]}
    grad_loads = [wires.own(src, dst) for src, dst in ((dwi_home, dwi), (dwm_home, dwm), (dwo_home, dwo))]
    tile_loads.update({t: wires.own(p_home.at[t], p.at[t]) for t in order[3:]})
    late_loads = [wires.own(src, dst) for src, dst in ((x_ref.at[0, h.z % 2], x), (gml_home, gml), (wqkv_home, wqkv), (normed_home, normed))]
    near = [h.to_mate] + [{"ctx": (h.c + i) % 4} for i in (1, 2, 3)]
    if h.split:
        near.append(h.to_x)
    h.meet(near)
    dw_parts = [(dwi.at[pl.ds(0, 1)], out_wi.at[pl.ds(0, 1)]), (dwi.at[pl.ds(1, 1)], out_wi.at[pl.ds(1, 1)]), (dwm, out_wm), (dwo, out_wo)]
    dw_parts += [(dw.at[pl.ds(i, 1)], out_qkv.at[pl.ds(i, 1)]) for i in range(3)] + [(gbuf, out_gain)]
    jobs = [Reduce(g, o, bufs[4 * i : 4 * i + 4], wires, h) for i, (g, o) in enumerate(dw_parts)]
    rows = 2 * TILE
    last = Stream(wires, h, layer_tail, layer_all, rows, 1, local // rows - 1)
    last.start(0)
    stream = Stream(wires, h, given, input_all, rows, local // rows)
    dk[...] = jnp.zeros_like(dk)
    dv[...] = jnp.zeros_like(dv)
    gg[...] = jnp.zeros_like(gg)
    wires.done(loads)
    wires.done(tile_loads[t] for t in order[:2])
    weights = wqkv.reshape(-1, width)

    def back(lo, hi, table):
        phase_attend_back(q, k, v, p, ctx, dctx, tables, dqkv, dk, dv, s_ref[2], lo, hi, between(jobs, table))

    def pack(lo, hi):
        phase_pack(dk, dv, tables, dqkv, s_ref[2], lo, hi)

    def finish(i):
        phase_input(x, gml, gains_ref, weights, dqkv, given, gg, i * rows, rows)
        stream.start(i)

    back(tiles - 1, tiles, {})
    wires.done(grad_loads)
    fire(jobs, 0, 1, 2, 3)
    back(0, 1, {})
    ext = local + 2 * HALF
    for i, ref in enumerate((dk, dv)):
        rim_out[0, i] = ref[:HALF, :].astype(BF16)
        rim_out[1, i] = ref[ext - HALF :, :].astype(BF16)
    rims = [wires.go(rim_out.at[0], rim_in.at[0], h.to_prev), wires.go(rim_out.at[1], rim_in.at[1], h.to_next)]
    fire(jobs, 100, 101)
    wires.done(tile_loads[t] for t in order[2:])
    back(1, 3, {1: (102, 103)})
    landed(rims)
    for i, ref in enumerate((dk, dv)):
        ref[HALF : 2 * HALF, :] += rim_in[1, i].astype(F32)
        ref[ext - 2 * HALF : ext - HALF, :] += rim_in[0, i].astype(F32)
    pack(0, 2)
    wires.done(late_loads)
    finish(0)
    back(3, 5, {3: (200, 201), 4: (202, 203)})
    pack(2, 4)
    finish(1)
    back(5, 7, {5: (300, 301), 6: (302, 303)})
    pack(4, 8)
    half = width // 2
    own = normed[HALF : HALF + local, :]
    for i in range(3):
        weight_grad(dqkv, own, dw.at[i].reshape(half, width), LANES, at=i * half, count=half)
        fire(jobs, 4 + i)
    finish(2)
    fire(jobs, 104, 105, 106)
    finish(3)
    gain_rows = jnp.concatenate([gg[...], gain2[...]], axis=0).astype(BF16)
    gain_rows = jnp.concatenate([gain_rows, gain_rows], axis=0)
    gbuf[0, 0] = gain_rows
    gbuf[0, 1] = gain_rows
    fire(jobs, 7, 400, 401, 402, 403, 107, 204, 207, 205, 206, 500, 501, 502, 503, 304, 307, 305, 306, 404, 407, 405, 406, 504, 507, 505, 506)
    stream.finish()
    last.finish()
    for job in jobs:
        job.close()
    wires.close()


def on_device(inputs, lengths, attn_gain, mlp_gain, qkv_weight, attn_weight, mlp_in_weight, mlp_out_weight, cotangent):
    n_tp = lax.axis_size("tp")
    n_ctx = lax.axis_size("ctx")
    tp = lax.axis_index("tp")
    ctx = lax.axis_index("ctx")
    seqs, local = inputs.shape[1], inputs.shape[2]
    width = inputs.shape[3]
    group = n_tp // 2
    mine = tp % seqs
    pair = tp // 2
    tables = tuple(jnp.asarray(t) for t in rope_constants(local * n_ctx))

    n_shard = lax.axis_size("shard")
    shards = [jnp.transpose(qkv_weight, (1, 2, 0)), attn_weight[None], jnp.transpose(mlp_in_weight, (1, 2, 0)), mlp_out_weight[None]]
    gains = jnp.pad(jnp.stack([attn_gain, mlp_gain]), ((0, 14), (0, 0)))
    if n_shard != 2:
        shards = [lax.all_gather(s, "shard", axis=2, tiled=True) for s in shards]
        gains = lax.all_gather(gains, "shard", axis=1, tiled=True)
    hbm = pl.BlockSpec(memory_space=pl.ANY)
    vmem = pl.BlockSpec(memory_space=pltpu.VMEM)
    smem = pl.BlockSpec(memory_space=pltpu.SMEM)
    length = lax.dynamic_index_in_dim(lengths[0], mine, 0, keepdims=True)
    block0 = ctx * (local // HALF) - 1
    pos0 = ctx * local
    scalars = jnp.stack([length[0], pos0.astype(jnp.int32), block0.astype(jnp.int32)])
    ext = local + 2 * HALF
    tiles = local // TILE
    chunks = width // LANES
    span = TILE + 2 * HALF
    wide = ((ext, width), BF16)
    tall = ((local, width), BF16)
    full_shapes = [(s.shape[0], n_tp, s.shape[1], width) for s in shards]
    ff_half = 2 * mlp_out_weight.shape[0]
    width_half = width // 2
    saved = [
        ((2, 3, 2, shards[0].shape[1], width), BF16),
        wide, wide, wide, wide,
        ((tiles, chunks, 2 * TILE, span), BF16),
        tall,
    ]
    outs = [
        ((2 * TILE, width), BF16),
        ((16, width), BF16),
        tall, tall,
        ((8, width), F32),
        ((ff_half, width), BF16), ((2 * ff_half, width), BF16), ((width_half, width), BF16),
    ]
    both = ((seqs, local, width), BF16)
    copies = 14 * Gather.SEMS + 24
    results = pl.pallas_call(
        functools.partial(front_kernel, n_shard),
        out_shape=[jax.ShapeDtypeStruct(*o) for o in saved + [both] + outs],
        in_specs=[smem] + [hbm] * 7 + [vmem] * 4,
        out_specs=[hbm] * 9 + [vmem] * 7,
        scratch_shapes=[pltpu.VMEM(*o) for o in saved]
        + [pltpu.VMEM(f, BF16) for f in full_shapes[1:]]
        + [
            pltpu.VMEM(*wide),
            pltpu.VMEM(*tall),
            pltpu.VMEM(*tall),
            pltpu.VMEM(*tall),
            pltpu.VMEM((local, ff_half), BF16),
            pltpu.VMEM((local, 2 * ff_half), BF16),
            pltpu.SemaphoreType.DMA((copies,)),
            pltpu.SemaphoreType.DMA((copies,)),
        ],
        compiler_params=pltpu.CompilerParams(collective_id=0, has_side_effects=True, vmem_limit_bytes=VMEM_LIMIT),
        name="front",
    )(scalars, inputs, cotangent, gains, *shards, *tables)
    wqkv, normed, q, k, v, probs, context, layer_all, layer_tail, gains, dctx, gml, gain2_part, dwm, dwi, dwo = results
    cols = width // n_shard if n_shard == 2 else width
    grads = [(3, 2, width_half // 2, width), (2, 2, ff_half // 2, width), (1, 2, ff_half // 2, width), (1, 2, width_half // 2, width), (1, 2, 32, width)]
    dwi, dwm, dwo = (g.reshape(shape) for g, shape in zip((dwi, dwm, dwo), grads[1:]))
    jobs = [(1, *grads[1][1:])] * 2 + grads[2:4] + [(1, *grads[0][1:])] * 3 + grads[4:]
    sends = 96
    homes = (q, k, v, probs, context, dctx, gml, normed, wqkv, dwi, dwm, dwo)
    layer_out, input_grad, *owned = pl.pallas_call(
        functools.partial(back_kernel, n_shard),
        out_shape=[jax.ShapeDtypeStruct(*both)] * 2 + [jax.ShapeDtypeStruct((g[0], g[2], cols), BF16) for g in grads],
        in_specs=[smem] + [vmem] * 6 + [hbm] * 15,
        out_specs=[hbm] * 2 + [vmem] * len(grads),
        input_output_aliases={20: 0},
        scratch_shapes=[pltpu.VMEM(a.shape, a.dtype) for a in homes]
        + [
            pltpu.VMEM(*tall),
            pltpu.VMEM((ext, width), F32),
            pltpu.VMEM((ext, width), F32),
            pltpu.VMEM((local, 3 * width), BF16),
            pltpu.VMEM(*tall),
            pltpu.VMEM((2, 2, HALF, width), BF16),
            pltpu.VMEM((2, 2, HALF, width), BF16),
            pltpu.VMEM(grads[0], BF16),
            pltpu.VMEM((8, width), F32),
            pltpu.VMEM(grads[4], BF16),
            pltpu.SemaphoreType.DMA((sends,)),
            pltpu.SemaphoreType.DMA((sends,)),
        ]
        + [b for g in jobs for b in Reduce.scratch(g, n_shard)],
        compiler_params=pltpu.CompilerParams(collective_id=1, has_side_effects=True, vmem_limit_bytes=VMEM_LIMIT),
        name="back",
    )(scalars, gains, gain2_part, *tables, *homes, inputs, layer_all, layer_tail)
    owned = [g.astype(F32) for g in owned]
    if n_shard != 2:
        owned = [lax.psum_scatter(g, "shard", scatter_dimension=2, tiled=True) for g in owned]
    qkv_grad = jnp.transpose(owned[0], (2, 0, 1))
    mlp_in_grad = jnp.transpose(owned[1], (2, 0, 1))
    mlp_out_grad, attn_grad = owned[2][0], owned[3][0]
    share = owned[4].shape[2] // n_tp
    gains = lax.dynamic_slice_in_dim(owned[4][0, :16], tp * share, share, axis=1)
    gains = jnp.sum(gains.reshape(2, 8, share), axis=1)
    return (layer_out[None], input_grad[None], qkv_grad, attn_grad, mlp_in_grad, mlp_out_grad, gains[0], gains[1])


def solution(mesh):
    in_specs = (
        P("shard", None, "ctx", None),
        P("shard", None),
        P("shard"),
        P("shard"),
        P("shard", None, "tp"),
        P("tp", "shard"),
        P("shard", None, "tp"),
        P("tp", "shard"),
        P("shard", None, "ctx", None),
    )
    out_specs = (
        P("shard", None, "ctx", None),
        P("shard", None, "ctx", None),
        P("shard", None, "tp"),
        P("tp", "shard"),
        P("shard", None, "tp"),
        P("tp", "shard"),
        P(("shard", "tp")),
        P(("shard", "tp")),
    )
    return jax.shard_map(on_device, mesh=mesh, in_specs=in_specs, out_specs=out_specs, check_vma=False)
```

time: 236 us -> 190 us (0.81)
  Pallas kernels: 213 us -> 171 us
  local copies, waits for them, and re-layouts: 13.7 us -> 8.65 us
    pallas_call x1, Pallas kernels: 102 us -> 74 us  [on_device(): pl.pallas_call(functools.partial(back_kernel, n_shard), out_shape=[jax.Sh...]
    pallas_call x2 -> x1, Pallas kernels: 111 us -> 97.3 us  [on_device(): pl.pallas_call(functools.partial(front_kernel, n_shard), out_shape=[jax.S...]
    squeeze x1 -> x0, local copies, waits for them, and re-layouts: 3.85 us -> none  [on_device(): cot = lax.dynamic_index_in_dim(cotangent[0], mine, 0, keepdims=False)]
    unnamed x10 -> x8, local copies, waits for them, and re-layouts: 5.33 us -> 5.33 us
where the time goes in v4:
time: 190 us
  Pallas kernels  171 us (90%)
  other arithmetic  9.27 us (5%)
  local copies, waits for them, and re-layouts  8.65 us (5%)
    pallas_call x1, Pallas kernels, on_device(): pl.pallas_call(functools.partial(front_kernel, n_shard), out_shape=[jax.S...  97.3 us
    pallas_call x1, Pallas kernels, on_device(): pl.pallas_call(functools.partial(back_kernel, n_shard), out_shape=[jax.Sh...  74 us
    unnamed x8, local copies, waits for them, and re-layouts  5.33 us

profile of v4, /device:TPU:0, one launch (start us, length us, event | category | flops | bytes accessed | tf_op | source)
XLA Modules:
  0.0 189.9 jit_solution(17451839968854280729)
XLA Ops:
  0.6 0.0 copy-start
  0.7 0.6 copy-done
  1.3 0.6 constant_dynamic-slice_fusion
  1.9 1.2 pad_add_fusion.s_ref
  3.1 0.7 stack.21
  3.8 0.7 stack.22
  4.5 0.6 fusion.2.gains_ref
  5.1 97.3 %front.1 = (bf16[2,3,2,192,768]{4,3,2,1,0:T(8,128)(2,1)}, bf16[1152,768]{1,0:T(8,128)(2,1)}, bf16[1152,768]{1,0:T(8,128)(2,1)}, bf16[1152,768]{1,0:T(8,128)(2,1)...) custom-call(s32[3]{0:T(128)} %pad_add_fusion.s_ref, ...), custom_call_target="tpu_custom_call" | custom-call | tf_op jit(solution)/shard_map/front/pallas_call | solution.py:725
  102.4 74.0 %back.1 = (bf16[2,1024,768]{2,1,0:T(8,128)(2,1)}, bf16[2,1024,768]{2,1,0:T(8,128)(2,1)}, bf16[3,192,384]{2,1,0:T(8,128)(2,1)}, bf16[2,288,384]{2,1,0:T(8,128)(2,...) custom-call(s32[3]{0:T(128)} %pad_add_fusion.s_ref, ...), custom_call_target="tpu_custom_call", output_to_operand_aliasing={{0}: (20, {})} | custom-call | tf_op jit(solution)/shard_map/back/pallas_call | solution.py:752
  176.4 0.0 copy-start.1
  176.4 0.9 slice.12
  177.3 0.1 bitcast_reduce_fusion
  177.4 0.5 slice_bitcast_fusion
  177.9 1.6 bitcast_convert_fusion.1
  179.5 1.7 bitcast_convert_fusion
  181.3 2.0 %convert_bitcast_fusion.1 = f32[384,3,192]{0,2,1:T(8,128)} fusion(bf16[3,192,384]{2,1,0:T(8,128)(2,1)} %get-tuple-element.49), kind=kLoop, calls=%fused_computation.1 | loop fusion | flops 221184 | bytes 1327104 | tf_op jit(solution)/shard_map/transpose | solution.py:780
  183.2 2.0 %convert_bitcast_fusion = f32[384,2,288]{0,2,1:T(8,128)} fusion(bf16[2,288,384]{2,1,0:T(8,128)(2,1)} %get-tuple-element.51), kind=kLoop, calls=%fused_computation | loop fusion | flops 221184 | bytes 1327104 | tf_op jit(solution)/shard_map/transpose | solution.py:781
  185.2 0.0 copy-done.1
  185.2 0.0 copy-start.2
  185.2 1.7 copy.25
  186.9 1.4 copy-done.2
  188.2 1.7 copy.26
Async XLA Ops:
  0.6 0.7 copy-start
  176.4 8.8 %copy-start.1 = (bf16[2,1024,768]{2,1,0:T(8,128)(2,1)S(1)}, bf16[2,1024,768]{2,1,0:T(8,128)(2,1)}, u32[]{:S(2)}) copy-start(bf16[2,1024,768]{2,1,0:T(8,128)(2,1)} %get-tuple-element.47) | copy-start | bytes 9437188
  185.2 3.0 %copy-start.2 = (bf16[2,1024,768]{2,1,0:T(8,128)(2,1)S(1)}, bf16[2,1024,768]{2,1,0:T(8,128)(2,1)}, u32[]{:S(2)}) copy-start(bf16[2,1024,768]{2,1,0:T(8,128)(2,1)} %get-tuple-element.48) | copy-start | bytes 9437188

commit v5 on v4

--- a/solution.py
+++ b/solution.py
@@ -19,6 +19,15 @@
 masked_score = -1e30
 F32 = jnp.float32
 BF16 = jnp.bfloat16
+FRONT_BLOCKS = 2
+FORWARD = (
+    (100, 101, 102, 106, 103, 200, 201, 104, 202, 300, 206, 400, 301, 105, 203, 401, 302, 204, 402),
+    {0: (306, 107, 108, 109, 110), 1: (303, 205)},
+    {0: (304,), 1: (207,), 3: (305, 111), 4: (208,), 6: (307,), 7: (403, 404, 405, 209)},
+    {0: (112,), 1: (308, 210)},
+    {2: (309, 211), 3: (113,), 4: (212, 310), 7: (406, 407, 408, 409, 410, 311)},
+    {0: (213, 312, 313, 411, 412, 413)},
+)
 VMEM_LIMIT = 60 * 1024 * 1024
 
 
@@ -144,9 +153,18 @@
     lax.fori_loop(lo, hi, body, 0)
 
 
-def phase_mlp(x_ref, cot_ref, ctx_ref, gain_ref, wo_ref, wi_ref, wm_ref, out_ref, gml_ref, nm_ref, hid_ref, dgu_ref, dctx_ref, gg_ref, pos0, length, rows, ready):
-    ff = wm_ref.shape[0]
-    half = hid_ref.shape[1]
+def units(nm, grad_low, wg, wu, wm):
+    gate = nt(nm, wg)
+    up = nt(nm, wu)
+    cdf = 0.5 + 0.5 * lax.erf(gate * math.sqrt(0.5))
+    gelu = gate * cdf
+    slope = cdf + gate * (jnp.exp(-0.5 * gate * gate) * (1.0 / math.sqrt(2.0 * math.pi)))
+    grad_hidden = nt(grad_low, wm)
+    return (gelu * up).astype(BF16), (grad_hidden * up * slope).astype(BF16), (grad_hidden * gelu).astype(BF16)
+
+
+def phase_mlp(x_ref, cot_ref, ctx_ref, gain_ref, wo_ref, wi_refs, wm_refs, out_ref, gml_ref, nm_ref, hid_ref, dgu_ref, dctx_ref, gg_ref, pos0, length, rows, between_halves, ready):
+    half = wm_refs[0].shape[0]
     gg_ref[...] = jnp.zeros_like(gg_ref)
 
     def body(t, carry):
@@ -157,28 +175,24 @@
         xhat, inv = layer_stats(middle)
         nm = (xhat * gain).astype(BF16)
         nm_ref[here, :] = nm
-        gate = nt(nm, wi_ref[:ff, :])
-        up = nt(nm, wi_ref[ff:, :])
-        cdf = 0.5 + 0.5 * lax.erf(gate * math.sqrt(0.5))
-        gelu = gate * cdf
-        slope = cdf + gate * (jnp.exp(-0.5 * gate * gate) * (1.0 / math.sqrt(2.0 * math.pi)))
-        hidden = (gelu * up).astype(BF16)
-        hid_ref[here, :] = hidden[:, :half]
         valid = pos0 + r0 + lax.broadcasted_iota(jnp.int32, (rows, 1), 0) < length
-        out_ref[here, :] = jnp.where(valid, middle + nn(hidden, wm_ref[...]), 0.0).astype(BF16)
+        grad_low = jnp.where(valid, cot_ref[here, :].astype(F32), 0.0).astype(BF16)
+        cot_ref[here, :] = grad_low
+        wg, wu, wm = wi_refs[0][:half, :], wi_refs[0][half:, :], wm_refs[0][...]
+        hidden, grad_gate, grad_up = units(nm, grad_low, wg, wu, wm)
+        hid_ref[here, :] = hidden
+        dgu_ref[here, :half] = grad_gate
+        dgu_ref[here, half:] = grad_up
+        mlp = nn(hidden, wm)
+        grad_nm = nn(grad_gate, wg) + nn(grad_up, wu)
+        between_halves(t)
+        wg, wu, wm = wi_refs[1][:half, :], wi_refs[1][half:, :], wm_refs[1][...]
+        hidden, grad_gate, grad_up = units(nm, grad_low, wg, wu, wm)
+        out_ref[here, :] = jnp.where(valid, middle + (mlp + nn(hidden, wm)), 0.0).astype(BF16)
         ready(t)
-        grad_out = jnp.where(valid, cot_ref[here, :].astype(F32), 0.0)
-        grad_low = grad_out.astype(BF16)
-        cot_ref[here, :] = grad_low
-        grad_hidden = nt(grad_low, wm_ref[...])
-        grad_gate = (grad_hidden * up * slope).astype(BF16)
-        grad_up = (grad_hidden * gelu).astype(BF16)
-        dgu_ref[here, :half] = grad_gate[:, :half]
-        dgu_ref[here, half:] = grad_up[:, :half]
-        grad_nm = nn(grad_gate, wi_ref[:ff, :]) + nn(grad_up, wi_ref[ff:, :])
+        grad_nm = grad_nm + nn(grad_gate, wg) + nn(grad_up, wu)
         gg_ref[...] += jnp.sum((grad_nm * xhat).reshape(rows // 8, 8, -1), axis=0)
-        grad_middle = grad_out + layer_back(grad_nm * gain, xhat, inv)
-        gm_low = grad_middle.astype(BF16)
+        gm_low = (grad_low.astype(F32) + layer_back(grad_nm * gain, xhat, inv)).astype(BF16)
         gml_ref[here, :] = gm_low
         dctx_ref[here, :] = nt(gm_low, wo_ref[...]).astype(BF16)
         return carry
@@ -332,22 +346,31 @@
 
 
 class Stream:
-    def __init__(self, wires, here, stage, target, rows, count, shift=0):
-        self.wires, self.here, self.stage, self.target, self.rows, self.count, self.shift = wires, here, stage, target, rows, count, shift
-        self.base = wires.block(2 * count)
-
-    def pair(self, t):
+    def __init__(self, wires, here, stage, target, rows, sent):
+        self.wires, self.here, self.stage, self.target, self.rows, self.sent = wires, here, stage, target, rows, sent
+        self.count = target.shape[1] // rows
+        self.base = wires.block(2 * self.count)
+
+    def block(self, t):
         rows = pl.ds(pl.multiple_of(t * self.rows, self.rows), self.rows)
-        to = pl.ds(pl.multiple_of((t + self.shift) * self.rows, self.rows), self.rows)
-        src, dst = self.stage.at[rows, :], self.target.at[self.here.z % 2, to, :]
-        return self.wires.remote(self.base + t, src, dst, self.here.to_mate), self.wires.local(self.base + self.count + t, src, dst)
+        dst = self.target.at[self.here.z % 2, rows, :]
+        return dst if self.stage is None else self.stage.at[rows, :], dst
+
+    def remote(self, t):
+        return self.wires.remote(self.base + t, *self.block(t), self.here.to_mate)
+
+    def local(self, t):
+        return self.wires.local(self.base + self.count + t, *self.block(t))
 
     def start(self, t):
-        started(self.pair(t))
+        self.local(t).start()
+        pl.when(t < self.sent)(lambda: self.remote(t).start())
 
     def finish(self):
         for t in range(self.count):
-            self.wires.done(self.pair(t))
+            self.local(t).wait()
+        for t in range(self.sent):
+            self.remote(t).wait()
 
 
 def landed(copies):
@@ -356,14 +379,14 @@
 
 
 class Gather:
-    SEMS = 12
+    SEMS = 7
 
     def __init__(self, shard, full, which, wires, here):
         self.shard, self.full, self.wires, self.here = shard, full, wires, here
         rows = shard.shape[0] // 6
-        self.mine = pl.ds(rows * here.c, rows)
-        self.rest = pl.ds(rows * (4 + here.k), rows)
-        self.theirs = pl.ds(rows * here.across, rows)
+        self.carried = pl.ds(rows * (3 * here.k + here.y), 2 * rows)
+        self.mine = pl.ds(rows * (3 * here.k + 2 * here.y), rows)
+        self.theirs = pl.ds(rows * (3 * here.k + 2 - 2 * here.y), rows)
         other = (here.z + 2) % 4
         self.to = [other, other + 1 - 2 * (other % 2)] if which else [here.mate]
         self.slots = [slot_of(to, here.z) - 2 * which for to in self.to]
@@ -376,40 +399,35 @@
         return pl.ds(pl.multiple_of(x * cols, LANES), cols) if self.here.split else pl.ds(0, cols)
 
     def spread(self):
-        cols = self.cols(self.here.x)
-        jobs = [(rows, to, slot) for rows in (self.rest, self.mine) for to, slot in zip(self.to, self.slots)]
+        src, cols = self.shard.at[self.carried, :], self.cols(self.here.x)
         return [
-            self.wires.remote(self.base + i, self.shard.at[rows, :], self.full.at[slot, rows, cols], {"tp": to})
-            for i, (rows, to, slot) in enumerate(jobs)
+            self.wires.remote(self.base + i, src, self.full.at[slot, self.carried, cols], {"tp": to})
+            for i, (to, slot) in enumerate(zip(self.to, self.slots))
         ]
 
     def kept(self):
-        cols = self.cols(self.here.x)
         if not self.keeps:
             return []
-        return [
-            self.wires.local(self.base + 4 + i, self.shard.at[rows, :], self.full.at[self.own_slot, rows, cols])
-            for i, rows in enumerate((self.rest, self.mine))
-        ]
+        dst = self.full.at[self.own_slot, self.carried, self.cols(self.here.x)]
+        return [self.wires.local(self.base + 2, self.shard.at[self.carried, :], dst)]
 
     def crossed(self):
         if not self.here.split:
             return []
-        cols = self.cols(self.here.x)
-        blocks = [self.full.at[:, rows, cols] for rows in (self.rest, self.mine)]
-        return [self.wires.remote(self.base + 6 + i, block, block, self.here.to_x) for i, block in enumerate(blocks)]
+        block = self.full.at[:, self.carried, self.cols(self.here.x)]
+        return [self.wires.remote(self.base + 3, block, block, self.here.to_x)]
 
     def level(self):
         block = self.full.at[:, self.mine, :]
-        return [self.wires.remote(self.base + 8, block, block, self.here.to_y)]
+        return [self.wires.remote(self.base + 4, block, block, self.here.to_y)]
 
     def pooled(self):
-        blocks = [self.full.at[:, rows, :] for rows in (self.rest, self.mine)]
-        return [self.wires.remote(self.base + 9 + i, block, block, self.here.to_core) for i, block in enumerate(blocks)]
+        block = self.full.at[:, self.carried, :]
+        return [self.wires.remote(self.base + 5, block, block, self.here.to_core)]
 
     def passed(self):
         block = self.full.at[:, self.theirs, :]
-        return [self.wires.remote(self.base + 11, block, block, self.here.to_core)]
+        return [self.wires.remote(self.base + 6, block, block, self.here.to_core)]
 
     def stage(self, number):
         if number == 0:
@@ -508,9 +526,9 @@
                 self.copy(number).wait_send()
 
 
-def front_kernel(n_shard, s_ref, x_ref, cot_hbm, gains_ref, *refs):
+def front_kernel(n_shard, len_ref, x_ref, cot_hbm, gains_ref, *refs):
     shards, tables, refs = refs[:4], refs[4:8], refs[8:]
-    saved, (layer_all, layer_tail, gains, dctx, gml, gg, dwm, dwi, dwo), refs = refs[:7], refs[7:16], refs[16:]
+    saved, (layer_all, gains, dctx, gml, gg, dwm, dwi, dwo), refs = refs[:7], refs[7:15], refs[15:]
     wqkv, normed, q, k, v, p, ctx, wo, wi, wm, ext, cot, out, nm, hid, dgu, send, recv = refs
     h = Place(n_shard)
     near = [{"tp": (h.z + i) % 4} for i in (1, 2, 3)] + [{"ctx": (h.c + i) % 4} for i in (1, 2, 3)]
@@ -519,6 +537,7 @@
     h.meet(near)
     wires = Wires(send, recv)
     local = x_ref.shape[2]
+    length, pos0, block0 = len_ref[0, h.z % 2], h.c * local, h.c * (local // HALF) - 1
     seq = x_ref.at[0, h.z % 2]
     kept = [wires.own(seq, ext.at[pl.ds(HALF, local), :]), wires.own(cot_hbm.at[0, h.z % 2], cot)]
     rims = [
@@ -532,48 +551,33 @@
         rims.append(wires.go(gains_ref, mine, h.to_x))
     else:
         kept.append(wires.own(gains_ref, gains))
-    others = [(shards[1], wo, 0), (shards[2], wi, 0), (shards[2], wi, 1), (shards[3], wm, 0)]
     jobs = [Gather(shards[0].at[i], wqkv.at[which, i], which, wires, h) for which in range(2) for i in range(3)]
-    jobs += [Gather(src.at[part], full.at[part, pl.ds(2 * which, 2)], which, wires, h) for which in range(2) for src, full, part in others]
-    stream = Stream(wires, h, out, layer_all, 2 * TILE, local // (2 * TILE) - 1)
-    fire(jobs, *range(9))
+    jobs += [Gather(shards[1].at[0], wo.at[which], which, wires, h) for which in range(2)]
+    for which in range(2):
+        jobs += [Gather(shards[2].at[i], wi.at[which, i], which, wires, h) for i in range(2)]
+        jobs.append(Gather(shards[3].at[0], wm.at[which], which, wires, h))
+    stream = Stream(wires, h, out, layer_all, 2 * TILE, FRONT_BLOCKS)
+    fire(jobs, *range(14))
     wires.done(kept)
     landed(rims)
     phase_norm(ext, gains, normed)
-    fire(jobs, 100, 9, 101, 102, 106, 103, 200, 107, 108, 10, 201, 109, 104, 202, 300, 400, 11, 206, 301, 105, 401, 203, 302, 402)
-    qkv = functools.partial(phase_qkv, normed, wqkv, tables, q, k, v, s_ref[2], 384)
-    attend = functools.partial(phase_attend, q, k, v, p, ctx, s_ref[1], s_ref[0])
+    fire(jobs, *FORWARD[0])
+    qkv = functools.partial(phase_qkv, normed, wqkv, tables, q, k, v, block0, 384)
+    attend = functools.partial(phase_attend, q, k, v, p, ctx, pos0, length)
     tiles = local // TILE
     half = p.shape[1] // 2
-    qkv(0, between(jobs, {0: (306, 207), 1: (303, 406, 110, 12), 2: (403, 208)}))
-    attend(
-        range(half),
-        0,
-        tiles,
-        between(
-            jobs,
-            {
-                1: (307,),
-                2: (209, 111),
-                3: (407, 13),
-                4: (204,),
-                5: (308,),
-                6: (205,),
-                7: (408, 210, 309, 112, 409, 304, 211, 404, 305, 405),
-            },
-        ),
-    )
-    qkv(1, between(jobs, {0: (310, 212, 113), 1: (410,), 2: (311,)}))
-    attend(range(half, 2 * half), 0, tiles, between(jobs, {1: (411,), 2: (312, 213), 4: (412,), 7: (313, 413)}))
+    qkv(0, between(jobs, FORWARD[1]))
+    attend(range(half), 0, tiles, between(jobs, FORWARD[2]))
+    qkv(1, between(jobs, FORWARD[3]))
+    attend(range(half, 2 * half), 0, tiles, between(jobs, FORWARD[4]))
     stores = [wires.own(src, dst) for src, dst in zip((wqkv, normed, q, k, v, p, ctx), saved)]
-    wo, wi, wm = (w.reshape(-1, w.shape[-1]) for w in (wo, wi, wm))
-    blocks = local // (2 * TILE)
-
-    def ready(t):
-        pl.when(t < blocks - 1)(functools.partial(stream.start, t))
-
-    phase_mlp(ext, cot, ctx, gains, wo, wi, wm, out, gml, nm, hid, dgu, dctx, gg, s_ref[1], s_ref[0], 2 * TILE, ready)
-    stores.append(wires.own(out.at[pl.ds(local - 2 * TILE, 2 * TILE), :], layer_tail))
+    width = wo.shape[-1]
+    wo = wo.reshape(-1, width)
+    wi_near, wi_far = (wi.at[i].reshape(-1, width) for i in range(2))
+    wm_near, wm_far = (wm.at[i].reshape(-1, width) for i in range(2))
+    rows = 2 * TILE
+    wis, wms = (wi_near, wi_far), (wm_near, wm_far)
+    phase_mlp(ext, cot, ctx, gains, wo, wis, wms, out, gml, nm, hid, dgu, dctx, gg, pos0, length, rows, between(jobs, FORWARD[5]), stream.start)
     weight_grad(hid, cot[...], dwm, 192)
     weight_grad(dgu, nm[...], dwi, 384)
     weight_grad(ctx, gml[...], dwo, LANES, count=dwo.shape[0])
@@ -584,8 +588,8 @@
     wires.close()
 
 
-def back_kernel(n_shard, s_ref, gains_ref, gain2, *refs):
-    tables, homes, (x_ref, layer_in, layer_tail), outs, refs = refs[:4], refs[4:16], refs[16:19], refs[19:26], refs[26:]
+def back_kernel(n_shard, gains_ref, gain2, *refs):
+    tables, homes, (x_ref, layer_in), outs, refs = refs[:4], refs[4:16], refs[16:18], refs[18:25], refs[25:]
     layer_all, input_all, out_qkv, out_wi, out_wm, out_wo, out_gain = outs
     q, k, v, p, ctx, dctx, gml, normed, wqkv, dwi, dwm, dwo, x = refs[:13]
     dk, dv, dqkv, given, rim_out, rim_in, dw, gg, gbuf, send, recv = refs[13:24]
@@ -594,6 +598,7 @@
     wires = Wires(send, recv)
     q_home, k_home, v_home, p_home, ctx_home, dctx_home, gml_home, normed_home, wqkv_home, dwi_home, dwm_home, dwo_home = homes
     local, width = x.shape
+    block0 = h.c * (local // HALF) - 1
     tiles = local // TILE
     loads = [wires.own(src, dst) for src, dst in ((k_home, k), (v_home, v), (q_home, q), (dctx_home, dctx), (ctx_home, ctx))]
     order = [tiles - 1, *range(tiles - 1)]
@@ -609,8 +614,9 @@
     dw_parts += [(dw.at[pl.ds(i, 1)], out_qkv.at[pl.ds(i, 1)]) for i in range(3)] + [(gbuf, out_gain)]
     jobs = [Reduce(g, o, bufs[4 * i : 4 * i + 4], wires, h) for i, (g, o) in enumerate(dw_parts)]
     rows = 2 * TILE
-    last = Stream(wires, h, layer_tail, layer_all, rows, 1, local // rows - 1)
-    last.start(0)
+    last = Stream(wires, h, None, layer_all, rows, local // rows)
+    for t in range(FRONT_BLOCKS, last.count):
+        last.remote(t).start()
     stream = Stream(wires, h, given, input_all, rows, local // rows)
     dk[...] = jnp.zeros_like(dk)
     dv[...] = jnp.zeros_like(dv)
@@ -620,57 +626,77 @@
     weights = wqkv.reshape(-1, width)
 
     def back(lo, hi, table):
-        phase_attend_back(q, k, v, p, ctx, dctx, tables, dqkv, dk, dv, s_ref[2], lo, hi, between(jobs, table))
+        phase_attend_back(q, k, v, p, ctx, dctx, tables, dqkv, dk, dv, block0, lo, hi, between(jobs, table))
 
     def pack(lo, hi):
-        phase_pack(dk, dv, tables, dqkv, s_ref[2], lo, hi)
+        phase_pack(dk, dv, tables, dqkv, block0, lo, hi)
 
     def finish(i):
         phase_input(x, gml, gains_ref, weights, dqkv, given, gg, i * rows, rows)
-        stream.start(i)
-
-    back(tiles - 1, tiles, {})
+
     wires.done(grad_loads)
     fire(jobs, 0, 1, 2, 3)
+    back(tiles - 1, tiles, {})
+    fire(jobs, 100, 101)
     back(0, 1, {})
     ext = local + 2 * HALF
     for i, ref in enumerate((dk, dv)):
         rim_out[0, i] = ref[:HALF, :].astype(BF16)
         rim_out[1, i] = ref[ext - HALF :, :].astype(BF16)
     rims = [wires.go(rim_out.at[0], rim_in.at[0], h.to_prev), wires.go(rim_out.at[1], rim_in.at[1], h.to_next)]
-    fire(jobs, 100, 101)
+    fire(jobs, 102, 103)
     wires.done(tile_loads[t] for t in order[2:])
-    back(1, 3, {1: (102, 103)})
+    back(1, tiles - 1, {4: (200,), 6: (201,)})
     landed(rims)
     for i, ref in enumerate((dk, dv)):
         ref[HALF : 2 * HALF, :] += rim_in[1, i].astype(F32)
         ref[ext - 2 * HALF : ext - HALF, :] += rim_in[0, i].astype(F32)
-    pack(0, 2)
+    pack(0, tiles)
     wires.done(late_loads)
     finish(0)
-    back(3, 5, {3: (200, 201), 4: (202, 203)})
-    pack(2, 4)
-    finish(1)
-    back(5, 7, {5: (300, 301), 6: (302, 303)})
-    pack(4, 8)
+    stream.start(0)
     half = width // 2
     own = normed[HALF : HALF + local, :]
     for i in range(3):
         weight_grad(dqkv, own, dw.at[i].reshape(half, width), LANES, at=i * half, count=half)
         fire(jobs, 4 + i)
+    fire(jobs, 202, 203)
+    finish(1)
+    stream.start(1)
+    fire(jobs, 104, 105, 106)
     finish(2)
-    fire(jobs, 104, 105, 106)
     finish(3)
     gain_rows = jnp.concatenate([gg[...], gain2[...]], axis=0).astype(BF16)
     gain_rows = jnp.concatenate([gain_rows, gain_rows], axis=0)
     gbuf[0, 0] = gain_rows
     gbuf[0, 1] = gain_rows
-    fire(jobs, 7, 400, 401, 402, 403, 107, 204, 207, 205, 206, 500, 501, 502, 503, 304, 307, 305, 306, 404, 407, 405, 406, 504, 507, 505, 506)
+    fire(jobs, 7, 300, 301, 107, 204, 205, 207, 206)
+    stream.start(2)
+    stream.start(3)
+    fire(jobs, 302, 303, 400, 401, 402, 403, 304, 305, 307, 306, 500, 501, 502, 503, 404, 405, 407, 406, 504, 505, 507, 506)
     stream.finish()
-    last.finish()
+    for t in range(FRONT_BLOCKS, last.count):
+        last.remote(t).wait()
     for job in jobs:
         job.close()
     wires.close()
+
+
+def last_kernel(layer_ref, input_ref, *refs):
+    *refs, layer_buf, input_buf, sems = refs
+    n = len(refs) // 2 - 1
+    grads, (layer_out, input_out), outs = refs[:n], refs[n : n + 2], refs[n + 2 :]
+    ways = ((layer_ref, layer_buf, layer_out), (input_ref, input_buf, input_out))
+    parts = [(i, j, pl.ds(j * 4 * TILE, 4 * TILE)) for i in range(2) for j in range(layer_buf.shape[0] // (4 * TILE))]
+    loads = [pltpu.make_async_copy(ways[i][0].at[rows, :], ways[i][1].at[rows, :], sems.at[0, i, j]) for i, j, rows in parts]
+    stores = [pltpu.make_async_copy(ways[i][1].at[rows, :], ways[i][2].at[rows, :], sems.at[1, i, j]) for i, j, rows in parts]
+    started(loads)
+    for grad, out in zip(grads, outs):
+        out[...] = grad[...].astype(F32)
+    for load, store in zip(loads, stores):
+        load.wait()
+        store.start()
+    Wires.done(stores)
 
 
 def on_device(inputs, lengths, attn_gain, mlp_gain, qkv_weight, attn_weight, mlp_in_weight, mlp_out_weight, cotangent):
@@ -694,17 +720,14 @@
     hbm = pl.BlockSpec(memory_space=pl.ANY)
     vmem = pl.BlockSpec(memory_space=pltpu.VMEM)
     smem = pl.BlockSpec(memory_space=pltpu.SMEM)
-    length = lax.dynamic_index_in_dim(lengths[0], mine, 0, keepdims=True)
-    block0 = ctx * (local // HALF) - 1
-    pos0 = ctx * local
-    scalars = jnp.stack([length[0], pos0.astype(jnp.int32), block0.astype(jnp.int32)])
     ext = local + 2 * HALF
     tiles = local // TILE
     chunks = width // LANES
     span = TILE + 2 * HALF
     wide = ((ext, width), BF16)
     tall = ((local, width), BF16)
-    full_shapes = [(s.shape[0], n_tp, s.shape[1], width) for s in shards]
+    heads_rows, ff_rows = attn_weight.shape[0], mlp_out_weight.shape[0]
+    full_shapes = [(2, 2, heads_rows, width), (2, 2, 2, ff_rows, width), (2, 2, ff_rows, width)]
     ff_half = 2 * mlp_out_weight.shape[0]
     width_half = width // 2
     saved = [
@@ -714,7 +737,6 @@
         tall,
     ]
     outs = [
-        ((2 * TILE, width), BF16),
         ((16, width), BF16),
         tall, tall,
         ((8, width), F32),
@@ -726,9 +748,9 @@
         functools.partial(front_kernel, n_shard),
         out_shape=[jax.ShapeDtypeStruct(*o) for o in saved + [both] + outs],
         in_specs=[smem] + [hbm] * 7 + [vmem] * 4,
-        out_specs=[hbm] * 9 + [vmem] * 7,
+        out_specs=[hbm] * 8 + [vmem] * 7,
         scratch_shapes=[pltpu.VMEM(*o) for o in saved]
-        + [pltpu.VMEM(f, BF16) for f in full_shapes[1:]]
+        + [pltpu.VMEM(f, BF16) for f in full_shapes]
         + [
             pltpu.VMEM(*wide),
             pltpu.VMEM(*tall),
@@ -741,8 +763,8 @@
         ],
         compiler_params=pltpu.CompilerParams(collective_id=0, has_side_effects=True, vmem_limit_bytes=VMEM_LIMIT),
         name="front",
-    )(scalars, inputs, cotangent, gains, *shards, *tables)
-    wqkv, normed, q, k, v, probs, context, layer_all, layer_tail, gains, dctx, gml, gain2_part, dwm, dwi, dwo = results
+    )(lengths, inputs, cotangent, gains, *shards, *tables)
+    wqkv, normed, q, k, v, probs, context, layer_all, gains, dctx, gml, gain2_part, dwm, dwi, dwo = results
     cols = width // n_shard if n_shard == 2 else width
     grads = [(3, 2, width_half // 2, width), (2, 2, ff_half // 2, width), (1, 2, ff_half // 2, width), (1, 2, width_half // 2, width), (1, 2, 32, width)]
     dwi, dwm, dwo = (g.reshape(shape) for g, shape in zip((dwi, dwm, dwo), grads[1:]))
@@ -752,9 +774,9 @@
     layer_out, input_grad, *owned = pl.pallas_call(
         functools.partial(back_kernel, n_shard),
         out_shape=[jax.ShapeDtypeStruct(*both)] * 2 + [jax.ShapeDtypeStruct((g[0], g[2], cols), BF16) for g in grads],
-        in_specs=[smem] + [vmem] * 6 + [hbm] * 15,
+        in_specs=[vmem] * 6 + [hbm] * 14,
         out_specs=[hbm] * 2 + [vmem] * len(grads),
-        input_output_aliases={20: 0},
+        input_output_aliases={19: 0},
         scratch_shapes=[pltpu.VMEM(a.shape, a.dtype) for a in homes]
         + [
             pltpu.VMEM(*tall),
@@ -773,8 +795,20 @@
         + [b for g in jobs for b in Reduce.scratch(g, n_shard)],
         compiler_params=pltpu.CompilerParams(collective_id=1, has_side_effects=True, vmem_limit_bytes=VMEM_LIMIT),
         name="back",
-    )(scalars, gains, gain2_part, *tables, *homes, inputs, layer_all, layer_tail)
-    owned = [g.astype(F32) for g in owned]
+    )(gains, gain2_part, *tables, *homes, inputs, layer_all)
+    gain_sums = owned.pop()
+    flat = jax.ShapeDtypeStruct((seqs * local, width), BF16)
+    layer_out, input_grad, *owned = pl.pallas_call(
+        last_kernel,
+        out_shape=[flat] * 2 + [jax.ShapeDtypeStruct(g.shape, F32) for g in owned],
+        in_specs=[hbm] * 2 + [vmem] * len(owned),
+        out_specs=[hbm] * 2 + [vmem] * len(owned),
+        scratch_shapes=[pltpu.VMEM(flat.shape, BF16), pltpu.VMEM(flat.shape, BF16), pltpu.SemaphoreType.DMA((2, 2, flat.shape[0] // (4 * TILE)))],
+        compiler_params=pltpu.CompilerParams(vmem_limit_bytes=VMEM_LIMIT),
+        name="last",
+    )(layer_out.reshape(flat.shape), input_grad.reshape(flat.shape), *owned)
+    layer_out, input_grad = (a.reshape(both[0]) for a in (layer_out, input_grad))
+    owned.append(gain_sums.astype(F32))
     if n_shard != 2:
         owned = [lax.psum_scatter(g, "shard", scatter_dimension=2, tiled=True) for g in owned]
     qkv_grad = jnp.transpose(owned[0], (2, 0, 1))

time: 190 us -> 183 us (0.963)
  other arithmetic: 9.27 us -> 0.71 us
  Pallas kernels: 171 us -> 179 us
  local copies, waits for them, and re-layouts: 8.65 us -> 1.89 us
    pallas_call x0 -> x1, Pallas kernels: none -> 8.2 us  [on_device(): pl.pallas_call(last_kernel, out_shape=[flat] * 2 + [jax.ShapeDtypeStruct(...]
    pallas_call x1, Pallas kernels: 97.3 us -> 91.4 us  [on_device(): pl.pallas_call(functools.partial(front_kernel, n_shard), out_shape=[jax.S...]
    pallas_call x1, Pallas kernels: 74 us -> 79.7 us  [on_device(): pl.pallas_call(functools.partial(back_kernel, n_shard), out_shape=[jax.Sh...]
    unnamed x8 -> x2, local copies, waits for them, and re-layouts: 5.33 us -> 0.01 us
    transpose x2 -> x0, other arithmetic: 3.96 us -> none  [the longest x1 1.98 us: on_device(): qkv_grad = jnp.transpose(owned[0], (2, 0, 1))]
    squeeze x2 -> x0, other arithmetic: 3.37 us -> none  [on_device(): mlp_out_grad, attn_grad = (owned[2][0], owned[3][0])]
where the time goes in v5:
time: 183 us
  Pallas kernels  179 us (98%)
  local copies, waits for them, and re-layouts  1.89 us (1%)
    pallas_call x1, Pallas kernels, on_device(): pl.pallas_call(functools.partial(front_kernel, n_shard), out_shape=[jax.S...  91.4 us
    pallas_call x1, Pallas kernels, on_device(): pl.pallas_call(functools.partial(back_kernel, n_shard), out_shape=[jax.Sh...  79.7 us
    pallas_call x1, Pallas kernels, on_device(): pl.pallas_call(last_kernel, out_shape=[flat] * 2 + [jax.ShapeDtypeStruct(...  8.2 us

profile of v5, /device:TPU:0, one launch (start us, length us, event | category | flops | bytes accessed | tf_op | source)
XLA Modules:
  0.0 182.6 jit_solution(16296947613140701952)
XLA Ops:
  0.6 0.7 stack.10
  1.3 0.7 stack.9
  2.0 0.6 fusion.2.gains_ref
  2.6 91.4 %front.1 = (bf16[2,3,2,192,768]{4,3,2,1,0:T(8,128)(2,1)}, bf16[1152,768]{1,0:T(8,128)(2,1)}, bf16[1152,768]{1,0:T(8,128)(2,1)}, bf16[1152,768]{1,0:T(8,128)(2,1)...) custom-call(s32[1,2]{1,0:T(1,128)} %len_ref.1, ...), custom_call_target="tpu_custom_call" | custom-call | tf_op jit(solution)/shard_map/front/pallas_call | solution.py:747
  94.0 79.7 %back.1 = (bf16[2,1024,768]{2,1,0:T(8,128)(2,1)}, bf16[2,1024,768]{2,1,0:T(8,128)(2,1)}, bf16[3,192,384]{2,1,0:T(8,128)(2,1)}, bf16[2,288,384]{2,1,0:T(8,128)(2,...) custom-call(bf16[16,768]{1,0:T(8,128)(2,1)} %get-tuple-element.36.ga, ...), custom_call_target="tpu_custom_call", output_to_operand_aliasing={{0}: (19, {})} | custom-call | tf_op jit(solution)/shard_map/back/pallas_call | solution.py:774
  173.7 0.0 copy-start
  173.7 8.2 %last.1 = (bf16[2048,768]{1,0:T(8,128)(2,1)}, bf16[2048,768]{1,0:T(8,128)(2,1)}, f32[3,192,384]{2,1,0:T(8,128)}, f32[2,288,384]{2,1,0:T(8,128)}, f32[1,288,384]{2,1,0:T(8,128)}, /*index=5*/f32[1,192,384]{2,1,0:T(8,128)}) custom-call(bf16[2048,768]{1,0:T(8,128)(2,1)} %bitcast.21, bf16[2048,768]{1,0:T(8,128)(2,1)} %bitcast.22, ...), custom_call_target="tpu_custom_call" | custom-call | tf_op jit(solution)/shard_map/last/pallas_call | solution.py:801
  181.9 0.0 copy-done
  181.9 0.1 bitcast_reduce_fusion
  182.0 0.5 slice_bitcast_fusion
  (1 shorter events, 0.0 us)
Async XLA Ops:
  173.7 8.2 %copy-start = (bf16[1,32,384]{2,1,0:T(8,128)(2,1)S(1)}, bf16[1,32,384]{2,1,0:T(8,128)(2,1)}, u32[]{:S(2)}) copy-start(bf16[1,32,384]{2,1,0:T(8,128)(2,1)} %get-tuple-element.63) | copy-start | bytes 73732

commit v6 on v5

--- a/solution.py
+++ b/solution.py
@@ -21,12 +21,12 @@
 BF16 = jnp.bfloat16
 FRONT_BLOCKS = 2
 FORWARD = (
-    (100, 101, 102, 106, 103, 200, 201, 104, 202, 300, 206, 400, 301, 105, 203, 401, 302, 204, 402),
-    {0: (306, 107, 108, 109, 110), 1: (303, 205)},
-    {0: (304,), 1: (207,), 3: (305, 111), 4: (208,), 6: (307,), 7: (403, 404, 405, 209)},
+    (100, 101, 102, 106, 103, 200, 201, 104, 202, 300, 206, 400, 301, 105, 203, 401, 302, 204, 402, 306),
+    {0: (107, 108, 109, 110), 1: (303, 205), 2: (304,)},
+    {1: (207,), 2: (305, 111), 4: (208,), 5: (307,), 6: (209,), 7: (403, 404, 405)},
     {0: (112,), 1: (308, 210)},
-    {2: (309, 211), 3: (113,), 4: (212, 310), 7: (406, 407, 408, 409, 410, 311)},
-    {0: (213, 312, 313, 411, 412, 413)},
+    {1: (309, 211), 2: (113,), 3: (212, 310), 6: (311,), 7: (406, 407, 408, 409, 410, 213)},
+    {0: (312, 313, 411, 412, 413)},
 )
 VMEM_LIMIT = 60 * 1024 * 1024
 
@@ -138,15 +138,15 @@
         bias = jnp.where(allowed, 0.0, masked_score).astype(F32)
         bias = jnp.concatenate([bias, bias], axis=0)
         low_head = head_masks((TILE, LANES))
-        for j in chunks:
-            lanes = slice(j * LANES, (j + 1) * LANES)
-            q2 = split_heads(q_ref[pl.ds(r0 + HALF, TILE), lanes], low_head)
-            scores = nt(q2, k_ref[pl.ds(r0, span), lanes]) + bias
-            terms = jnp.exp(scores - jnp.max(scores, axis=-1, keepdims=True))
-            probs = (terms * (1.0 / jnp.sum(terms, axis=-1, keepdims=True))).astype(BF16)
-            p_ref[t, j] = probs
-            out = nn(probs, v_ref[pl.ds(r0, span), lanes])
-            ctx_ref[pl.ds(r0, TILE), lanes] = jnp.where(low_head, out[:TILE], out[TILE:]).astype(BF16)
+        lanes = [slice(j * LANES, (j + 1) * LANES) for j in chunks]
+        queries = [split_heads(q_ref[pl.ds(r0 + HALF, TILE), at], low_head) for at in lanes]
+        scores = [nt(q2, k_ref[pl.ds(r0, span), at]) + bias for q2, at in zip(queries, lanes)]
+        terms = [jnp.exp(s - jnp.max(s, axis=-1, keepdims=True)) for s in scores]
+        probs = [(e * (1.0 / jnp.sum(e, axis=-1, keepdims=True))).astype(BF16) for e in terms]
+        outs = [nn(p, v_ref[pl.ds(r0, span), at]) for p, at in zip(probs, lanes)]
+        for j, p, out, at in zip(chunks, probs, outs, lanes):
+            p_ref[t, j] = p
+            ctx_ref[pl.ds(r0, TILE), at] = jnp.where(low_head, out[:TILE], out[TILE:]).astype(BF16)
         after(t)
         return carry
 
@@ -682,19 +682,22 @@
     wires.close()
 
 
-def last_kernel(layer_ref, input_ref, *refs):
-    *refs, layer_buf, input_buf, sems = refs
-    n = len(refs) // 2 - 1
-    grads, (layer_out, input_out), outs = refs[:n], refs[n : n + 2], refs[n + 2 :]
-    ways = ((layer_ref, layer_buf, layer_out), (input_ref, input_buf, input_out))
-    parts = [(i, j, pl.ds(j * 4 * TILE, 4 * TILE)) for i in range(2) for j in range(layer_buf.shape[0] // (4 * TILE))]
-    loads = [pltpu.make_async_copy(ways[i][0].at[rows, :], ways[i][1].at[rows, :], sems.at[0, i, j]) for i, j, rows in parts]
-    stores = [pltpu.make_async_copy(ways[i][1].at[rows, :], ways[i][2].at[rows, :], sems.at[1, i, j]) for i, j, rows in parts]
+def last_kernel(n, *refs):
+    sources, results, lows, highs, (layer_buf, input_buf, sems) = refs[:n], refs[n : 2 * n], refs[2 * n : 3 * n - 2], refs[3 * n - 2 : 4 * n - 4], refs[4 * n - 4 :]
+    parts = []
+    for i, (low, high) in enumerate(zip(lows, highs)):
+        parts.append((sources[2 + i], low, high, results[2 + i]))
+    for i, buf in enumerate((layer_buf, input_buf)):
+        for at in range(0, buf.shape[0], 4 * TILE):
+            rows = pl.ds(at, 4 * TILE)
+            parts.append((sources[i].at[rows, :], buf.at[rows, :], buf.at[rows, :], results[i].at[rows, :]))
+    loads = [pltpu.make_async_copy(src, low, sems.at[0, i]) for i, (src, low, _, _) in enumerate(parts)]
+    stores = [pltpu.make_async_copy(high, dst, sems.at[1, i]) for i, (_, _, high, dst) in enumerate(parts)]
     started(loads)
-    for grad, out in zip(grads, outs):
-        out[...] = grad[...].astype(F32)
-    for load, store in zip(loads, stores):
+    for i, (load, store) in enumerate(zip(loads, stores)):
         load.wait()
+        if i < n - 2:
+            parts[i][2][...] = parts[i][1][...].astype(F32)
         store.start()
     Wires.done(stores)
 
@@ -799,11 +802,14 @@
     gain_sums = owned.pop()
     flat = jax.ShapeDtypeStruct((seqs * local, width), BF16)
     layer_out, input_grad, *owned = pl.pallas_call(
-        last_kernel,
+        functools.partial(last_kernel, 2 + len(owned)),
         out_shape=[flat] * 2 + [jax.ShapeDtypeStruct(g.shape, F32) for g in owned],
-        in_specs=[hbm] * 2 + [vmem] * len(owned),
-        out_specs=[hbm] * 2 + [vmem] * len(owned),
-        scratch_shapes=[pltpu.VMEM(flat.shape, BF16), pltpu.VMEM(flat.shape, BF16), pltpu.SemaphoreType.DMA((2, 2, flat.shape[0] // (4 * TILE)))],
+        in_specs=[hbm] * (2 + len(owned)),
+        out_specs=[hbm] * (2 + len(owned)),
+        scratch_shapes=[pltpu.VMEM(g.shape, BF16) for g in owned]
+        + [pltpu.VMEM(g.shape, F32) for g in owned]
+        + [pltpu.VMEM(flat.shape, BF16)] * 2
+        + [pltpu.SemaphoreType.DMA((2, len(owned) + 2 * (flat.shape[0] // (4 * TILE))))],
         compiler_params=pltpu.CompilerParams(vmem_limit_bytes=VMEM_LIMIT),
         name="last",
     )(layer_out.reshape(flat.shape), input_grad.reshape(flat.shape), *owned)

time: 183 us -> 176 us (0.962)
  Pallas kernels: 179 us -> 173 us
    pallas_call x1, Pallas kernels: 91.4 us -> 86.5 us  [on_device(): pl.pallas_call(functools.partial(front_kernel, n_shard), out_shape=[jax.S...]
where the time goes in v6:
time: 176 us
  Pallas kernels  173 us (98%)
  local copies, waits for them, and re-layouts  1.89 us (1%)
    pallas_call x1, Pallas kernels, on_device(): pl.pallas_call(functools.partial(front_kernel, n_shard), out_shape=[jax.S...  86.5 us
    pallas_call x1, Pallas kernels, on_device(): pl.pallas_call(functools.partial(back_kernel, n_shard), out_shape=[jax.Sh...  79.6 us
    pallas_call x1, Pallas kernels, on_device(): pl.pallas_call(functools.partial(last_kernel, 2 + len(owned)), out_shape=...  6.68 us

profile of v6, /device:TPU:0, one launch (start us, length us, event | category | flops | bytes accessed | tf_op | source)
XLA Modules:
  0.0 176.1 jit_solution(7237196137737831548)
XLA Ops:
  0.6 0.7 stack.10
  1.3 0.7 stack.9
  2.0 0.6 fusion.2.gains_ref
  2.6 86.5 %front.1 = (bf16[2,3,2,192,768]{4,3,2,1,0:T(8,128)(2,1)}, bf16[1152,768]{1,0:T(8,128)(2,1)}, bf16[1152,768]{1,0:T(8,128)(2,1)}, bf16[1152,768]{1,0:T(8,128)(2,1)...) custom-call(s32[1,2]{1,0:T(1,128)} %len_ref.1, ...), custom_call_target="tpu_custom_call" | custom-call | tf_op jit(solution)/shard_map/front/pallas_call | solution.py:750
  89.2 79.6 %back.1 = (bf16[2,1024,768]{2,1,0:T(8,128)(2,1)}, bf16[2,1024,768]{2,1,0:T(8,128)(2,1)}, bf16[3,192,384]{2,1,0:T(8,128)(2,1)}, bf16[2,288,384]{2,1,0:T(8,128)(2,...) custom-call(bf16[16,768]{1,0:T(8,128)(2,1)} %get-tuple-element.36.ga, ...), custom_call_target="tpu_custom_call", output_to_operand_aliasing={{0}: (19, {})} | custom-call | tf_op jit(solution)/shard_map/back/pallas_call | solution.py:777
  168.8 0.0 copy-start
  168.8 6.7 %last.1 = (bf16[2048,768]{1,0:T(8,128)(2,1)}, bf16[2048,768]{1,0:T(8,128)(2,1)}, f32[3,192,384]{2,1,0:T(8,128)}, f32[2,288,384]{2,1,0:T(8,128)}, f32[1,288,384]{2,1,0:T(8,128)}, /*index=5*/f32[1,192,384]{2,1,0:T(8,128)}) custom-call(bf16[2048,768]{1,0:T(8,128)(2,1)} %bitcast.21, bf16[2048,768]{1,0:T(8,128)(2,1)} %bitcast.22, ...), custom_call_target="tpu_custom_call" | custom-call | tf_op jit(solution)/shard_map/last/pallas_call | solution.py:804
  175.5 0.0 copy-done
  175.5 0.1 bitcast_reduce_fusion
  175.6 0.5 slice_bitcast_fusion
  (1 shorter events, 0.0 us)
Async XLA Ops:
  168.8 6.7 %copy-start = (bf16[1,32,384]{2,1,0:T(8,128)(2,1)S(1)}, bf16[1,32,384]{2,1,0:T(8,128)(2,1)}, u32[]{:S(2)}) copy-start(bf16[1,32,384]{2,1,0:T(8,128)(2,1)} %get-tuple-element.63) | copy-start | bytes 73732

commit v7 on v6

--- a/solution.py
+++ b/solution.py
@@ -528,8 +528,8 @@
 
 def front_kernel(n_shard, len_ref, x_ref, cot_hbm, gains_ref, *refs):
     shards, tables, refs = refs[:4], refs[4:8], refs[8:]
-    saved, (layer_all, gains, dctx, gml, gg, dwm, dwi, dwo), refs = refs[:7], refs[7:15], refs[15:]
-    wqkv, normed, q, k, v, p, ctx, wo, wi, wm, ext, cot, out, nm, hid, dgu, send, recv = refs
+    saved, (layer_all, gains, dctx_home, gml_home, gg, dwm_home, dwi_home, dwo_home), refs = refs[:7], refs[7:15], refs[15:]
+    wqkv, normed, q, k, v, p, ctx, wo, wi, wm, ext, cot, out, nm, hid, dgu, dctx, gml, dwm, dwi, dwo, send, recv = refs
     h = Place(n_shard)
     near = [{"tp": (h.z + i) % 4} for i in (1, 2, 3)] + [{"ctx": (h.c + i) % 4} for i in (1, 2, 3)]
     if h.split:
@@ -578,9 +578,13 @@
     rows = 2 * TILE
     wis, wms = (wi_near, wi_far), (wm_near, wm_far)
     phase_mlp(ext, cot, ctx, gains, wo, wis, wms, out, gml, nm, hid, dgu, dctx, gg, pos0, length, rows, between(jobs, FORWARD[5]), stream.start)
+    stores += [wires.own(dctx, dctx_home), wires.own(gml, gml_home)]
+    weight_grad(dgu, nm[...], dwi, 384)
+    stores.append(wires.own(dwi, dwi_home))
     weight_grad(hid, cot[...], dwm, 192)
-    weight_grad(dgu, nm[...], dwi, 384)
+    stores.append(wires.own(dwm, dwm_home))
     weight_grad(ctx, gml[...], dwo, LANES, count=dwo.shape[0])
+    stores.append(wires.own(dwo, dwo_home))
     wires.done(stores)
     stream.finish()
     for job in jobs:
@@ -746,12 +750,12 @@
         ((ff_half, width), BF16), ((2 * ff_half, width), BF16), ((width_half, width), BF16),
     ]
     both = ((seqs, local, width), BF16)
-    copies = 14 * Gather.SEMS + 24
+    copies = 14 * Gather.SEMS + 32
     results = pl.pallas_call(
         functools.partial(front_kernel, n_shard),
         out_shape=[jax.ShapeDtypeStruct(*o) for o in saved + [both] + outs],
         in_specs=[smem] + [hbm] * 7 + [vmem] * 4,
-        out_specs=[hbm] * 8 + [vmem] * 7,
+        out_specs=[hbm] * 8 + [vmem, hbm, hbm, vmem, hbm, hbm, hbm],
         scratch_shapes=[pltpu.VMEM(*o) for o in saved]
         + [pltpu.VMEM(f, BF16) for f in full_shapes]
         + [
@@ -761,6 +765,11 @@
             pltpu.VMEM(*tall),
             pltpu.VMEM((local, ff_half), BF16),
             pltpu.VMEM((local, 2 * ff_half), BF16),
+            pltpu.VMEM(*tall),
+            pltpu.VMEM(*tall),
+            pltpu.VMEM((ff_half, width), BF16),
+            pltpu.VMEM((2 * ff_half, width), BF16),
+            pltpu.VMEM((width_half, width), BF16),
             pltpu.SemaphoreType.DMA((copies,)),
             pltpu.SemaphoreType.DMA((copies,)),
         ],

time: 176 us -> 175 us (level)
  Pallas kernels: 173 us -> 171 us
    pallas_call x1, Pallas kernels: 86.5 us -> 84.7 us  [on_device(): pl.pallas_call(functools.partial(front_kernel, n_shard), out_shape=[jax.S...]
where the time goes in v7:
time: 175 us
  Pallas kernels  171 us (98%)
  local copies, waits for them, and re-layouts  1.89 us (1%)
    pallas_call x1, Pallas kernels, on_device(): pl.pallas_call(functools.partial(front_kernel, n_shard), out_shape=[jax.S...  84.7 us
    pallas_call x1, Pallas kernels, on_device(): pl.pallas_call(functools.partial(back_kernel, n_shard), out_shape=[jax.Sh...  80 us
    pallas_call x1, Pallas kernels, on_device(): pl.pallas_call(functools.partial(last_kernel, 2 + len(owned)), out_shape=...  6.68 us

profile of v7, /device:TPU:0, one launch (start us, length us, event | category | flops | bytes accessed | tf_op | source)
XLA Modules:
  0.0 174.6 jit_solution(7298317004375761281)
XLA Ops:
  0.6 0.7 stack.10
  1.3 0.7 stack.9
  2.0 0.6 fusion.2.gains_ref
  2.6 84.7 %front.1 = (bf16[2,3,2,192,768]{4,3,2,1,0:T(8,128)(2,1)}, bf16[1152,768]{1,0:T(8,128)(2,1)}, bf16[1152,768]{1,0:T(8,128)(2,1)}, bf16[1152,768]{1,0:T(8,128)(2,1)...) custom-call(s32[1,2]{1,0:T(1,128)} %len_ref.1, ...), custom_call_target="tpu_custom_call" | custom-call | tf_op jit(solution)/shard_map/front/pallas_call | solution.py:754
  87.3 80.0 %back.1 = (bf16[2,1024,768]{2,1,0:T(8,128)(2,1)}, bf16[2,1024,768]{2,1,0:T(8,128)(2,1)}, bf16[3,192,384]{2,1,0:T(8,128)(2,1)}, bf16[2,288,384]{2,1,0:T(8,128)(2,...) custom-call(bf16[16,768]{1,0:T(8,128)(2,1)} %get-tuple-element.36.ga, ...), custom_call_target="tpu_custom_call", output_to_operand_aliasing={{0}: (19, {})} | custom-call | tf_op jit(solution)/shard_map/back/pallas_call | solution.py:786
  167.3 0.0 copy-start
  167.3 6.7 %last.1 = (bf16[2048,768]{1,0:T(8,128)(2,1)}, bf16[2048,768]{1,0:T(8,128)(2,1)}, f32[3,192,384]{2,1,0:T(8,128)}, f32[2,288,384]{2,1,0:T(8,128)}, f32[1,288,384]{2,1,0:T(8,128)}, /*index=5*/f32[1,192,384]{2,1,0:T(8,128)}) custom-call(bf16[2048,768]{1,0:T(8,128)(2,1)} %bitcast.21, bf16[2048,768]{1,0:T(8,128)(2,1)} %bitcast.22, ...), custom_call_target="tpu_custom_call" | custom-call | tf_op jit(solution)/shard_map/last/pallas_call | solution.py:813
  174.0 0.0 copy-done
  174.0 0.1 bitcast_reduce_fusion
  174.1 0.5 slice_bitcast_fusion
  (1 shorter events, 0.0 us)
Async XLA Ops:
  167.3 6.7 %copy-start = (bf16[1,32,384]{2,1,0:T(8,128)(2,1)S(1)}, bf16[1,32,384]{2,1,0:T(8,128)(2,1)}, u32[]{:S(2)}) copy-start(bf16[1,32,384]{2,1,0:T(8,128)(2,1)} %get-tuple-element.63) | copy-start | bytes 73732
